TPU v7x, 256 devices: a whole 4x4x8 slice. The times are simulated.
256 devices in a mesh: section: 8 (over z), expert: 8 (over x_lo, y), mp: 4 (over x_hi, core).
Axes of the slice: x: 4 (x_hi: 2, x_lo: 2; x = x_hi * 2 + x_lo), y: 4, z: 8, core: 2. Of those that a mesh axis runs over, the one named last changes fastest.
Arguments:
- grad_in: bfloat16 [8, 1024, 3072], P('section', 'expert', 'mp'), may hold values from -6 to 6
- saved_input: bfloat16 [8, 2, 1024, 3072], P('section', None, 'expert', 'mp'), may hold values from -6 to 6
- routes: int32 [8, 2, 1024, 2], P('section', None, 'expert'), may hold values from 0 to 3, all different within a row; in each aligned block of 128 rows (0 to 127, 128 to 255, ..., all dimensions but the last counted through in order) at most 72 rows name the same one
- route_weights: float32 [8, 2, 1024, 2], P('section', None, 'expert'), may hold values from 0.2 to 1
- plan: int32 [8, 2], P('section'), may hold values from 0 to 1, each once within a row
- up_weight: bfloat16 [8, 3072, 32768], P('section', None, ('expert', 'mp')), may hold values from -0.109375 to 0.109375
- down_weight: bfloat16 [8, 32768, 3072], P('section', ('expert', 'mp')), may hold values from -0.0625 to 0.0625
Outputs:
- passed_grad: bfloat16 [8, 1024, 3072], P('section', 'expert', 'mp')
Inputs may be any that keep to these rules, and one draw needn't show every extreme that they name: `routes`: the numbers of a row differ. In each aligned block of 128 rows (the rows of one index of expert within one section and microbatch) no expert is named by more than 72 rows, and some block reaches 72. `plan`: each row is a permutation of 0 to 1.
All inputs are finite; a program needn't handle non-finite values.
Results may differ from a plain program's by a relative error of at most 0.0065.
Values may be sent and summed in bfloat16 or wider, within the bound.
No kernel may reach another device: no remote copies, remote signals or barrier semaphores. Data moves between devices by JAX's collectives and lax.ppermute only.
A program may use at most 128 MiB of HBM per device.

v0:
```python
import jax
import jax.numpy as jnp
from jax import lax
from jax.sharding import PartitionSpec as P

EXPERTS = 4
CAPACITY = 72


def from_behind(value, axis, by):
    devices = lax.axis_size(axis)
    return lax.ppermute(value, axis, [(i, (i + by) % devices) for i in range(devices)])


def targets(route_now):
    expert_ids = jnp.arange(EXPERTS, dtype=jnp.int32)
    onehot = (route_now[:, :, None] == expert_ids[None, None, :]).astype(jnp.int32)
    counts = jnp.sum(onehot, axis=1)
    before = jnp.cumsum(counts, axis=0) - counts
    slot_pos = jnp.sum(before[:, None, :] * onehot, axis=2)
    return route_now * CAPACITY + slot_pos


def per_device(grad_in, saved_input, routes, route_weights, plan, up_weight, down_weight):
    n_expert = lax.axis_size("expert")
    n_mp = lax.axis_size("mp")
    split_size = n_expert * n_mp // EXPERTS
    quarter = grad_in.shape[2]
    width = quarter * n_mp
    up_local = up_weight[0]
    down_local = down_weight[0]
    slot_ids = jnp.arange(EXPERTS * CAPACITY, dtype=jnp.int32)
    contract_last = (((1,), (1,)), ((), ()))
    current = grad_in[0]
    for step_index in range(plan.shape[1]):
        micro_index = plan[0, step_index]
        saved_now = lax.dynamic_index_in_dim(saved_input[0], micro_index, 0, keepdims=False)
        route_now = lax.dynamic_index_in_dim(routes[0], micro_index, 0, keepdims=False)
        share_now = lax.dynamic_index_in_dim(route_weights[0], micro_index, 0, keepdims=False)
        target = targets(route_now)
        hit_mask = target[None, :, :] == slot_ids[:, None, None]
        select = jnp.any(hit_mask, axis=2).astype(jnp.bfloat16)
        saved_sent = (
            jnp.dot(select, saved_now, preferred_element_type=jnp.float32)
            .astype(jnp.bfloat16)
            .reshape(EXPERTS, CAPACITY, quarter)
        )
        grad_sent = (
            jnp.dot(select, current, preferred_element_type=jnp.float32)
            .astype(jnp.bfloat16)
            .reshape(EXPERTS, CAPACITY, quarter)
        )

        def copies(array):
            return jnp.broadcast_to(
                array[:, None], (EXPERTS, split_size, CAPACITY, quarter)
            ).reshape(EXPERTS * split_size, CAPACITY, quarter)

        saved_got, grad_got = (
            lax.all_to_all(
                copies(saved_sent), ("expert", "mp"), split_axis=0, concat_axis=0, tiled=True
            ),
            lax.all_to_all(
                copies(grad_sent), ("expert", "mp"), split_axis=0, concat_axis=0, tiled=True
            ),
        )

        def assemble(array):
            return (
                array.reshape(n_expert, n_mp, CAPACITY, quarter)
                .transpose(0, 2, 1, 3)
                .reshape(n_expert * CAPACITY, width)
            )

        saved_rows = assemble(saved_got)
        grad_rows = assemble(grad_got)
        upper_pre = jnp.dot(saved_rows, up_local, preferred_element_type=jnp.float32)
        grad_act = lax.dot_general(
            grad_rows, down_local, contract_last, preferred_element_type=jnp.float32
        )
        sigma_up = jax.nn.sigmoid(upper_pre)
        grad_pre = (grad_act * sigma_up * (1.0 + upper_pre * (1.0 - sigma_up))).astype(jnp.bfloat16)
        partial_rows = lax.dot_general(
            grad_pre, up_local, contract_last, preferred_element_type=jnp.float32
        )
        outgoing = (
            partial_rows.reshape(n_expert, CAPACITY, n_mp, quarter)
            .transpose(0, 2, 1, 3)
            .reshape(n_expert * n_mp, CAPACITY, quarter)
        )
        arrived = lax.all_to_all(
            outgoing, ("expert", "mp"), split_axis=0, concat_axis=0, tiled=True
        )
        summed = jnp.sum(arrived.reshape(EXPERTS, split_size, CAPACITY, quarter), axis=1)
        mixing = jnp.sum(jnp.where(hit_mask, share_now[None, :, :], 0.0), axis=2)
        moe_term = lax.dot_general(
            mixing,
            summed.reshape(EXPERTS * CAPACITY, quarter),
            (((0,), (0,)), ((), ())),
            precision=lax.Precision.HIGHEST,
            preferred_element_type=jnp.float32,
        )
        result = (current.astype(jnp.float32) + moe_term).astype(jnp.bfloat16)
        current = from_behind(result, "section", -1)
    return current[None]


def solution(mesh):
    placed = (
        P("section", "expert", "mp"),
        P("section", None, "expert", "mp"),
        P("section", None, "expert", None),
        P("section", None, "expert", None),
        P("section", None),
        P("section", None, ("expert", "mp")),
        P("section", ("expert", "mp"), None),
    )
    return jax.shard_map(
        per_device,
        mesh=mesh,
        in_specs=placed,
        out_specs=P("section", "expert", "mp"),
        check_vma=False,
    )
```

profile of v0, /device:TPU:8, one launch (start us, length us, event | category | flops | bytes accessed | tf_op | source)
XLA Modules:
  0.0 482.0 jit_solution(12657258194341166876)
XLA Ops:
  0.0 1.4 fusion.26
  5.4 0.7 fusion.22
  6.1 0.1 copy.24
  6.2 0.2 reduce_window_sum.17
  6.4 0.1 copy.26
  6.5 0.1 copy.29
  6.6 0.2 reduce_window_sum.18
  6.8 0.1 copy.31
  7.0 1.2 convolution_convert_fusion.3
  8.2 2.0 broadcast_in_dim.69
  10.2 7.6 %all-to-all-start = ((bf16[32,72,768]{2,1,0:T(8,128)(2,1)}), bf16[32,72,768]{2,1,0:T(8,128)(2,1)}, u32[]{:S(2)}, u32[]{:S(2)}) async-start(bf16[32,72,768]{2,1,0:T(8,128)(2,1)} %bitcast.117), calls=%async_computation | async-start | bytes 7077888 | tf_op jit(solution)/shard_map/all_to_all | solution.py:63
  17.8 0.0 copy-done
  17.8 0.3 convolution_convert_fusion.2
  18.1 42.3 %all-to-all-done = bf16[32,72,768]{2,1,0:T(8,128)(2,1)} async-done(((bf16[32,72,768]{2,1,0:T(8,128)(2,1)}), bf16[32,72,768]{2,1,0:T(8,128)(2,1)}, u32[]{:S(2)}, u32[]{:S(2)}) %all-to-all-start) | async-done | bytes 3538976 | tf_op jit(solution)/shard_map/all_to_all | solution.py:63
  60.4 2.0 broadcast_in_dim.71
  62.4 10.0 %all-to-all-start.1 = ((bf16[32,72,768]{2,1,0:T(8,128)(2,1)}), bf16[32,72,768]{2,1,0:T(8,128)(2,1)}, u32[]{:S(2)}, u32[]{:S(2)}) async-start(bf16[32,72,768]{2,1,0:T(8,128)(2,1)} %bitcast.115), calls=%async_computation.1 | async-start | bytes 7077888 | tf_op jit(solution)/shard_map/all_to_all | solution.py:60
  72.4 3.5 copy.27
  75.9 2.5 copy.36
  78.4 36.5 %all-to-all-done.1 = bf16[32,72,768]{2,1,0:T(8,128)(2,1)} async-done(((bf16[32,72,768]{2,1,0:T(8,128)(2,1)}), bf16[32,72,768]{2,1,0:T(8,128)(2,1)}, u32[]{:S(2)}, u32[]{:S(2)}) %all-to-all-start.1) | async-done | bytes 3538976 | tf_op jit(solution)/shard_map/all_to_all | solution.py:60
  114.9 3.5 copy.28
  118.4 0.0 slice-start
  118.4 0.8 copy.37
  119.2 1.2 copy-done.2
  120.4 6.5 %fusion.6 = f32[576,1024]{1,0:T(8,128)S(1)} fusion(bf16[576,3072]{1,0:T(8,128)(2,1)S(1)} %bitcast.121, bf16[1,1024,3072]{2,1,0:T(8,128)(2,1)} %param.13), kind=kOutput, calls=%fused_computation.8 | convolution fusion | flops 3623878656 | bytes 12189696 | tf_op jit(solution)/shard_map/dot_general | solution.py:78
  126.9 0.0 slice-done
  126.9 0.0 slice-done.1
  126.9 4.5 multiply_convert_fusion.1
  131.4 6.0 %fusion.27 = f32[8,72,4,768]{3,1,2,0:T(8,128)} fusion(bf16[8,72,1024,1]{2,1,3,0:T(8,128)(2,1)S(1)} %bitcast.137, bf16[4,768,1024,1]{2,1,0,3:T(8,128)(2,1)S(1)} %bitcast.133), kind=kOutput, calls=%fused_computation.49 | convolution fusion | flops 3623878656 | bytes 14548992 | tf_op jit(solution)/shard_map/dot_general | solution.py:83
  137.4 9.9 %all-to-all-start.2 = ((f32[32,72,768]{2,1,0:T(8,128)}), f32[32,72,768]{2,1,0:T(8,128)}, u32[]{:S(2)}, u32[]{:S(2)}) async-start(f32[32,72,768]{2,1,0:T(8,128)} %bitcast.118), calls=%async_computation.2 | async-start | bytes 14155776 | tf_op jit(solution)/shard_map/all_to_all | solution.py:91
  147.4 0.6 copy-done.6
  148.0 0.3 convolution_convert_fusion
  148.3 89.2 %all-to-all-done.2 = f32[32,72,768]{2,1,0:T(8,128)} async-done(((f32[32,72,768]{2,1,0:T(8,128)}), f32[32,72,768]{2,1,0:T(8,128)}, u32[]{:S(2)}, u32[]{:S(2)}) %all-to-all-start.2) | async-done | bytes 7077920 | tf_op jit(solution)/shard_map/all_to_all | solution.py:91
  237.4 2.0 broadcast_in_dim.77
  239.5 8.0 %all-to-all-start.4 = ((bf16[32,72,768]{2,1,0:T(8,128)(2,1)}), bf16[32,72,768]{2,1,0:T(8,128)(2,1)S(1)}, u32[]{:S(2)}, u32[]{:S(2)}) async-start(bf16[32,72,768]{2,1,0:T(8,128)(2,1)} %bitcast.114), calls=%async_computation.4 | async-start | bytes 7077888 | tf_op jit(solution)/shard_map/all_to_all | solution.py:60
  247.5 0.0 copy-start.3
  247.6 0.0 copy-start.7
  247.6 3.6 bitcast_reduce_fusion.1
  251.2 0.9 fusion.12
  252.0 5.9 %collective-permute-start = (bf16[128,768]{1,0:T(8,128)(2,1)S(1)}, bf16[128,768]{1,0:T(8,128)(2,1)S(1)}, u32[]{:S(2)}, u32[]{:S(2)}) collective-permute-start(bf16[128,768]{1,0:T(8,128)(2,1)S(1)} %fusion.12), channel_id=1, source_target_pairs={{0,224},{32,0},{64,32},{96,64},{128,96},{160,128},{192,160},{224,1... | collective-permute-start | bytes 589832 | tf_op jit(solution)/shard_map/ppermute | solution.py:12
  258.0 4.5 collective-permute-done
  262.5 0.7 copy-done.4
  263.1 1.0 convolution_convert_fusion.1
  264.2 25.8 %all-to-all-done.4 = bf16[32,72,768]{2,1,0:T(8,128)(2,1)S(1)} async-done(((bf16[32,72,768]{2,1,0:T(8,128)(2,1)}), bf16[32,72,768]{2,1,0:T(8,128)(2,1)S(1)}, u32[]{:S(2)}, u32[]{:S(2)}) %all-to-all-start.4) | async-done | bytes 3538976 | tf_op jit(solution)/shard_map/all_to_all | solution.py:60
  290.0 3.0 broadcast_in_dim.75
  293.0 10.0 %all-to-all-start.3 = ((bf16[32,72,768]{2,1,0:T(8,128)(2,1)}), bf16[32,72,768]{2,1,0:T(8,128)(2,1)}, u32[]{:S(2)}, u32[]{:S(2)}) async-start(bf16[32,72,768]{2,1,0:T(8,128)(2,1)} %bitcast.116), calls=%async_computation.3 | async-start | bytes 7077888 | tf_op jit(solution)/shard_map/all_to_all | solution.py:63
  302.9 1.5 copy.33
  304.4 0.8 copy.39
  305.2 40.3 %all-to-all-done.3 = bf16[32,72,768]{2,1,0:T(8,128)(2,1)} async-done(((bf16[32,72,768]{2,1,0:T(8,128)(2,1)}), bf16[32,72,768]{2,1,0:T(8,128)(2,1)}, u32[]{:S(2)}, u32[]{:S(2)}) %all-to-all-start.3) | async-done | bytes 3538976 | tf_op jit(solution)/shard_map/all_to_all | solution.py:63
  345.5 3.5 copy.32
  349.0 0.0 slice-start.2
  349.0 0.8 copy.38
  349.8 0.0 slice-start.3
  349.8 6.6 %fusion.4 = f32[576,1024]{1,0:T(8,128)S(1)} fusion(bf16[576,3072]{1,0:T(8,128)(2,1)S(1)} %bitcast.123, bf16[1,1024,3072]{2,1,0:T(8,128)(2,1)} %param.13), kind=kOutput, calls=%fused_computation.6 | convolution fusion | flops 3623878656 | bytes 12189696 | tf_op jit(solution)/shard_map/dot_general | solution.py:78
  356.4 4.5 multiply_convert_fusion
  361.0 6.0 %fusion.28 = f32[8,72,4,768]{3,1,2,0:T(8,128)} fusion(bf16[8,72,1024,1]{2,1,3,0:T(8,128)(2,1)S(1)} %bitcast.138, bf16[4,768,1024,1]{2,1,0,3:T(8,128)(2,1)S(1)} %bitcast.136), kind=kOutput, calls=%fused_computation.50 | convolution fusion | flops 3623878656 | bytes 14548992 | tf_op jit(solution)/shard_map/dot_general | solution.py:83
  367.0 10.0 %all-to-all-start.5 = ((f32[32,72,768]{2,1,0:T(8,128)}), f32[32,72,768]{2,1,0:T(8,128)}, u32[]{:S(2)}, u32[]{:S(2)}) async-start(f32[32,72,768]{2,1,0:T(8,128)} %bitcast.119), calls=%async_computation.5 | async-start | bytes 14155776 | tf_op jit(solution)/shard_map/all_to_all | solution.py:91
  376.9 0.0 copy-start.1
  377.0 0.0 copy-start.5
  377.0 90.0 %all-to-all-done.5 = f32[32,72,768]{2,1,0:T(8,128)} async-done(((f32[32,72,768]{2,1,0:T(8,128)}), f32[32,72,768]{2,1,0:T(8,128)}, u32[]{:S(2)}, u32[]{:S(2)}) %all-to-all-start.5) | async-done | bytes 7077920 | tf_op jit(solution)/shard_map/all_to_all | solution.py:91
  467.0 3.6 bitcast_reduce_fusion
  470.6 0.8 add_convert_fusion
  471.4 5.9 %collective-permute-start.1 = (bf16[128,768]{1,0:T(8,128)(2,1)S(1)}, bf16[128,768]{1,0:T(8,128)(2,1)S(1)}, u32[]{:S(2)}, u32[]{:S(2)}) collective-permute-start(bf16[128,768]{1,0:T(8,128)(2,1)S(1)} %add_convert_fusion), channel_id=1, source_target_pairs={{0,224},{32,0},{64,32},{96,64},{128,96},{160,128},{192,160},{224,1... | collective-permute-start | bytes 589832 | tf_op jit(solution)/shard_map/ppermute | solution.py:12
  477.4 4.0 collective-permute-done.1
  481.3 0.7 copy.41
  (27 shorter events, 0.3 us)
Async XLA Ops:
  0.0 17.8 %copy-start = (bf16[1,2,128,768]{3,2,1,0:T(8,128)(2,1)S(1)}, bf16[1,2,128,768]{3,2,1,0:T(8,128)(2,1)}, u32[]{:S(2)}) copy-start(bf16[1,2,128,768]{3,2,1,0:T(8,128)(2,1)} %param.8) | copy-start | bytes 1179652
  10.2 50.1 %all-to-all-start = ((bf16[32,72,768]{2,1,0:T(8,128)(2,1)}), bf16[32,72,768]{2,1,0:T(8,128)(2,1)}, u32[]{:S(2)}, u32[]{:S(2)}) async-start(bf16[32,72,768]{2,1,0:T(8,128)(2,1)} %bitcast.117), calls=%async_computation | async-start | bytes 7077888 | tf_op jit(solution)/shard_map/all_to_all | solution.py:63
  62.4 52.5 %all-to-all-start.1 = ((bf16[32,72,768]{2,1,0:T(8,128)(2,1)}), bf16[32,72,768]{2,1,0:T(8,128)(2,1)}, u32[]{:S(2)}, u32[]{:S(2)}) async-start(bf16[32,72,768]{2,1,0:T(8,128)(2,1)} %bitcast.115), calls=%async_computation.1 | async-start | bytes 7077888 | tf_op jit(solution)/shard_map/all_to_all | solution.py:60
  118.4 2.0 copy-start.2
  118.4 8.5 %slice-start = ((s8[6291456]{0:T(1024)(128)(4,1)}), s8[4194304]{0:T(1024)(128)(4,1)S(1)}, s32[]{:S(2)}) async-start(s8[6291456]{0:T(1024)(128)(4,1)} %bitcast.131), calls=%async_computation.6 | async-start | bytes 8388608
  120.4 6.5 %slice-start.1 = ((s8[6291456]{0:T(1024)(128)(4,1)}), s8[2097152]{0:T(1024)(128)(4,1)S(1)}, s32[]{:S(2)}) async-start(s8[6291456]{0:T(1024)(128)(4,1)} %bitcast.131), calls=%async_computation.7 | async-start | bytes 4194304
  137.4 100.1 %all-to-all-start.2 = ((f32[32,72,768]{2,1,0:T(8,128)}), f32[32,72,768]{2,1,0:T(8,128)}, u32[]{:S(2)}, u32[]{:S(2)}) async-start(f32[32,72,768]{2,1,0:T(8,128)} %bitcast.118), calls=%async_computation.2 | async-start | bytes 14155776 | tf_op jit(solution)/shard_map/all_to_all | solution.py:91
  147.4 0.6 copy-start.6
  239.5 8.0 %copy-start.8 = (f32[1,2,128,2]{2,3,1,0:T(2,128)S(1)}, f32[1,2,128,2]{2,3,1,0:T(2,128)}, u32[]{:S(2)}) copy-start(f32[1,2,128,2]{2,3,1,0:T(2,128)} %param.10) | copy-start | bytes 6148
  239.5 50.5 %all-to-all-start.4 = ((bf16[32,72,768]{2,1,0:T(8,128)(2,1)}), bf16[32,72,768]{2,1,0:T(8,128)(2,1)S(1)}, u32[]{:S(2)}, u32[]{:S(2)}) async-start(bf16[32,72,768]{2,1,0:T(8,128)(2,1)} %bitcast.114), calls=%async_computation.4 | async-start | bytes 7077888 | tf_op jit(solution)/shard_map/all_to_all | solution.py:60
  247.5 3.6 copy-start.3
  247.6 15.6 %copy-start.7 = (pred[288,128]{1,0:T(8,128)(4,1)S(1)}, pred[288,128]{1,0:T(8,128)(4,1)}, u32[]{:S(2)}) copy-start(pred[288,128]{1,0:T(8,128)(4,1)} %copy-done.6) | copy-start | bytes 110596
  252.0 10.4 %collective-permute-start = (bf16[128,768]{1,0:T(8,128)(2,1)S(1)}, bf16[128,768]{1,0:T(8,128)(2,1)S(1)}, u32[]{:S(2)}, u32[]{:S(2)}) collective-permute-start(bf16[128,768]{1,0:T(8,128)(2,1)S(1)} %fusion.12), channel_id=1, source_target_pairs={{0,224},{32,0},{64,32},{96,64},{128,96},{160,128},{192,160},{224,1... | collective-permute-start | bytes 589832 | tf_op jit(solution)/shard_map/ppermute | solution.py:12
  262.5 0.7 copy-start.4
  293.0 52.5 %all-to-all-start.3 = ((bf16[32,72,768]{2,1,0:T(8,128)(2,1)}), bf16[32,72,768]{2,1,0:T(8,128)(2,1)}, u32[]{:S(2)}, u32[]{:S(2)}) async-start(bf16[32,72,768]{2,1,0:T(8,128)(2,1)} %bitcast.116), calls=%async_computation.3 | async-start | bytes 7077888 | tf_op jit(solution)/shard_map/all_to_all | solution.py:63
  349.0 7.4 %slice-start.2 = ((s8[6291456]{0:T(1024)(128)(4,1)}), s8[4194304]{0:T(1024)(128)(4,1)S(1)}, s32[]{:S(2)}) async-start(s8[6291456]{0:T(1024)(128)(4,1)} %bitcast.134), calls=%async_computation.8 | async-start | bytes 8388608
  349.8 6.7 %slice-start.3 = ((s8[6291456]{0:T(1024)(128)(4,1)}), s8[2097152]{0:T(1024)(128)(4,1)S(1)}, s32[]{:S(2)}) async-start(s8[6291456]{0:T(1024)(128)(4,1)} %bitcast.134), calls=%async_computation.9 | async-start | bytes 4194304
  367.0 100.1 %all-to-all-start.5 = ((f32[32,72,768]{2,1,0:T(8,128)}), f32[32,72,768]{2,1,0:T(8,128)}, u32[]{:S(2)}, u32[]{:S(2)}) async-start(f32[32,72,768]{2,1,0:T(8,128)} %bitcast.119), calls=%async_computation.5 | async-start | bytes 14155776 | tf_op jit(solution)/shard_map/all_to_all | solution.py:91
  376.9 105.1 %copy-start.1 = (bf16[1,2,128,768]{3,2,1,0:T(8,128)(2,1)S(1)}, bf16[1,2,128,768]{3,2,1,0:T(8,128)(2,1)}, u32[]{:S(2)}) copy-start(bf16[1,2,128,768]{3,2,1,0:T(8,128)(2,1)} %param.8) | copy-start | bytes 1179652
  377.0 93.6 %copy-start.5 = (bf16[128,768]{1,0:T(8,128)(2,1)S(1)}, bf16[128,768]{1,0:T(8,128)(2,1)}, u32[]{:S(2)}) copy-start(bf16[128,768]{1,0:T(8,128)(2,1)} %copy-done.4) | copy-start | bytes 589828
  471.4 9.9 %collective-permute-start.1 = (bf16[128,768]{1,0:T(8,128)(2,1)S(1)}, bf16[128,768]{1,0:T(8,128)(2,1)S(1)}, u32[]{:S(2)}, u32[]{:S(2)}) collective-permute-start(bf16[128,768]{1,0:T(8,128)(2,1)S(1)} %add_convert_fusion), channel_id=1, source_target_pairs={{0,224},{32,0},{64,32},{96,64},{128,96},{160,128},{192,160},{224,1... | collective-permute-start | bytes 589832 | tf_op jit(solution)/shard_map/ppermute | solution.py:12
where the time goes:
time: 484 us; the launch traced here: 482 us
  waiting for transfers between devices  333 us (69%)
  starting transfers between devices  67.2 us (14%)
  matrix products  38.5 us (8%)
  local copies, waits for them, and re-layouts  31.5 us (7%)
  other arithmetic  7.76 us (2%)
    all_to_all x2, waiting for transfers between devices, per_device(): lax.all_to_all(outgoing, ('expert', 'mp'), split_axis=0, concat_axis=0, t...  179 us
    all_to_all x2, waiting for transfers between devices, per_device(): lax.all_to_all(copies(grad_sent), ('expert', 'mp'), split_axis=0, concat_...  82.6 us
    all_to_all x2, waiting for transfers between devices, per_device(): lax.all_to_all(copies(saved_sent), ('expert', 'mp'), split_axis=0, concat...  62.3 us
    all_to_all x2, starting transfers between devices, per_device(): lax.all_to_all(outgoing, ('expert', 'mp'), split_axis=0, concat_axis=0, t...  19.9 us
    all_to_all x2, starting transfers between devices, per_device(): lax.all_to_all(copies(saved_sent), ('expert', 'mp'), split_axis=0, concat...  17.9 us
    all_to_all x2, starting transfers between devices, per_device(): lax.all_to_all(copies(grad_sent), ('expert', 'mp'), split_axis=0, concat_...  17.5 us
    dot_general x2, matrix products, per_device(): lax.dot_general(grad_rows, down_local, contract_last, preferred_element_t...  13.1 us
    dot_general x2, matrix products, per_device(): lax.dot_general(grad_pre, up_local, contract_last, preferred_element_type...  11.9 us
  transfers between devices with their start and end apart: 8, of which 8 were waited for; matrix products, arithmetic and copies ran while one was open for 3% of the time, Pallas kernels for 0%

commit v1 on v0

v1 whole, which is shorter than its diff:
```python
import jax
import jax.numpy as jnp
from jax import lax
from jax.experimental import pallas as pl
from jax.experimental.pallas import tpu as pltpu
from jax.sharding import Mesh, PartitionSpec as P

EXPERTS = 4
CAPACITY = 72
HIDDEN_BLOCK = 256
VMEM_LIMIT = 48 * 1024 * 1024


def contract_last(left, right):
    return lax.dot_general(
        left, right, (((1,), (1,)), ((), ())), preferred_element_type=jnp.float32
    )


def factor_kernel(core_ref, mine_ref, other_ref, up_ref, factor_ref):
    core = core_ref[0]
    quarter = mine_ref.shape[2]
    pre = None
    for xhi in range(mine_ref.shape[0]):
        own = pl.multiple_of((2 * xhi + core) * quarter, quarter)
        theirs = pl.multiple_of((2 * xhi + 1 - core) * quarter, quarter)
        part = jnp.dot(
            mine_ref[xhi], up_ref[pl.ds(own, quarter), :], preferred_element_type=jnp.float32
        ) + jnp.dot(
            other_ref[xhi], up_ref[pl.ds(theirs, quarter), :], preferred_element_type=jnp.float32
        )
        pre = part if pre is None else pre + part
    sigma = jax.nn.sigmoid(pre)
    factor_ref[...] = sigma * (1.0 + pre * (1.0 - sigma))


def factor(core, mine, other, up):
    halves, rows, quarter = mine.shape
    width, hidden = up.shape
    whole = pl.BlockSpec((halves, rows, quarter), lambda i, c: (0, 0, 0))
    return pl.pallas_call(
        factor_kernel,
        out_shape=jax.ShapeDtypeStruct((rows, hidden), jnp.float32),
        grid_spec=pltpu.PrefetchScalarGridSpec(
            num_scalar_prefetch=1,
            grid=(hidden // HIDDEN_BLOCK,),
            in_specs=[whole, whole, pl.BlockSpec((width, HIDDEN_BLOCK), lambda i, c: (0, i))],
            out_specs=pl.BlockSpec((rows, HIDDEN_BLOCK), lambda i, c: (0, i)),
        ),
        compiler_params=pltpu.CompilerParams(
            dimension_semantics=("arbitrary",), vmem_limit_bytes=VMEM_LIMIT
        ),
        name="factor",
    )(core, mine, other, up)


def branch_kernel(
    core_ref, mine_ref, other_ref, down_ref, factor_ref, up_ref, send_ref, keep_ref, grad_pre
):
    core = core_ref[0]
    step = pl.program_id(0)
    halves, _, quarter = mine_ref.shape
    blocks = grad_pre.shape[0]

    @pl.when(step < blocks)
    def _():
        act = None
        for xhi in range(halves):
            own = pl.multiple_of((2 * xhi + core) * quarter, quarter)
            theirs = pl.multiple_of((2 * xhi + 1 - core) * quarter, quarter)
            part = contract_last(mine_ref[xhi], down_ref[:, pl.ds(own, quarter)]) + contract_last(
                other_ref[xhi], down_ref[:, pl.ds(theirs, quarter)]
            )
            act = part if act is None else act + part
        grad_pre[step] = (act * factor_ref[...]).astype(jnp.bfloat16)

    def partial():
        total = None
        for block in range(blocks):
            part = contract_last(
                grad_pre[block], up_ref[:, block * HIDDEN_BLOCK : (block + 1) * HIDDEN_BLOCK]
            )
            total = part if total is None else total + part
        return total.astype(jnp.bfloat16)

    @pl.when((step >= blocks) & (step < blocks + halves))
    def _():
        send_ref[0] = partial()

    @pl.when(step >= blocks + halves)
    def _():
        keep_ref[0] = partial()


def branch(core, mine, other, down, factors, up):
    halves, rows, quarter = mine.shape
    hidden, width = down.shape
    blocks = hidden // HIDDEN_BLOCK
    whole = pl.BlockSpec((halves, rows, quarter), lambda i, c: (0, 0, 0))

    def hidden_block(i):
        return jnp.minimum(i, blocks - 1)

    def up_block(i, c):
        late = jnp.maximum(i - blocks, 0)
        half = late % halves
        side = jnp.where(late < halves, 1 - c[0], c[0])
        return (2 * half + side, 0)

    out = jax.ShapeDtypeStruct((halves, rows, quarter), jnp.bfloat16)
    return pl.pallas_call(
        branch_kernel,
        out_shape=(out, out),
        grid_spec=pltpu.PrefetchScalarGridSpec(
            num_scalar_prefetch=1,
            grid=(blocks + 2 * halves,),
            in_specs=[
                whole,
                whole,
                pl.BlockSpec((HIDDEN_BLOCK, width), lambda i, c: (hidden_block(i), 0)),
                pl.BlockSpec((rows, HIDDEN_BLOCK), lambda i, c: (0, hidden_block(i))),
                pl.BlockSpec((quarter, hidden), up_block),
            ],
            out_specs=(
                pl.BlockSpec(
                    (1, rows, quarter), lambda i, c: (jnp.clip(i - blocks, 0, halves - 1), 0, 0)
                ),
                pl.BlockSpec(
                    (1, rows, quarter),
                    lambda i, c: (jnp.clip(i - blocks - halves, 0, halves - 1), 0, 0),
                ),
            ),
            scratch_shapes=[pltpu.VMEM((blocks, rows, HIDDEN_BLOCK), jnp.bfloat16)],
        ),
        compiler_params=pltpu.CompilerParams(
            dimension_semantics=("arbitrary",), vmem_limit_bytes=VMEM_LIMIT
        ),
        name="branch",
    )(core, mine, other, down, factors, up)


def slots(route_now, share_now):
    rows = route_now.shape[0]
    named = route_now.T[None] == jnp.arange(EXPERTS, dtype=jnp.int32)[:, None, None]
    chosen = jnp.any(named, axis=1)
    mix = jnp.sum(jnp.where(named, share_now.T[None], 0.0), axis=1)
    token = jnp.arange(rows, dtype=jnp.int32)
    earlier = (token[:, None] < token[None, :]).astype(jnp.bfloat16)
    before = jnp.dot(
        chosen.astype(jnp.bfloat16), earlier, preferred_element_type=jnp.float32
    ).astype(jnp.int32)
    place = jnp.where(chosen, before, -1)
    hit = place[:, None, :] == jnp.arange(CAPACITY, dtype=jnp.int32)[None, :, None]
    mixing = jnp.where(hit, mix[:, None, :], 0.0).reshape(EXPERTS * CAPACITY, rows)
    return hit, mixing


def per_device(grad_in, saved_input, routes, route_weights, plan, up_weight, down_weight):
    n_expert = lax.axis_size("expert")
    n_xhi = lax.axis_size("xhi")
    n_section = lax.axis_size("section")
    per_expert = n_expert // EXPERTS
    peers = n_xhi * n_expert
    rows, quarter = grad_in.shape[1:]
    up_local = up_weight[0]
    down_local = down_weight[0]
    core = lax.axis_index("core").astype(jnp.int32).reshape(1)

    def swap_cores(value):
        return lax.ppermute(value, "core", [(0, 1), (1, 0)])

    def exchange(value):
        return lax.all_to_all(value, ("xhi", "expert"), split_axis=0, concat_axis=0, tiled=True)

    def dispatch(hit, value):
        select = jnp.broadcast_to(
            hit[None, :, None], (n_xhi, EXPERTS, per_expert, CAPACITY, rows)
        ).reshape(peers * CAPACITY, rows)
        sent = jnp.dot(
            select.astype(jnp.bfloat16), value, preferred_element_type=jnp.float32
        ).astype(jnp.bfloat16)
        got = exchange(sent.reshape(peers, CAPACITY, quarter))
        mine = got.reshape(n_xhi, n_expert * CAPACITY, quarter)
        return mine, swap_cores(mine)

    ticks = []
    for step_index in range(plan.shape[1]):
        micro = plan[0, step_index]
        saved_now = lax.dynamic_index_in_dim(saved_input[0], micro, 0, keepdims=False)
        route_now = lax.dynamic_index_in_dim(routes[0], micro, 0, keepdims=False)
        share_now = lax.dynamic_index_in_dim(route_weights[0], micro, 0, keepdims=False)
        hit, mixing = slots(route_now, share_now)
        ticks.append((saved_now, hit, mixing))

    current = grad_in[0]
    for saved_now, hit, mixing in ticks:
        factors = factor(core, *dispatch(hit, saved_now), up_local)
        send, keep = branch(core, *dispatch(hit, current), down_local, factors, up_local)
        outgoing = (
            keep.astype(jnp.float32) + swap_cores(send).astype(jnp.float32)
        ).astype(jnp.bfloat16)
        arrived = exchange(outgoing.reshape(peers, CAPACITY, quarter))
        summed = jnp.sum(
            arrived.reshape(n_xhi, EXPERTS, per_expert, CAPACITY, quarter).astype(jnp.float32),
            axis=(0, 2),
        )
        moe_term = lax.dot_general(
            mixing,
            summed.reshape(EXPERTS * CAPACITY, quarter),
            (((0,), (0,)), ((), ())),
            precision=lax.Precision.HIGHEST,
            preferred_element_type=jnp.float32,
        )
        result = (current.astype(jnp.float32) + moe_term).astype(jnp.bfloat16)
        current = lax.ppermute(
            result, "section", [(i, (i - 1) % n_section) for i in range(n_section)]
        )
    return current[None]


def solution(mesh):
    sections, experts, parts = (mesh.shape[name] for name in ("section", "expert", "mp"))
    refined = Mesh(
        mesh.devices.reshape(sections, experts, parts // 2, 2),
        ("section", "expert", "xhi", "core"),
    )
    mp = ("xhi", "core")
    placed = (
        P("section", "expert", mp),
        P("section", None, "expert", mp),
        P("section", None, "expert", None),
        P("section", None, "expert", None),
        P("section", None),
        P("section", None, ("expert", "xhi", "core")),
        P("section", ("expert", "xhi", "core"), None),
    )
    return jax.shard_map(
        per_device,
        mesh=refined,
        in_specs=placed,
        out_specs=P("section", "expert", mp),
        check_vma=False,
    )
```

time: 484 us -> 256 us (0.53)
  waiting for transfers between devices: 333 us -> 140 us
  Pallas kernels: 0 us -> 41.1 us
  matrix products: 38.5 us -> 9.32 us
  local copies, waits for them, and re-layouts: 31.5 us -> 8.06 us
  starting transfers between devices: 67.2 us -> 47.5 us
    all_to_all x6, waiting for transfers between devices: 324 us -> 127 us  [exchange(): lax.all_to_all(value, ('xhi', 'expert'), split_axis=0, concat_axis=0, til...]
    pallas_call x0 -> x4, Pallas kernels: none -> 41.1 us  [the longest x2 27.3 us: branch(): pl.pallas_call(branch_kernel, out_shape=(out, out), grid_spec=pltpu.Prefe...]
    dot_general x10 -> x6, matrix products: 36.8 us -> 7.63 us  [the longest x4 7.36 us: dispatch(): jnp.dot(select.astype(jnp.bfloat16), value, preferred_element_type=jnp.fl...]
    all_to_all x6, starting transfers between devices: 55.4 us -> 34.5 us  [exchange(): lax.all_to_all(value, ('xhi', 'expert'), split_axis=0, concat_axis=0, til...]
    transpose x4 -> x2, local copies, waits for them, and re-layouts: 11.9 us -> 0.71 us  [the longest x1 0.7 us: slots(): route_now.T[None] == jnp.arange(EXPERTS, dtype=jnp.int32)[:, None, None]]
    broadcast_in_dim x5 -> x2, local copies, waits for them, and re-layouts: 9.14 us -> 0.08 us  [dispatch(): jnp.broadcast_to(hit[None, :, None], (n_xhi, EXPERTS, per_expert, CAPACIT...]
    reduce_sum x7 -> x4, other arithmetic: 7.31 us -> 2.1 us  [the longest x2 2.07 us: per_device(): jnp.sum(arrived.reshape(n_xhi, EXPERTS, per_expert, CAPACITY, quarter).as...]
    ppermute x2 -> x8, waiting for transfers between devices: 8.44 us -> 13.2 us  [the longest x6 6.65 us: swap_cores(): return lax.ppermute(value, 'core', [(0, 1), (1, 0)])]
  transfers between devices with their start and end apart: 8 -> 14, of which waited for: 8 -> 10; matrix products, arithmetic and copies ran while one was open for 3% -> 3% of each run, Pallas kernels for 0% -> 5%
where the time goes in v1:
time: 256 us; the launch traced here: 255 us
  waiting for transfers between devices  140 us (55%)
  starting transfers between devices  47.5 us (19%)
  Pallas kernels  41.1 us (16%)
  matrix products  9.32 us (4%)
  local copies, waits for them, and re-layouts  8.06 us (3%)
  other arithmetic  5.56 us (2%)
  between operations  4 us (2%)
    all_to_all x6, waiting for transfers between devices, exchange(): lax.all_to_all(value, ('xhi', 'expert'), split_axis=0, concat_axis=0, til...  127 us
    all_to_all x6, starting transfers between devices, exchange(): lax.all_to_all(value, ('xhi', 'expert'), split_axis=0, concat_axis=0, til...  34.5 us
    pallas_call x2, Pallas kernels, branch(): pl.pallas_call(branch_kernel, out_shape=(out, out), grid_spec=pltpu.Prefe...  27.3 us
    pallas_call x2, Pallas kernels, factor(): pl.pallas_call(factor_kernel, out_shape=jax.ShapeDtypeStruct((rows, hidde...  13.8 us
    ppermute x2, starting transfers between devices, per_device(): lax.ppermute(result, 'section', [(i, (i - 1) % n_section) for i in range(...  11.8 us
    dot_general x4, matrix products, dispatch(): jnp.dot(select.astype(jnp.bfloat16), value, preferred_element_type=jnp.fl...  7.36 us
    ppermute x6, waiting for transfers between devices, swap_cores(): return lax.ppermute(value, 'core', [(0, 1), (1, 0)])  6.65 us
    ppermute x2, waiting for transfers between devices, per_device(): lax.ppermute(result, 'section', [(i, (i - 1) % n_section) for i in range(...  6.56 us
  transfers between devices with their start and end apart: 14, of which 10 were waited for; matrix products, arithmetic and copies ran while one was open for 3% of the time, Pallas kernels for 5%

profile of v1, /device:TPU:8, one launch (start us, length us, event | category | flops | bytes accessed | tf_op | source)
XLA Modules:
  0.0 255.3 jit_solution(5091522960166179397)
XLA Ops:
  0.0 0.0 copy-start
  0.0 1.3 fusion.27
  5.2 0.7 fusion.23
  5.9 0.1 fusion.3
  6.1 0.0 copy-done
  6.1 1.9 convolution_convert_fusion.2
  8.0 0.0 copy-start.5
  8.0 7.5 %all-to-all-start.1 = ((bf16[16,72,768]{2,1,0:T(8,128)(2,1)}), bf16[16,72,768]{2,1,0:T(8,128)(2,1)S(1)}, u32[]{:S(2)}, u32[]{:S(2)}) async-start(bf16[16,72,768]{2,1,0:T(8,128)(2,1)} %bitcast.78), calls=%async_computation.1 | async-start | bytes 3538944 | tf_op jit(solution)/shard_map/all_to_all | solution.py:173
  15.5 0.0 copy-done.5
  15.5 1.8 convolution_convert_fusion.3
  17.3 23.0 %all-to-all-done.1 = bf16[16,72,768]{2,1,0:T(8,128)(2,1)S(1)} async-done(((bf16[16,72,768]{2,1,0:T(8,128)(2,1)}), bf16[16,72,768]{2,1,0:T(8,128)(2,1)S(1)}, u32[]{:S(2)}, u32[]{:S(2)}) %all-to-all-start.1) | async-done | bytes 1769504 | tf_op jit(solution)/shard_map/all_to_all | solution.py:173
  40.3 5.6 %all-to-all-start = ((bf16[16,72,768]{2,1,0:T(8,128)(2,1)}), bf16[16,72,768]{2,1,0:T(8,128)(2,1)}, u32[]{:S(2)}, u32[]{:S(2)}) async-start(bf16[16,72,768]{2,1,0:T(8,128)(2,1)} %bitcast.80), calls=%async_computation | async-start | bytes 3538944 | tf_op jit(solution)/shard_map/all_to_all | solution.py:173
  45.9 0.0 collective-permute-start.1
  46.0 22.3 %all-to-all-done = bf16[16,72,768]{2,1,0:T(8,128)(2,1)} async-done(((bf16[16,72,768]{2,1,0:T(8,128)(2,1)}), bf16[16,72,768]{2,1,0:T(8,128)(2,1)}, u32[]{:S(2)}, u32[]{:S(2)}) %all-to-all-start) | async-done | bytes 1769504 | tf_op jit(solution)/shard_map/all_to_all | solution.py:173
  68.2 0.0 collective-permute-start
  68.2 0.0 collective-permute-done.1.other_ref
  68.2 6.9 %factor.2.factor_ref = f32[576,1024]{1,0:T(8,128)S(1)} custom-call(s32[1]{0:T(128)} %bitcast.6.core_ref, bf16[2,576,768]{2,1,0:T(8,128)(2,1)S(1)} %bitcast.70, bf16[2,576,768]{2,1,0:T(8,128)(2,1)} %collective-permute-done.1.other_ref, bf16[3072,1024]{1,0:T(8,128)(2,1)} %bitcast.71), custom_call_target="tpu_custom_call" | custom-call | tf_op jit(solution)/shard_map/factor/pallas_call | solution.py:41
  75.1 0.0 copy-start.2
  75.1 1.4 copy-done.2
  76.5 0.0 collective-permute-done.other_ref
  76.5 13.7 %branch.2 = (bf16[2,576,768]{2,1,0:T(8,128)(2,1)S(1)}, bf16[2,576,768]{2,1,0:T(8,128)(2,1)S(1)}) custom-call(s32[1]{0:T(128)} %bitcast.6.core_ref, bf16[2,576,768]{2,1,0:T(8,128)(2,1)} %bitcast.9.mine_ref, bf16[2,576,768]{2,1,0:T(8,128)(2,1)} %collective-permute-done.other_ref, bf16[1024,3072]{1,0:T(8,128)(2,1)} %bitcast.75, f32[576,1024]{1,0:T(8,128)} %copy-done.2, ...), custom_call_target="tpu_custom_call" | custom-call | tf_op jit(solution)/shard_map/branch/pallas_call | solution.py:111
  90.2 0.6 collective-permute-start.2
  90.8 3.3 %collective-permute-done.2 = bf16[2,576,768]{2,1,0:T(8,128)(2,1)S(1)} collective-permute-done((bf16[2,576,768]{2,1,0:T(8,128)(2,1)S(1)}, bf16[2,576,768]{2,1,0:T(8,128)(2,1)S(1)}, u32[]{:S(2)}, u32[]{:S(2)}) %collective-permute-start.2) | collective-permute-done | bytes 1769504 | tf_op jit(solution)/shard_map/ppermute | solution.py:170
  94.1 1.7 add_convert_fusion.1
  95.8 5.7 %all-to-all-start.2 = ((bf16[16,72,768]{2,1,0:T(8,128)(2,1)}), bf16[16,72,768]{2,1,0:T(8,128)(2,1)S(1)}, u32[]{:S(2)}, u32[]{:S(2)}) async-start(bf16[16,72,768]{2,1,0:T(8,128)(2,1)} %bitcast.83), calls=%async_computation.2 | async-start | bytes 3538944 | tf_op jit(solution)/shard_map/all_to_all | solution.py:173
  101.5 0.1 fusion.2
  101.7 1.9 convolution_convert_fusion
  103.6 23.9 %all-to-all-done.2 = bf16[16,72,768]{2,1,0:T(8,128)(2,1)S(1)} async-done(((bf16[16,72,768]{2,1,0:T(8,128)(2,1)}), bf16[16,72,768]{2,1,0:T(8,128)(2,1)S(1)}, u32[]{:S(2)}, u32[]{:S(2)}) %all-to-all-start.2) | async-done | bytes 1769504 | tf_op jit(solution)/shard_map/all_to_all | solution.py:173
  127.5 0.0 copy-start.3
  127.5 0.0 copy-start.6
  127.5 1.2 copy-done.3
  128.7 5.2 %all-to-all-start.4 = ((bf16[16,72,768]{2,1,0:T(8,128)(2,1)}), bf16[16,72,768]{2,1,0:T(8,128)(2,1)S(1)}, u32[]{:S(2)}, u32[]{:S(2)}) async-start(bf16[16,72,768]{2,1,0:T(8,128)(2,1)} %bitcast.77), calls=%async_computation.4 | async-start | bytes 3538944 | tf_op jit(solution)/shard_map/all_to_all | solution.py:173
  133.9 0.0 copy-done.6
  134.0 1.8 convert_reduce_fusion.1
  135.8 0.8 fusion.1
  136.7 5.9 %collective-permute-start.3 = (bf16[128,768]{1,0:T(8,128)(2,1)S(1)}, bf16[128,768]{1,0:T(8,128)(2,1)S(1)}, u32[]{:S(2)}, u32[]{:S(2)}) collective-permute-start(bf16[128,768]{1,0:T(8,128)(2,1)S(1)} %fusion.1), channel_id=1, source_target_pairs={{0,224},{32,0},{64,32},{96,64},{128,96},{160,128},{192,160},{224,1... | collective-permute-start | bytes 589832 | tf_op jit(solution)/shard_map/ppermute | solution.py:215
  142.6 3.2 %collective-permute-done.3 = bf16[128,768]{1,0:T(8,128)(2,1)S(1)} collective-permute-done((bf16[128,768]{1,0:T(8,128)(2,1)S(1)}, bf16[128,768]{1,0:T(8,128)(2,1)S(1)}, u32[]{:S(2)}, u32[]{:S(2)}) %collective-permute-start.3) | collective-permute-done | bytes 196640 | tf_op jit(solution)/shard_map/ppermute | solution.py:215
  145.8 1.8 convolution_convert_fusion.1
  147.6 10.1 %all-to-all-done.4 = bf16[16,72,768]{2,1,0:T(8,128)(2,1)S(1)} async-done(((bf16[16,72,768]{2,1,0:T(8,128)(2,1)}), bf16[16,72,768]{2,1,0:T(8,128)(2,1)S(1)}, u32[]{:S(2)}, u32[]{:S(2)}) %all-to-all-start.4) | async-done | bytes 1769504 | tf_op jit(solution)/shard_map/all_to_all | solution.py:173
  157.7 5.6 %all-to-all-start.3 = ((bf16[16,72,768]{2,1,0:T(8,128)(2,1)}), bf16[16,72,768]{2,1,0:T(8,128)(2,1)}, u32[]{:S(2)}, u32[]{:S(2)}) async-start(bf16[16,72,768]{2,1,0:T(8,128)(2,1)} %bitcast.81), calls=%async_computation.3 | async-start | bytes 3538944 | tf_op jit(solution)/shard_map/all_to_all | solution.py:173
  163.3 0.0 collective-permute-start.5
  163.3 21.4 %all-to-all-done.3 = bf16[16,72,768]{2,1,0:T(8,128)(2,1)} async-done(((bf16[16,72,768]{2,1,0:T(8,128)(2,1)}), bf16[16,72,768]{2,1,0:T(8,128)(2,1)}, u32[]{:S(2)}, u32[]{:S(2)}) %all-to-all-start.3) | async-done | bytes 1769504 | tf_op jit(solution)/shard_map/all_to_all | solution.py:173
  184.7 0.0 collective-permute-start.4
  184.7 0.0 collective-permute-done.5.other_ref
  184.7 6.9 %factor.3.factor_ref = f32[576,1024]{1,0:T(8,128)S(1)} custom-call(s32[1]{0:T(128)} %bitcast.6.core_ref, bf16[2,576,768]{2,1,0:T(8,128)(2,1)S(1)} %bitcast.68, bf16[2,576,768]{2,1,0:T(8,128)(2,1)} %collective-permute-done.5.other_ref, bf16[3072,1024]{1,0:T(8,128)(2,1)} %bitcast.73), custom_call_target="tpu_custom_call" | custom-call | tf_op jit(solution)/shard_map/factor/pallas_call | solution.py:41
  191.6 0.0 copy-start.1
  191.6 1.4 copy-done.1
  193.0 0.0 collective-permute-done.4.other_ref
  193.0 0.0 copy-start.4
  193.0 1.2 copy-done.4
  194.3 13.6 %branch.3 = (bf16[2,576,768]{2,1,0:T(8,128)(2,1)S(1)}, bf16[2,576,768]{2,1,0:T(8,128)(2,1)S(1)}) custom-call(s32[1]{0:T(128)} %bitcast.6.core_ref, bf16[2,576,768]{2,1,0:T(8,128)(2,1)} %bitcast.25.mine_ref, bf16[2,576,768]{2,1,0:T(8,128)(2,1)} %copy-done.4, bf16[1024,3072]{1,0:T(8,128)(2,1)} %bitcast.76, f32[576,1024]{1,0:T(8,128)} %copy-done.1, ...), custom_call_target="tpu_custom_call" | custom-call | tf_op jit(solution)/shard_map/branch/pallas_call | solution.py:111
  207.9 0.6 collective-permute-start.6
  208.5 3.3 %collective-permute-done.6 = bf16[2,576,768]{2,1,0:T(8,128)(2,1)S(1)} collective-permute-done((bf16[2,576,768]{2,1,0:T(8,128)(2,1)S(1)}, bf16[2,576,768]{2,1,0:T(8,128)(2,1)S(1)}, u32[]{:S(2)}, u32[]{:S(2)}) %collective-permute-start.6) | collective-permute-done | bytes 1769504 | tf_op jit(solution)/shard_map/ppermute | solution.py:170
  211.8 1.7 add_convert_fusion
  213.5 4.8 %all-to-all-start.5 = ((bf16[16,72,768]{2,1,0:T(8,128)(2,1)}), bf16[16,72,768]{2,1,0:T(8,128)(2,1)S(1)}, u32[]{:S(2)}, u32[]{:S(2)}) async-start(bf16[16,72,768]{2,1,0:T(8,128)(2,1)} %bitcast.84), calls=%async_computation.5 | async-start | bytes 3538944 | tf_op jit(solution)/shard_map/all_to_all | solution.py:173
  218.4 25.8 %all-to-all-done.5 = bf16[16,72,768]{2,1,0:T(8,128)(2,1)S(1)} async-done(((bf16[16,72,768]{2,1,0:T(8,128)(2,1)}), bf16[16,72,768]{2,1,0:T(8,128)(2,1)S(1)}, u32[]{:S(2)}, u32[]{:S(2)}) %all-to-all-start.5) | async-done | bytes 1769504 | tf_op jit(solution)/shard_map/all_to_all | solution.py:173
  244.2 0.2 convert_reduce_fusion
  244.4 0.8 add_convert_fusion.2
  245.3 5.9 %collective-permute-start.7 = (bf16[128,768]{1,0:T(8,128)(2,1)S(1)}, bf16[128,768]{1,0:T(8,128)(2,1)S(1)}, u32[]{:S(2)}, u32[]{:S(2)}) collective-permute-start(bf16[128,768]{1,0:T(8,128)(2,1)S(1)} %add_convert_fusion.2), channel_id=1, source_target_pairs={{0,224},{32,0},{64,32},{96,64},{128,96},{160,128},{192,160},{224,1... | collective-permute-start | bytes 589832 | tf_op jit(solution)/shard_map/ppermute | solution.py:215
  251.2 3.4 %collective-permute-done.7 = bf16[128,768]{1,0:T(8,128)(2,1)S(1)} collective-permute-done((bf16[128,768]{1,0:T(8,128)(2,1)S(1)}, bf16[128,768]{1,0:T(8,128)(2,1)S(1)}, u32[]{:S(2)}, u32[]{:S(2)}) %collective-permute-start.7) | collective-permute-done | bytes 196640 | tf_op jit(solution)/shard_map/ppermute | solution.py:215
  254.6 0.7 copy.9
  (9 shorter events, 0.2 us)
Async XLA Ops:
  0.0 6.1 %copy-start = (bf16[1,2,128,768]{3,2,1,0:T(8,128)(2,1)S(1)}, bf16[1,2,128,768]{3,2,1,0:T(8,128)(2,1)}, u32[]{:S(2)}) copy-start(bf16[1,2,128,768]{3,2,1,0:T(8,128)(2,1)} %param.8) | copy-start | bytes 1179652
  8.0 7.5 %copy-start.5 = (bf16[1,128,768]{2,1,0:T(8,128)(2,1)S(1)}, bf16[1,128,768]{2,1,0:T(8,128)(2,1)}, u32[]{:S(2)}) copy-start(bf16[1,128,768]{2,1,0:T(8,128)(2,1)} %param.7) | copy-start | bytes 589828
  8.0 32.4 %all-to-all-start.1 = ((bf16[16,72,768]{2,1,0:T(8,128)(2,1)}), bf16[16,72,768]{2,1,0:T(8,128)(2,1)S(1)}, u32[]{:S(2)}, u32[]{:S(2)}) async-start(bf16[16,72,768]{2,1,0:T(8,128)(2,1)} %bitcast.78), calls=%async_computation.1 | async-start | bytes 3538944 | tf_op jit(solution)/shard_map/all_to_all | solution.py:173
  40.3 27.9 %all-to-all-start = ((bf16[16,72,768]{2,1,0:T(8,128)(2,1)}), bf16[16,72,768]{2,1,0:T(8,128)(2,1)}, u32[]{:S(2)}, u32[]{:S(2)}) async-start(bf16[16,72,768]{2,1,0:T(8,128)(2,1)} %bitcast.80), calls=%async_computation | async-start | bytes 3538944 | tf_op jit(solution)/shard_map/all_to_all | solution.py:173
  45.9 22.3 %collective-permute-start.1 = (bf16[2,576,768]{2,1,0:T(8,128)(2,1)S(1)}, bf16[2,576,768]{2,1,0:T(8,128)(2,1)}, u32[]{:S(2)}, u32[]{:S(2)}) collective-permute-start(bf16[2,576,768]{2,1,0:T(8,128)(2,1)S(1)} %bitcast.69), channel_id=1, source_target_pairs={{0,1},{1,0},{2,3},{3,2},{4,5},{5,4},{6,7},{7,6},{8,9},{9,8},{10,11... | collective-permute-start | bytes 5308424 | tf_op jit(solution)/shard_map/ppermute | solution.py:170
  68.2 8.3 %collective-permute-start = (bf16[2,576,768]{2,1,0:T(8,128)(2,1)}, bf16[2,576,768]{2,1,0:T(8,128)(2,1)}, u32[]{:S(2)}, u32[]{:S(2)}) collective-permute-start(bf16[2,576,768]{2,1,0:T(8,128)(2,1)} %bitcast.9.mine_ref), channel_id=1, source_target_pairs={{0,1},{1,0},{2,3},{3,2},{4,5},{5,4},{6,7},{7,6},{8,9},{9,8},{10,11... | collective-permute-start | bytes 5308424 | tf_op jit(solution)/shard_map/ppermute | solution.py:170
  75.1 1.4 copy-start.2
  90.2 3.9 %collective-permute-start.2 = (bf16[2,576,768]{2,1,0:T(8,128)(2,1)S(1)}, bf16[2,576,768]{2,1,0:T(8,128)(2,1)S(1)}, u32[]{:S(2)}, u32[]{:S(2)}) collective-permute-start(bf16[2,576,768]{2,1,0:T(8,128)(2,1)S(1)} %get-tuple-element.10), channel_id=1, source_target_pairs={{0,1},{1,0},{2,3},{3,2},{4,5},{5,4},{6,7},{7,6},{8,9},{9,8},{10,11... | collective-permute-start | bytes 5308424 | tf_op jit(solution)/shard_map/ppermute | solution.py:170
  95.8 31.7 %all-to-all-start.2 = ((bf16[16,72,768]{2,1,0:T(8,128)(2,1)}), bf16[16,72,768]{2,1,0:T(8,128)(2,1)S(1)}, u32[]{:S(2)}, u32[]{:S(2)}) async-start(bf16[16,72,768]{2,1,0:T(8,128)(2,1)} %bitcast.83), calls=%async_computation.2 | async-start | bytes 3538944 | tf_op jit(solution)/shard_map/all_to_all | solution.py:173
  127.5 1.2 copy-start.3
  127.5 6.4 %copy-start.6 = (f32[1,2,128,2]{2,3,1,0:T(2,128)S(1)}, f32[1,2,128,2]{2,3,1,0:T(2,128)}, u32[]{:S(2)}) copy-start(f32[1,2,128,2]{2,3,1,0:T(2,128)} %param.10) | copy-start | bytes 6148
  128.7 29.0 %all-to-all-start.4 = ((bf16[16,72,768]{2,1,0:T(8,128)(2,1)}), bf16[16,72,768]{2,1,0:T(8,128)(2,1)S(1)}, u32[]{:S(2)}, u32[]{:S(2)}) async-start(bf16[16,72,768]{2,1,0:T(8,128)(2,1)} %bitcast.77), calls=%async_computation.4 | async-start | bytes 3538944 | tf_op jit(solution)/shard_map/all_to_all | solution.py:173
  136.7 9.1 %collective-permute-start.3 = (bf16[128,768]{1,0:T(8,128)(2,1)S(1)}, bf16[128,768]{1,0:T(8,128)(2,1)S(1)}, u32[]{:S(2)}, u32[]{:S(2)}) collective-permute-start(bf16[128,768]{1,0:T(8,128)(2,1)S(1)} %fusion.1), channel_id=1, source_target_pairs={{0,224},{32,0},{64,32},{96,64},{128,96},{160,128},{192,160},{224,1... | collective-permute-start | bytes 589832 | tf_op jit(solution)/shard_map/ppermute | solution.py:215
  157.7 27.0 %all-to-all-start.3 = ((bf16[16,72,768]{2,1,0:T(8,128)(2,1)}), bf16[16,72,768]{2,1,0:T(8,128)(2,1)}, u32[]{:S(2)}, u32[]{:S(2)}) async-start(bf16[16,72,768]{2,1,0:T(8,128)(2,1)} %bitcast.81), calls=%async_computation.3 | async-start | bytes 3538944 | tf_op jit(solution)/shard_map/all_to_all | solution.py:173
  163.3 21.4 %collective-permute-start.5 = (bf16[2,576,768]{2,1,0:T(8,128)(2,1)S(1)}, bf16[2,576,768]{2,1,0:T(8,128)(2,1)}, u32[]{:S(2)}, u32[]{:S(2)}) collective-permute-start(bf16[2,576,768]{2,1,0:T(8,128)(2,1)S(1)} %bitcast.67), channel_id=1, source_target_pairs={{0,1},{1,0},{2,3},{3,2},{4,5},{5,4},{6,7},{7,6},{8,9},{9,8},{10,11... | collective-permute-start | bytes 5308424 | tf_op jit(solution)/shard_map/ppermute | solution.py:170
  184.7 8.3 %collective-permute-start.4 = (bf16[2,576,768]{2,1,0:T(8,128)(2,1)}, bf16[2,576,768]{2,1,0:T(8,128)(2,1)S(1)}, u32[]{:S(2)}, u32[]{:S(2)}) collective-permute-start(bf16[2,576,768]{2,1,0:T(8,128)(2,1)} %bitcast.25.mine_ref), channel_id=1, source_target_pairs={{0,1},{1,0},{2,3},{3,2},{4,5},{5,4},{6,7},{7,6},{8,9},{9,8},{10,11... | collective-permute-start | bytes 5308424 | tf_op jit(solution)/shard_map/ppermute | solution.py:170
  191.6 1.4 copy-start.1
  193.0 1.2 copy-start.4
  207.9 3.9 %collective-permute-start.6 = (bf16[2,576,768]{2,1,0:T(8,128)(2,1)S(1)}, bf16[2,576,768]{2,1,0:T(8,128)(2,1)S(1)}, u32[]{:S(2)}, u32[]{:S(2)}) collective-permute-start(bf16[2,576,768]{2,1,0:T(8,128)(2,1)S(1)} %get-tuple-element.12), channel_id=1, source_target_pairs={{0,1},{1,0},{2,3},{3,2},{4,5},{5,4},{6,7},{7,6},{8,9},{9,8},{10,11... | collective-permute-start | bytes 5308424 | tf_op jit(solution)/shard_map/ppermute | solution.py:170
  213.5 30.7 %all-to-all-start.5 = ((bf16[16,72,768]{2,1,0:T(8,128)(2,1)}), bf16[16,72,768]{2,1,0:T(8,128)(2,1)S(1)}, u32[]{:S(2)}, u32[]{:S(2)}) async-start(bf16[16,72,768]{2,1,0:T(8,128)(2,1)} %bitcast.84), calls=%async_computation.5 | async-start | bytes 3538944 | tf_op jit(solution)/shard_map/all_to_all | solution.py:173
  245.3 9.3 %collective-permute-start.7 = (bf16[128,768]{1,0:T(8,128)(2,1)S(1)}, bf16[128,768]{1,0:T(8,128)(2,1)S(1)}, u32[]{:S(2)}, u32[]{:S(2)}) collective-permute-start(bf16[128,768]{1,0:T(8,128)(2,1)S(1)} %add_convert_fusion.2), channel_id=1, source_target_pairs={{0,224},{32,0},{64,32},{96,64},{128,96},{160,128},{192,160},{224,1... | collective-permute-start | bytes 589832 | tf_op jit(solution)/shard_map/ppermute | solution.py:215

commit v2 on v1

--- a/solution.py
+++ b/solution.py
@@ -8,7 +8,11 @@
 EXPERTS = 4
 CAPACITY = 72
 HIDDEN_BLOCK = 256
-VMEM_LIMIT = 48 * 1024 * 1024
+VMEM_LIMIT = 32 * 1024 * 1024
+
+
+def together(*values):
+    return lax.optimization_barrier(values)
 
 
 def contract_last(left, right):
@@ -40,7 +44,7 @@
     whole = pl.BlockSpec((halves, rows, quarter), lambda i, c: (0, 0, 0))
     return pl.pallas_call(
         factor_kernel,
-        out_shape=jax.ShapeDtypeStruct((rows, hidden), jnp.float32),
+        out_shape=pltpu.HBM((rows, hidden), jnp.float32),
         grid_spec=pltpu.PrefetchScalarGridSpec(
             num_scalar_prefetch=1,
             grid=(hidden // HIDDEN_BLOCK,),
@@ -49,6 +53,11 @@
         ),
         compiler_params=pltpu.CompilerParams(
             dimension_semantics=("arbitrary",), vmem_limit_bytes=VMEM_LIMIT
+        ),
+        cost_estimate=pl.CostEstimate(
+            flops=2 * rows * width * hidden,
+            transcendentals=2 * rows * hidden,
+            bytes_accessed=2 * width * (rows + hidden) + 4 * rows * hidden,
         ),
         name="factor",
     )(core, mine, other, up)
@@ -135,6 +144,11 @@
         compiler_params=pltpu.CompilerParams(
             dimension_semantics=("arbitrary",), vmem_limit_bytes=VMEM_LIMIT
         ),
+        cost_estimate=pl.CostEstimate(
+            flops=4 * rows * hidden,
+            transcendentals=0,
+            bytes_accessed=4 * rows * hidden,
+        ),
         name="branch",
     )(core, mine, other, down, factors, up)
 
@@ -162,8 +176,8 @@
     per_expert = n_expert // EXPERTS
     peers = n_xhi * n_expert
     rows, quarter = grad_in.shape[1:]
-    up_local = up_weight[0]
-    down_local = down_weight[0]
+    up_local = pltpu.with_memory_space_constraint(up_weight[0], pltpu.HBM)
+    down_local = pltpu.with_memory_space_constraint(down_weight[0], pltpu.HBM)
     core = lax.axis_index("core").astype(jnp.int32).reshape(1)
 
     def swap_cores(value):
@@ -172,49 +186,67 @@
     def exchange(value):
         return lax.all_to_all(value, ("xhi", "expert"), split_axis=0, concat_axis=0, tiled=True)
 
-    def dispatch(hit, value):
-        select = jnp.broadcast_to(
+    def select(hit, value):
+        picks = jnp.broadcast_to(
             hit[None, :, None], (n_xhi, EXPERTS, per_expert, CAPACITY, rows)
         ).reshape(peers * CAPACITY, rows)
         sent = jnp.dot(
-            select.astype(jnp.bfloat16), value, preferred_element_type=jnp.float32
+            picks.astype(jnp.bfloat16), value, preferred_element_type=jnp.float32
         ).astype(jnp.bfloat16)
-        got = exchange(sent.reshape(peers, CAPACITY, quarter))
-        mine = got.reshape(n_xhi, n_expert * CAPACITY, quarter)
-        return mine, swap_cores(mine)
-
-    ticks = []
+        return sent.reshape(peers, CAPACITY, quarter)
+
+    def deliver(sent):
+        return exchange(sent).reshape(n_xhi, n_expert * CAPACITY, quarter)
+
+    def combine(current, mixing, arrived):
+        summed = jnp.sum(
+            arrived.reshape(n_xhi, EXPERTS, per_expert, CAPACITY, quarter).astype(jnp.float32),
+            axis=(0, 2),
+        )
+        moe_term = lax.dot_general(
+            mixing,
+            summed.reshape(EXPERTS * CAPACITY, quarter),
+            (((0,), (0,)), ((), ())),
+            precision=lax.Precision.HIGHEST,
+            preferred_element_type=jnp.float32,
+        )
+        result = (current.astype(jnp.float32) + moe_term).astype(jnp.bfloat16)
+        return lax.ppermute(
+            result, "section", [(i, (i - 1) % n_section) for i in range(n_section)]
+        )
+
+    def outgoing(send, keep):
+        return (
+            keep.astype(jnp.float32) + swap_cores(send).astype(jnp.float32)
+        ).astype(jnp.bfloat16).reshape(peers, CAPACITY, quarter)
+
+    picked = []
     for step_index in range(plan.shape[1]):
         micro = plan[0, step_index]
         saved_now = lax.dynamic_index_in_dim(saved_input[0], micro, 0, keepdims=False)
         route_now = lax.dynamic_index_in_dim(routes[0], micro, 0, keepdims=False)
         share_now = lax.dynamic_index_in_dim(route_weights[0], micro, 0, keepdims=False)
         hit, mixing = slots(route_now, share_now)
-        ticks.append((saved_now, hit, mixing))
-
+        picked.append((hit, mixing, select(hit, saved_now)))
+
+    ticks = len(picked)
     current = grad_in[0]
-    for saved_now, hit, mixing in ticks:
-        factors = factor(core, *dispatch(hit, saved_now), up_local)
-        send, keep = branch(core, *dispatch(hit, current), down_local, factors, up_local)
-        outgoing = (
-            keep.astype(jnp.float32) + swap_cores(send).astype(jnp.float32)
-        ).astype(jnp.bfloat16)
-        arrived = exchange(outgoing.reshape(peers, CAPACITY, quarter))
-        summed = jnp.sum(
-            arrived.reshape(n_xhi, EXPERTS, per_expert, CAPACITY, quarter).astype(jnp.float32),
-            axis=(0, 2),
-        )
-        moe_term = lax.dot_general(
-            mixing,
-            summed.reshape(EXPERTS * CAPACITY, quarter),
-            (((0,), (0,)), ((), ())),
-            precision=lax.Precision.HIGHEST,
-            preferred_element_type=jnp.float32,
-        )
-        result = (current.astype(jnp.float32) + moe_term).astype(jnp.bfloat16)
-        current = lax.ppermute(
-            result, "section", [(i, (i - 1) % n_section) for i in range(n_section)]
-        )
+    saved_rows = deliver(picked[0][2])
+    for tick in range(ticks):
+        hit, mixing, _ = picked[tick]
+        grad_sent, saved_rows = together(select(hit, current), saved_rows)
+        grad_rows = deliver(grad_sent)
+        factors = pltpu.with_memory_space_constraint(
+            factor(core, saved_rows, swap_cores(saved_rows), up_local), pltpu.HBM
+        )
+        grad_rows, factors = together(grad_rows, factors)
+        if tick + 1 < ticks:
+            saved_sent, grad_rows = together(picked[tick + 1][2], grad_rows)
+            saved_rows = deliver(saved_sent)
+        send, keep = branch(core, grad_rows, swap_cores(grad_rows), down_local, factors, up_local)
+        if tick + 1 < ticks:
+            send, saved_rows = together(send, saved_rows)
+        current = combine(current, mixing, exchange(outgoing(send, keep)))
     return current[None]
 
 

time: 256 us -> 248 us (0.969)
  waiting for transfers between devices: 140 us -> 134 us
  local copies, waits for them, and re-layouts: 8.06 us -> 5.24 us
    all_to_all x6, waiting for transfers between devices: 127 us -> 117 us  [exchange(): lax.all_to_all(value, ('xhi', 'expert'), split_axis=0, concat_axis=0, til...]
    ppermute x6, waiting for transfers between devices: 6.65 us -> 11.1 us  [swap_cores(): return lax.ppermute(value, 'core', [(0, 1), (1, 0)])]
    pallas_call x2, Pallas kernels: 13.8 us -> 17 us  [factor(): pl.pallas_call(factor_kernel, out_shape=pltpu.HBM((rows, hidden), jnp.flo...]
    unnamed x15 -> x11, local copies, waits for them, and re-layouts: 5.95 us -> 3.13 us
  transfers between devices with their start and end apart: 14 -> 14, of which waited for: 10 -> 11; matrix products, arithmetic and copies ran while one was open for 3% -> 2% of each run, Pallas kernels for 5% -> 12%
where the time goes in v2:
time: 248 us; the launch traced here: 247 us
  waiting for transfers between devices  134 us (54%)
  starting transfers between devices  46.2 us (19%)
  Pallas kernels  42.5 us (17%)
  matrix products  9.39 us (4%)
  other arithmetic  5.46 us (2%)
  local copies, waits for them, and re-layouts  5.24 us (2%)
  between operations  3.77 us (2%)
    all_to_all x6, waiting for transfers between devices, exchange(): lax.all_to_all(value, ('xhi', 'expert'), split_axis=0, concat_axis=0, til...  117 us
    all_to_all x6, starting transfers between devices, exchange(): lax.all_to_all(value, ('xhi', 'expert'), split_axis=0, concat_axis=0, til...  36.3 us
    pallas_call x2, Pallas kernels, branch(): pl.pallas_call(branch_kernel, out_shape=(out, out), grid_spec=pltpu.Prefe...  25.6 us
    pallas_call x2, Pallas kernels, factor(): pl.pallas_call(factor_kernel, out_shape=pltpu.HBM((rows, hidden), jnp.flo...  17 us
    ppermute x6, waiting for transfers between devices, swap_cores(): return lax.ppermute(value, 'core', [(0, 1), (1, 0)])  11.1 us
    ppermute x2, starting transfers between devices, combine(): lax.ppermute(result, 'section', [(i, (i - 1) % n_section) for i in range(...  9.7 us
    dot_general x4, matrix products, select(): jnp.dot(picks.astype(jnp.bfloat16), value, preferred_element_type=jnp.flo...  7.42 us
    ppermute x2, waiting for transfers between devices, combine(): lax.ppermute(result, 'section', [(i, (i - 1) % n_section) for i in range(...  6.38 us
  transfers between devices with their start and end apart: 14, of which 11 were waited for; matrix products, arithmetic and copies ran while one was open for 2% of the time, Pallas kernels for 12%

profile of v2, /device:TPU:8, one launch (start us, length us, event | category | flops | bytes accessed | tf_op | source)
XLA Modules:
  0.0 247.0 jit_solution(14786228248736831226)
XLA Ops:
  0.0 0.0 copy-start
  0.0 1.3 fusion.27
  4.9 0.7 fusion.21
  5.7 0.1 fusion.3
  5.9 0.0 copy-done
  5.9 1.9 convolution_convert_fusion.1
  7.8 0.0 copy-start.3
  7.8 7.5 %all-to-all-start = ((bf16[16,72,768]{2,1,0:T(8,128)(2,1)}), bf16[16,72,768]{2,1,0:T(8,128)(2,1)}, u32[]{:S(2)}, u32[]{:S(2)}) async-start(bf16[16,72,768]{2,1,0:T(8,128)(2,1)} %bitcast.16), calls=%async_computation | async-start | bytes 3538944 | tf_op jit(solution)/shard_map/all_to_all | solution.py:187
  15.3 0.0 copy-done.3
  15.3 1.8 convolution_convert_fusion.2
  17.1 23.1 %all-to-all-done = bf16[16,72,768]{2,1,0:T(8,128)(2,1)} async-done(((bf16[16,72,768]{2,1,0:T(8,128)(2,1)}), bf16[16,72,768]{2,1,0:T(8,128)(2,1)}, u32[]{:S(2)}, u32[]{:S(2)}) %all-to-all-start) | async-done | bytes 1769504 | tf_op jit(solution)/shard_map/all_to_all | solution.py:187
  40.2 0.0 collective-permute-start
  40.3 5.2 %all-to-all-start.1 = ((bf16[16,72,768]{2,1,0:T(8,128)(2,1)}), bf16[16,72,768]{2,1,0:T(8,128)(2,1)S(1)}, u32[]{:S(2)}, u32[]{:S(2)}) async-start(bf16[16,72,768]{2,1,0:T(8,128)(2,1)} %bitcast.78), calls=%async_computation.1 | async-start | bytes 3538944 | tf_op jit(solution)/shard_map/all_to_all | solution.py:187
  45.5 0.1 fusion.2
  45.7 1.9 convolution_convert_fusion.3
  47.5 0.0 collective-permute-done.other_ref
  47.5 8.5 %factor.2.factor_ref = f32[576,1024]{1,0:T(8,128)} custom-call(s32[1]{0:T(128)} %bitcast.6.core_ref, bf16[2,576,768]{2,1,0:T(8,128)(2,1)} %bitcast.17.mine_ref, bf16[2,576,768]{2,1,0:T(8,128)(2,1)} %collective-permute-done.other_ref, bf16[3072,1024]{1,0:T(8,128)(2,1)} %bitcast.73), custom_call_target="tpu_custom_call" | custom-call | flops 3623878656 | bytes 12189696 | tf_op jit(solution)/shard_map/factor/pallas_call | solution.py:45
  56.0 15.3 %all-to-all-done.1 = bf16[16,72,768]{2,1,0:T(8,128)(2,1)S(1)} async-done(((bf16[16,72,768]{2,1,0:T(8,128)(2,1)}), bf16[16,72,768]{2,1,0:T(8,128)(2,1)S(1)}, u32[]{:S(2)}, u32[]{:S(2)}) %all-to-all-start.1) | async-done | bytes 1769504 | tf_op jit(solution)/shard_map/all_to_all | solution.py:187
  71.3 0.0 collective-permute-start.1
  71.3 6.0 %all-to-all-start.2 = ((bf16[16,72,768]{2,1,0:T(8,128)(2,1)}), bf16[16,72,768]{2,1,0:T(8,128)(2,1)}, u32[]{:S(2)}, u32[]{:S(2)}) async-start(bf16[16,72,768]{2,1,0:T(8,128)(2,1)} %bitcast.77), calls=%async_computation.2 | async-start | bytes 3538944 | tf_op jit(solution)/shard_map/all_to_all | solution.py:187
  77.3 0.0 collective-permute-done.1.other_ref
  77.3 13.2 %branch.2 = (bf16[2,576,768]{2,1,0:T(8,128)(2,1)S(1)}, bf16[2,576,768]{2,1,0:T(8,128)(2,1)S(1)}) custom-call(s32[1]{0:T(128)} %bitcast.6.core_ref, bf16[2,576,768]{2,1,0:T(8,128)(2,1)S(1)} %bitcast.68, bf16[2,576,768]{2,1,0:T(8,128)(2,1)} %collective-permute-done.1.other_ref, bf16[1024,3072]{1,0:T(8,128)(2,1)} %bitcast.71, f32[576,1024]{1,0:T(8,128)} %factor.2.factor_ref, ...), custom_call_target="tpu_custom_call" | custom-call | flops 2359296 | bytes 2359296 | tf_op jit(solution)/shard_map/branch/pallas_call | solution.py:120
  90.5 0.0 copy-start.1
  90.5 1.2 copy-done.1
  91.8 0.0 copy-start.2
  91.8 1.2 copy-done.2
  93.0 10.4 %all-to-all-done.2 = bf16[16,72,768]{2,1,0:T(8,128)(2,1)} async-done(((bf16[16,72,768]{2,1,0:T(8,128)(2,1)}), bf16[16,72,768]{2,1,0:T(8,128)(2,1)}, u32[]{:S(2)}, u32[]{:S(2)}) %all-to-all-start.2) | async-done | bytes 1769504 | tf_op jit(solution)/shard_map/all_to_all | solution.py:187
  103.4 0.0 collective-permute-start.2
  103.4 3.9 %collective-permute-done.2 = bf16[2,576,768]{2,1,0:T(8,128)(2,1)S(1)} collective-permute-done((bf16[2,576,768]{2,1,0:T(8,128)(2,1)}, bf16[2,576,768]{2,1,0:T(8,128)(2,1)S(1)}, u32[]{:S(2)}, u32[]{:S(2)}) %collective-permute-start.2) | collective-permute-done | bytes 1769504 | tf_op jit(solution)/shard_map/ppermute | solution.py:184
  107.3 3.2 %add_convert_fusion.1 = bf16[2,576,768]{2,1,0:T(8,128)(2,1)} fusion(bf16[2,576,768]{2,1,0:T(8,128)(2,1)S(1)} %collective-permute-done.2, bf16[2,576,768]{2,1,0:T(8,128)(2,1)} %copy-done.1), kind=kLoop, calls=%fused_computation.3 | loop fusion | flops 3538944 | bytes 5308416 | tf_op jit(solution)/shard_map/convert_element_type | solution.py:221
  110.4 0.0 copy-start.4
  110.4 6.0 %all-to-all-start.3 = ((bf16[16,72,768]{2,1,0:T(8,128)(2,1)}), bf16[16,72,768]{2,1,0:T(8,128)(2,1)S(1)}, u32[]{:S(2)}, u32[]{:S(2)}) async-start(bf16[16,72,768]{2,1,0:T(8,128)(2,1)} %bitcast.82), calls=%async_computation.3 | async-start | bytes 3538944 | tf_op jit(solution)/shard_map/all_to_all | solution.py:187
  116.4 0.0 copy-done.4
  116.5 25.4 %all-to-all-done.3 = bf16[16,72,768]{2,1,0:T(8,128)(2,1)S(1)} async-done(((bf16[16,72,768]{2,1,0:T(8,128)(2,1)}), bf16[16,72,768]{2,1,0:T(8,128)(2,1)S(1)}, u32[]{:S(2)}, u32[]{:S(2)}) %all-to-all-start.3) | async-done | bytes 1769504 | tf_op jit(solution)/shard_map/all_to_all | solution.py:187
  141.9 0.2 convert_reduce_fusion.1
  142.1 0.8 fusion.1
  143.0 5.9 %collective-permute-start.3 = (bf16[128,768]{1,0:T(8,128)(2,1)S(1)}, bf16[128,768]{1,0:T(8,128)(2,1)S(1)}, u32[]{:S(2)}, u32[]{:S(2)}) collective-permute-start(bf16[128,768]{1,0:T(8,128)(2,1)S(1)} %fusion.1), channel_id=1, source_target_pairs={{0,224},{32,0},{64,32},{96,64},{128,96},{160,128},{192,160},{224,1... | collective-permute-start | bytes 589832 | tf_op jit(solution)/shard_map/ppermute | solution.py:214
  148.9 3.2 %collective-permute-done.3 = bf16[128,768]{1,0:T(8,128)(2,1)S(1)} collective-permute-done((bf16[128,768]{1,0:T(8,128)(2,1)S(1)}, bf16[128,768]{1,0:T(8,128)(2,1)S(1)}, u32[]{:S(2)}, u32[]{:S(2)}) %collective-permute-start.3) | collective-permute-done | bytes 196640 | tf_op jit(solution)/shard_map/ppermute | solution.py:214
  152.1 1.9 convolution_convert_fusion
  153.9 0.0 collective-permute-start.4
  153.9 5.0 %all-to-all-start.4 = ((bf16[16,72,768]{2,1,0:T(8,128)(2,1)}), bf16[16,72,768]{2,1,0:T(8,128)(2,1)S(1)}, u32[]{:S(2)}, u32[]{:S(2)}) async-start(bf16[16,72,768]{2,1,0:T(8,128)(2,1)} %bitcast.80), calls=%async_computation.4 | async-start | bytes 3538944 | tf_op jit(solution)/shard_map/all_to_all | solution.py:187
  158.9 0.0 collective-permute-done.4.other_ref
  158.9 8.5 %factor.3.factor_ref = f32[576,1024]{1,0:T(8,128)} custom-call(s32[1]{0:T(128)} %bitcast.6.core_ref, bf16[2,576,768]{2,1,0:T(8,128)(2,1)} %bitcast.21.mine_ref, bf16[2,576,768]{2,1,0:T(8,128)(2,1)} %collective-permute-done.4.other_ref, bf16[3072,1024]{1,0:T(8,128)(2,1)} %bitcast.75), custom_call_target="tpu_custom_call" | custom-call | flops 3623878656 | bytes 12189696 | tf_op jit(solution)/shard_map/factor/pallas_call | solution.py:45
  167.4 17.3 %all-to-all-done.4 = bf16[16,72,768]{2,1,0:T(8,128)(2,1)S(1)} async-done(((bf16[16,72,768]{2,1,0:T(8,128)(2,1)}), bf16[16,72,768]{2,1,0:T(8,128)(2,1)S(1)}, u32[]{:S(2)}, u32[]{:S(2)}) %all-to-all-start.4) | async-done | bytes 1769504 | tf_op jit(solution)/shard_map/all_to_all | solution.py:187
  184.8 0.0 collective-permute-start.5
  184.8 3.7 %collective-permute-done.5.other_ref = bf16[2,576,768]{2,1,0:T(8,128)(2,1)S(1)} collective-permute-done((bf16[2,576,768]{2,1,0:T(8,128)(2,1)S(1)}, bf16[2,576,768]{2,1,0:T(8,128)(2,1)S(1)}, u32[]{:S(2)}, u32[]{:S(2)}) %collective-permute-start.5) | collective-permute-done | bytes 1769504 | tf_op jit(solution)/shard_map/ppermute | solution.py:184
  188.4 12.4 %branch.3 = (bf16[2,576,768]{2,1,0:T(8,128)(2,1)S(1)}, bf16[2,576,768]{2,1,0:T(8,128)(2,1)S(1)}) custom-call(s32[1]{0:T(128)} %bitcast.6.core_ref, bf16[2,576,768]{2,1,0:T(8,128)(2,1)S(1)} %bitcast.70, bf16[2,576,768]{2,1,0:T(8,128)(2,1)S(1)} %collective-permute-done.5.other_ref, bf16[1024,3072]{1,0:T(8,128)(2,1)} %bitcast.72, ...), custom_call_target="tpu_custom_call" | custom-call | flops 2359296 | bytes 2359296 | tf_op jit(solution)/shard_map/branch/pallas_call | solution.py:120
  200.8 0.2 collective-permute-start.6
  201.1 3.5 %collective-permute-done.6 = bf16[2,576,768]{2,1,0:T(8,128)(2,1)S(1)} collective-permute-done((bf16[2,576,768]{2,1,0:T(8,128)(2,1)S(1)}, bf16[2,576,768]{2,1,0:T(8,128)(2,1)S(1)}, u32[]{:S(2)}, u32[]{:S(2)}) %collective-permute-start.6) | collective-permute-done | bytes 1769504 | tf_op jit(solution)/shard_map/ppermute | solution.py:184
  204.6 1.7 add_convert_fusion
  206.3 6.5 %all-to-all-start.5 = ((bf16[16,72,768]{2,1,0:T(8,128)(2,1)}), bf16[16,72,768]{2,1,0:T(8,128)(2,1)S(1)}, u32[]{:S(2)}, u32[]{:S(2)}) async-start(bf16[16,72,768]{2,1,0:T(8,128)(2,1)} %bitcast.83), calls=%async_computation.5 | async-start | bytes 3538944 | tf_op jit(solution)/shard_map/all_to_all | solution.py:187
  212.9 25.4 %all-to-all-done.5 = bf16[16,72,768]{2,1,0:T(8,128)(2,1)S(1)} async-done(((bf16[16,72,768]{2,1,0:T(8,128)(2,1)}), bf16[16,72,768]{2,1,0:T(8,128)(2,1)S(1)}, u32[]{:S(2)}, u32[]{:S(2)}) %all-to-all-start.5) | async-done | bytes 1769504 | tf_op jit(solution)/shard_map/all_to_all | solution.py:187
  238.3 0.2 convert_reduce_fusion
  238.5 0.8 add_convert_fusion.2
  239.4 3.8 %collective-permute-start.7 = (bf16[128,768]{1,0:T(8,128)(2,1)S(1)}, bf16[128,768]{1,0:T(8,128)(2,1)S(1)}, u32[]{:S(2)}, u32[]{:S(2)}) collective-permute-start(bf16[128,768]{1,0:T(8,128)(2,1)S(1)} %add_convert_fusion.2), channel_id=1, source_target_pairs={{0,224},{32,0},{64,32},{96,64},{128,96},{160,128},{192,160},{224,1... | collective-permute-start | bytes 589832 | tf_op jit(solution)/shard_map/ppermute | solution.py:214
  243.2 3.2 %collective-permute-done.7 = bf16[128,768]{1,0:T(8,128)(2,1)S(1)} collective-permute-done((bf16[128,768]{1,0:T(8,128)(2,1)S(1)}, bf16[128,768]{1,0:T(8,128)(2,1)S(1)}, u32[]{:S(2)}, u32[]{:S(2)}) %collective-permute-start.7) | collective-permute-done | bytes 196640 | tf_op jit(solution)/shard_map/ppermute | solution.py:214
  246.4 0.7 copy.9
  (8 shorter events, 0.2 us)
Async XLA Ops:
  0.0 5.9 %copy-start = (bf16[1,2,128,768]{3,2,1,0:T(8,128)(2,1)S(1)}, bf16[1,2,128,768]{3,2,1,0:T(8,128)(2,1)}, u32[]{:S(2)}) copy-start(bf16[1,2,128,768]{3,2,1,0:T(8,128)(2,1)} %param.8) | copy-start | bytes 1179652
  7.8 7.5 %copy-start.3 = (bf16[1,128,768]{2,1,0:T(8,128)(2,1)S(1)}, bf16[1,128,768]{2,1,0:T(8,128)(2,1)}, u32[]{:S(2)}) copy-start(bf16[1,128,768]{2,1,0:T(8,128)(2,1)} %param.7) | copy-start | bytes 589828
  7.8 32.5 %all-to-all-start = ((bf16[16,72,768]{2,1,0:T(8,128)(2,1)}), bf16[16,72,768]{2,1,0:T(8,128)(2,1)}, u32[]{:S(2)}, u32[]{:S(2)}) async-start(bf16[16,72,768]{2,1,0:T(8,128)(2,1)} %bitcast.16), calls=%async_computation | async-start | bytes 3538944 | tf_op jit(solution)/shard_map/all_to_all | solution.py:187
  40.2 7.3 %collective-permute-start = (bf16[2,576,768]{2,1,0:T(8,128)(2,1)}, bf16[2,576,768]{2,1,0:T(8,128)(2,1)}, u32[]{:S(2)}, u32[]{:S(2)}) collective-permute-start(bf16[2,576,768]{2,1,0:T(8,128)(2,1)} %bitcast.17.mine_ref), channel_id=1, source_target_pairs={{0,1},{1,0},{2,3},{3,2},{4,5},{5,4},{6,7},{7,6},{8,9},{9,8},{10,11... | collective-permute-start | bytes 5308424 | tf_op jit(solution)/shard_map/ppermute | solution.py:184
  40.3 31.0 %all-to-all-start.1 = ((bf16[16,72,768]{2,1,0:T(8,128)(2,1)}), bf16[16,72,768]{2,1,0:T(8,128)(2,1)S(1)}, u32[]{:S(2)}, u32[]{:S(2)}) async-start(bf16[16,72,768]{2,1,0:T(8,128)(2,1)} %bitcast.78), calls=%async_computation.1 | async-start | bytes 3538944 | tf_op jit(solution)/shard_map/all_to_all | solution.py:187
  71.3 6.0 %collective-permute-start.1 = (bf16[2,576,768]{2,1,0:T(8,128)(2,1)S(1)}, bf16[2,576,768]{2,1,0:T(8,128)(2,1)}, u32[]{:S(2)}, u32[]{:S(2)}) collective-permute-start(bf16[2,576,768]{2,1,0:T(8,128)(2,1)S(1)} %bitcast.67), channel_id=1, source_target_pairs={{0,1},{1,0},{2,3},{3,2},{4,5},{5,4},{6,7},{7,6},{8,9},{9,8},{10,11... | collective-permute-start | bytes 5308424 | tf_op jit(solution)/shard_map/ppermute | solution.py:184
  71.3 32.1 %all-to-all-start.2 = ((bf16[16,72,768]{2,1,0:T(8,128)(2,1)}), bf16[16,72,768]{2,1,0:T(8,128)(2,1)}, u32[]{:S(2)}, u32[]{:S(2)}) async-start(bf16[16,72,768]{2,1,0:T(8,128)(2,1)} %bitcast.77), calls=%async_computation.2 | async-start | bytes 3538944 | tf_op jit(solution)/shard_map/all_to_all | solution.py:187
  90.5 1.2 copy-start.1
  91.8 1.2 copy-start.2
  103.4 3.9 %collective-permute-start.2 = (bf16[2,576,768]{2,1,0:T(8,128)(2,1)}, bf16[2,576,768]{2,1,0:T(8,128)(2,1)S(1)}, u32[]{:S(2)}, u32[]{:S(2)}) collective-permute-start(bf16[2,576,768]{2,1,0:T(8,128)(2,1)} %copy-done.2), channel_id=1, source_target_pairs={{0,1},{1,0},{2,3},{3,2},{4,5},{5,4},{6,7},{7,6},{8,9},{9,8},{10,11... | collective-permute-start | bytes 5308424 | tf_op jit(solution)/shard_map/ppermute | solution.py:184
  110.4 6.0 %copy-start.4 = (f32[1,2,128,2]{2,3,1,0:T(2,128)S(1)}, f32[1,2,128,2]{2,3,1,0:T(2,128)}, u32[]{:S(2)}) copy-start(f32[1,2,128,2]{2,3,1,0:T(2,128)} %param.10) | copy-start | bytes 6148
  110.4 31.4 %all-to-all-start.3 = ((bf16[16,72,768]{2,1,0:T(8,128)(2,1)}), bf16[16,72,768]{2,1,0:T(8,128)(2,1)S(1)}, u32[]{:S(2)}, u32[]{:S(2)}) async-start(bf16[16,72,768]{2,1,0:T(8,128)(2,1)} %bitcast.82), calls=%async_computation.3 | async-start | bytes 3538944 | tf_op jit(solution)/shard_map/all_to_all | solution.py:187
  143.0 9.1 %collective-permute-start.3 = (bf16[128,768]{1,0:T(8,128)(2,1)S(1)}, bf16[128,768]{1,0:T(8,128)(2,1)S(1)}, u32[]{:S(2)}, u32[]{:S(2)}) collective-permute-start(bf16[128,768]{1,0:T(8,128)(2,1)S(1)} %fusion.1), channel_id=1, source_target_pairs={{0,224},{32,0},{64,32},{96,64},{128,96},{160,128},{192,160},{224,1... | collective-permute-start | bytes 589832 | tf_op jit(solution)/shard_map/ppermute | solution.py:214
  153.9 5.0 %collective-permute-start.4 = (bf16[2,576,768]{2,1,0:T(8,128)(2,1)}, bf16[2,576,768]{2,1,0:T(8,128)(2,1)}, u32[]{:S(2)}, u32[]{:S(2)}) collective-permute-start(bf16[2,576,768]{2,1,0:T(8,128)(2,1)} %bitcast.21.mine_ref), channel_id=1, source_target_pairs={{0,1},{1,0},{2,3},{3,2},{4,5},{5,4},{6,7},{7,6},{8,9},{9,8},{10,11... | collective-permute-start | bytes 5308424 | tf_op jit(solution)/shard_map/ppermute | solution.py:184
  153.9 30.8 %all-to-all-start.4 = ((bf16[16,72,768]{2,1,0:T(8,128)(2,1)}), bf16[16,72,768]{2,1,0:T(8,128)(2,1)S(1)}, u32[]{:S(2)}, u32[]{:S(2)}) async-start(bf16[16,72,768]{2,1,0:T(8,128)(2,1)} %bitcast.80), calls=%async_computation.4 | async-start | bytes 3538944 | tf_op jit(solution)/shard_map/all_to_all | solution.py:187
  184.8 3.7 %collective-permute-start.5 = (bf16[2,576,768]{2,1,0:T(8,128)(2,1)S(1)}, bf16[2,576,768]{2,1,0:T(8,128)(2,1)S(1)}, u32[]{:S(2)}, u32[]{:S(2)}) collective-permute-start(bf16[2,576,768]{2,1,0:T(8,128)(2,1)S(1)} %bitcast.69), channel_id=1, source_target_pairs={{0,1},{1,0},{2,3},{3,2},{4,5},{5,4},{6,7},{7,6},{8,9},{9,8},{10,11... | collective-permute-start | bytes 5308424 | tf_op jit(solution)/shard_map/ppermute | solution.py:184
  200.8 3.8 %collective-permute-start.6 = (bf16[2,576,768]{2,1,0:T(8,128)(2,1)S(1)}, bf16[2,576,768]{2,1,0:T(8,128)(2,1)S(1)}, u32[]{:S(2)}, u32[]{:S(2)}) collective-permute-start(bf16[2,576,768]{2,1,0:T(8,128)(2,1)S(1)} %get-tuple-element.36), channel_id=1, source_target_pairs={{0,1},{1,0},{2,3},{3,2},{4,5},{5,4},{6,7},{7,6},{8,9},{9,8},{10,11... | collective-permute-start | bytes 5308424 | tf_op jit(solution)/shard_map/ppermute | solution.py:184
  206.3 32.0 %all-to-all-start.5 = ((bf16[16,72,768]{2,1,0:T(8,128)(2,1)}), bf16[16,72,768]{2,1,0:T(8,128)(2,1)S(1)}, u32[]{:S(2)}, u32[]{:S(2)}) async-start(bf16[16,72,768]{2,1,0:T(8,128)(2,1)} %bitcast.83), calls=%async_computation.5 | async-start | bytes 3538944 | tf_op jit(solution)/shard_map/all_to_all | solution.py:187
  239.4 7.0 %collective-permute-start.7 = (bf16[128,768]{1,0:T(8,128)(2,1)S(1)}, bf16[128,768]{1,0:T(8,128)(2,1)S(1)}, u32[]{:S(2)}, u32[]{:S(2)}) collective-permute-start(bf16[128,768]{1,0:T(8,128)(2,1)S(1)} %add_convert_fusion.2), channel_id=1, source_target_pairs={{0,224},{32,0},{64,32},{96,64},{128,96},{160,128},{192,160},{224,1... | collective-permute-start | bytes 589832 | tf_op jit(solution)/shard_map/ppermute | solution.py:214

commit v3 on v2

v3 whole, which is shorter than its diff:
```python
import jax
import jax.numpy as jnp
from jax import lax
from jax.experimental import pallas as pl
from jax.experimental.pallas import tpu as pltpu
from jax.sharding import Mesh, PartitionSpec as P

EXPERTS = 4
CAPACITY = 72
HIDDEN_BLOCK = 256
VMEM_LIMIT = 32 * 1024 * 1024


def together(*values):
    return lax.optimization_barrier(values)


def contract_last(left, right):
    return lax.dot_general(
        left, right, (((1,), (1,)), ((), ())), preferred_element_type=jnp.float32
    )


def factor_kernel(core_ref, mine_ref, other_ref, up_ref, factor_ref):
    core = core_ref[0]
    quarter = mine_ref.shape[2]
    pre = None
    for xhi in range(mine_ref.shape[0]):
        own = pl.multiple_of((2 * xhi + core) * quarter, quarter)
        theirs = pl.multiple_of((2 * xhi + 1 - core) * quarter, quarter)
        part = jnp.dot(
            mine_ref[xhi], up_ref[pl.ds(own, quarter), :], preferred_element_type=jnp.float32
        ) + jnp.dot(
            other_ref[xhi], up_ref[pl.ds(theirs, quarter), :], preferred_element_type=jnp.float32
        )
        pre = part if pre is None else pre + part
    sigma = jax.nn.sigmoid(pre)
    factor_ref[...] = sigma * (1.0 + pre * (1.0 - sigma))


def factor(core, saved, up):
    mine, other, column = saved
    halves, rows = mine.shape[:2]
    width, hidden = up.shape
    quarter = width // (2 * halves)
    whole = pl.BlockSpec((halves, rows, quarter), lambda i, c: (0, 0, column))
    return pl.pallas_call(
        factor_kernel,
        out_shape=pltpu.HBM((rows, hidden), jnp.float32),
        grid_spec=pltpu.PrefetchScalarGridSpec(
            num_scalar_prefetch=1,
            grid=(hidden // HIDDEN_BLOCK,),
            in_specs=[whole, whole, pl.BlockSpec((width, HIDDEN_BLOCK), lambda i, c: (0, i))],
            out_specs=pl.BlockSpec((rows, HIDDEN_BLOCK), lambda i, c: (0, i)),
        ),
        compiler_params=pltpu.CompilerParams(
            dimension_semantics=("arbitrary",), vmem_limit_bytes=VMEM_LIMIT
        ),
        cost_estimate=pl.CostEstimate(
            flops=2 * rows * width * hidden,
            transcendentals=2 * rows * hidden,
            bytes_accessed=2 * width * (rows + hidden) + 4 * rows * hidden,
        ),
        name="factor",
    )(core, mine, other, up)


def sent_kernel(
    core_ref, mine_ref, other_ref, down_ref, factor_ref, up_ref, grad_pre_ref, send_ref
):
    core = core_ref[0]
    step = pl.program_id(0)
    halves, _, quarter = mine_ref.shape
    blocks = grad_pre_ref.shape[1] // HIDDEN_BLOCK

    for block in range(blocks):

        @pl.when(step == block)
        def _(block=block):
            act = None
            for xhi in range(halves):
                own = pl.multiple_of((2 * xhi + core) * quarter, quarter)
                theirs = pl.multiple_of((2 * xhi + 1 - core) * quarter, quarter)
                part = contract_last(
                    mine_ref[xhi], down_ref[:, pl.ds(own, quarter)]
                ) + contract_last(other_ref[xhi], down_ref[:, pl.ds(theirs, quarter)])
                act = part if act is None else act + part
            grad_pre_ref[:, block * HIDDEN_BLOCK : (block + 1) * HIDDEN_BLOCK] = (
                act * factor_ref[...]
            ).astype(jnp.bfloat16)

    @pl.when(step >= blocks)
    def _():
        send_ref[0] = contract_last(grad_pre_ref[...], up_ref[...]).astype(jnp.bfloat16)


def sent_part(core, grads, down, factors, up):
    mine, other, column = grads
    halves, rows = mine.shape[:2]
    hidden, width = down.shape
    quarter = width // (2 * halves)
    blocks = hidden // HIDDEN_BLOCK
    whole = pl.BlockSpec((halves, rows, quarter), lambda i, c: (0, 0, column))

    def hidden_block(i):
        return jnp.minimum(i, blocks - 1)

    def late(i):
        return jnp.maximum(i - blocks, 0)

    return pl.pallas_call(
        sent_kernel,
        out_shape=(
            jax.ShapeDtypeStruct((rows, hidden), jnp.bfloat16),
            jax.ShapeDtypeStruct((halves, rows, quarter), jnp.bfloat16),
        ),
        grid_spec=pltpu.PrefetchScalarGridSpec(
            num_scalar_prefetch=1,
            grid=(blocks + halves,),
            in_specs=[
                whole,
                whole,
                pl.BlockSpec((HIDDEN_BLOCK, width), lambda i, c: (hidden_block(i), 0)),
                pl.BlockSpec((rows, HIDDEN_BLOCK), lambda i, c: (0, hidden_block(i))),
                pl.BlockSpec((quarter, hidden), lambda i, c: (2 * late(i) + 1 - c[0], 0)),
            ],
            out_specs=(
                pl.BlockSpec((rows, hidden), lambda i, c: (0, 0)),
                pl.BlockSpec((1, rows, quarter), lambda i, c: (late(i), 0, 0)),
            ),
        ),
        compiler_params=pltpu.CompilerParams(
            dimension_semantics=("arbitrary",), vmem_limit_bytes=VMEM_LIMIT
        ),
        cost_estimate=pl.CostEstimate(
            flops=4 * rows * hidden, transcendentals=0, bytes_accessed=4 * rows * hidden
        ),
        name="sent_part",
    )(core, mine, other, down, factors, up)


def kept_kernel(core_ref, grad_pre_ref, up_ref, keep_ref):
    keep_ref[0] = contract_last(grad_pre_ref[...], up_ref[...]).astype(jnp.bfloat16)


def kept_part(core, grad_pre, up):
    rows, hidden = grad_pre.shape
    quarter = up.shape[0] // 4
    halves = 2
    return pl.pallas_call(
        kept_kernel,
        out_shape=jax.ShapeDtypeStruct((halves, rows, quarter), jnp.bfloat16),
        grid_spec=pltpu.PrefetchScalarGridSpec(
            num_scalar_prefetch=1,
            grid=(halves,),
            in_specs=[
                pl.BlockSpec((rows, hidden), lambda i, c: (0, 0)),
                pl.BlockSpec((quarter, hidden), lambda i, c: (2 * i + c[0], 0)),
            ],
            out_specs=pl.BlockSpec((1, rows, quarter), lambda i, c: (i, 0, 0)),
        ),
        compiler_params=pltpu.CompilerParams(
            dimension_semantics=("arbitrary",), vmem_limit_bytes=VMEM_LIMIT
        ),
        cost_estimate=pl.CostEstimate(
            flops=2 * rows * hidden * halves * quarter,
            transcendentals=0,
            bytes_accessed=2 * hidden * (rows + halves * quarter),
        ),
        name="kept_part",
    )(core, grad_pre, up)


def pick_kernel(step, plan_ref, routes_ref, *refs):
    del plan_ref
    values, out_ref = refs[:-1], refs[-1]
    expert = pl.program_id(0)
    rows = routes_ref.shape[2]
    named = (routes_ref[0] == expert).astype(jnp.float32)
    chosen = jnp.max(named, axis=0, keepdims=True)
    earlier = (
        lax.broadcasted_iota(jnp.int32, (rows, rows), 0)
        < lax.broadcasted_iota(jnp.int32, (rows, rows), 1)
    ).astype(jnp.bfloat16)
    before = jnp.dot(
        jnp.broadcast_to(chosen, (16, rows)).astype(jnp.bfloat16),
        earlier,
        preferred_element_type=jnp.float32,
    )[0:1]
    place = jnp.where(chosen > 0.0, before, -1.0).astype(jnp.int32)
    hit = place == lax.broadcasted_iota(jnp.int32, (CAPACITY, rows), 0)
    select = hit.astype(jnp.float32).astype(jnp.bfloat16)
    copies = [(i, k) for i in range(out_ref.shape[0]) for k in range(out_ref.shape[2])]
    start = 0
    for value_ref in values:
        value = value_ref[0]
        width = value.shape[1]
        rows_sent = jnp.dot(select, value, preferred_element_type=jnp.float32).astype(jnp.bfloat16)
        for i, k in copies:
            out_ref[i, 0, k, :, start : start + width] = rows_sent
        start += width


def pick(step, plan, routes, values, n_xhi, per_expert):
    rows = routes.shape[2]
    width = sum(value.shape[2] for value, _ in values)
    specs = [pl.BlockSpec((1,) + routes.shape[1:], lambda j, p: (p[step], 0, 0))]
    for value, planned in values:
        if planned:
            specs.append(pl.BlockSpec((1,) + value.shape[1:], lambda j, p: (p[step], 0, 0)))
        else:
            specs.append(pl.BlockSpec((1,) + value.shape[1:], lambda j, p: (0, 0, 0)))
    out = pl.pallas_call(
        lambda *refs: pick_kernel(step, *refs),
        out_shape=jax.ShapeDtypeStruct(
            (n_xhi, EXPERTS, per_expert, CAPACITY, width), jnp.bfloat16
        ),
        grid_spec=pltpu.PrefetchScalarGridSpec(
            num_scalar_prefetch=1,
            grid=(EXPERTS,),
            in_specs=specs,
            out_specs=pl.BlockSpec(
                (n_xhi, 1, per_expert, CAPACITY, width), lambda j, p: (0, j, 0, 0, 0)
            ),
        ),
        compiler_params=pltpu.CompilerParams(dimension_semantics=("arbitrary",)),
        name="pick",
    )(plan, routes, *[value for value, _ in values])
    return out.reshape(n_xhi * EXPERTS * per_expert, CAPACITY, width)


def slots(route_now, share_now):
    rows = route_now.shape[0]
    named = route_now.T[None] == jnp.arange(EXPERTS, dtype=jnp.int32)[:, None, None]
    chosen = jnp.any(named, axis=1)
    mix = jnp.sum(jnp.where(named, share_now.T[None], 0.0), axis=1)
    token = jnp.arange(rows, dtype=jnp.int32)
    earlier = (token[:, None] < token[None, :]).astype(jnp.bfloat16)
    before = jnp.dot(
        chosen.astype(jnp.bfloat16), earlier, preferred_element_type=jnp.float32
    ).astype(jnp.int32)
    place = jnp.where(chosen, before, -1)
    hit = place[:, None, :] == jnp.arange(CAPACITY, dtype=jnp.int32)[None, :, None]
    mixing = jnp.where(hit, mix[:, None, :], 0.0).reshape(EXPERTS * CAPACITY, rows)
    return mixing


def per_device(grad_in, saved_input, routes, route_weights, plan, up_weight, down_weight):
    n_expert = lax.axis_size("expert")
    n_xhi = lax.axis_size("xhi")
    n_section = lax.axis_size("section")
    per_expert = n_expert // EXPERTS
    peers = n_xhi * n_expert
    rows, quarter = grad_in.shape[1:]
    up_local = pltpu.with_memory_space_constraint(up_weight[0], pltpu.HBM)
    down_local = pltpu.with_memory_space_constraint(down_weight[0], pltpu.HBM)
    core = lax.axis_index("core").astype(jnp.int32).reshape(1)

    def swap_cores(value):
        return lax.ppermute(value, "core", [(0, 1), (1, 0)])

    def exchange(value):
        return lax.all_to_all(value, ("xhi", "expert"), split_axis=0, concat_axis=0, tiled=True)

    def deliver(sent):
        return exchange(sent).reshape(n_xhi, n_expert * CAPACITY, sent.shape[2])

    def combine(current, mixing, arrived):
        summed = jnp.sum(
            arrived.reshape(n_xhi, EXPERTS, per_expert, CAPACITY, quarter).astype(jnp.float32),
            axis=(0, 2),
        )
        moe_term = lax.dot_general(
            mixing,
            summed.reshape(EXPERTS * CAPACITY, quarter),
            (((0,), (0,)), ((), ())),
            precision=lax.Precision.HIGHEST,
            preferred_element_type=jnp.float32,
        )
        result = (current.astype(jnp.float32) + moe_term).astype(jnp.bfloat16)
        return lax.ppermute(
            result, "section", [(i, (i - 1) % n_section) for i in range(n_section)]
        )

    def outgoing(send, keep):
        return (
            keep.astype(jnp.float32) + swap_cores(send).astype(jnp.float32)
        ).astype(jnp.bfloat16).reshape(peers, CAPACITY, quarter)

    micros = plan[0]
    routes_by_choice = routes[0].transpose(0, 2, 1)
    saved_all = saved_input[0]
    current = grad_in[0]
    ticks = micros.shape[0]

    def mixing_of(tick):
        route_now = lax.dynamic_index_in_dim(routes[0], micros[tick], 0, keepdims=False)
        share_now = lax.dynamic_index_in_dim(route_weights[0], micros[tick], 0, keepdims=False)
        return slots(route_now, share_now)

    def pick_rows(tick, *values):
        return pick(tick, micros, routes_by_choice, values, n_xhi, per_expert)

    def in_hbm(value):
        return pltpu.with_memory_space_constraint(value, pltpu.HBM)

    rows_in = deliver(pick_rows(0, (saved_all, True), (current[None], False)))
    later = None
    for tick in range(ticks):
        if tick == 0:
            both, swapped = rows_in, None
            if ticks > 1:
                saved_sent, both = together(pick_rows(1, (saved_all, True)), both)
                later = deliver(saved_sent)
            swapped = swap_cores(both)
            saved, grads = (both, swapped, 0), (both, swapped, 1)
            factors = in_hbm(factor(core, saved, up_local))
        else:
            grad_sent, later = together(pick_rows(tick, (current[None], False)), later)
            grad_rows = deliver(grad_sent)
            factors = in_hbm(factor(core, (later, swap_cores(later), 0), up_local))
            grad_rows, factors = together(grad_rows, factors)
            grads = (grad_rows, swap_cores(grad_rows), 0)
        grad_pre, send = sent_part(core, grads, down_local, factors, up_local)
        keep = kept_part(core, grad_pre, up_local)
        if tick + 1 < ticks:
            send, later, keep = together(send, later, keep)
        partial_rows = (
            keep.astype(jnp.float32) + swap_cores(send).astype(jnp.float32)
        ).astype(jnp.bfloat16)
        arrived = exchange(partial_rows.reshape(peers, CAPACITY, quarter))
        current = combine(current, mixing_of(tick), arrived)
    return current[None]


def solution(mesh):
    sections, experts, parts = (mesh.shape[name] for name in ("section", "expert", "mp"))
    refined = Mesh(
        mesh.devices.reshape(sections, experts, parts // 2, 2),
        ("section", "expert", "xhi", "core"),
    )
    mp = ("xhi", "core")
    placed = (
        P("section", "expert", mp),
        P("section", None, "expert", mp),
        P("section", None, "expert", None),
        P("section", None, "expert", None),
        P("section", None),
        P("section", None, ("expert", "xhi", "core")),
        P("section", ("expert", "xhi", "core"), None),
    )
    return jax.shard_map(
        per_device,
        mesh=refined,
        in_specs=placed,
        out_specs=P("section", "expert", mp),
        check_vma=False,
    )
```

time: 248 us -> 240 us (0.968)
  Pallas kernels: 42.5 us -> 56.6 us
  waiting for transfers between devices: 134 us -> 122 us
  matrix products: 9.39 us -> 1.97 us
    pallas_call x2 -> x7, Pallas kernels: 25.6 us -> 40.7 us  [the longest x2 20.3 us: sent_part(): pl.pallas_call(sent_kernel, out_shape=(jax.ShapeDtypeStruct((rows, hidden...]
    all_to_all x6 -> x5, waiting for transfers between devices: 117 us -> 109 us  [exchange(): lax.all_to_all(value, ('xhi', 'expert'), split_axis=0, concat_axis=0, til...]
    dot_general x4 -> x0, matrix products: 7.42 us -> none  [select(): jnp.dot(picks.astype(jnp.bfloat16), value, preferred_element_type=jnp.flo...]
    ppermute x6 -> x5, waiting for transfers between devices: 11.1 us -> 7.39 us  [swap_cores(): return lax.ppermute(value, 'core', [(0, 1), (1, 0)])]
    all_to_all x6 -> x5, starting transfers between devices: 36.3 us -> 36.8 us  [exchange(): lax.all_to_all(value, ('xhi', 'expert'), split_axis=0, concat_axis=0, til...]
  transfers between devices with their start and end apart: 14 -> 12, of which waited for: 11 -> 9; matrix products, arithmetic and copies ran while one was open for 2% -> 0% of each run, Pallas kernels for 12% -> 16%
where the time goes in v3:
time: 240 us; the launch traced here: 239 us
  waiting for transfers between devices  122 us (51%)
  Pallas kernels  56.6 us (24%)
  starting transfers between devices  46.7 us (19%)
  between operations  4.02 us (2%)
  other arithmetic  3.89 us (2%)
  local copies, waits for them, and re-layouts  3.19 us (1%)
    all_to_all x5, waiting for transfers between devices, exchange(): lax.all_to_all(value, ('xhi', 'expert'), split_axis=0, concat_axis=0, til...  109 us
    all_to_all x5, starting transfers between devices, exchange(): lax.all_to_all(value, ('xhi', 'expert'), split_axis=0, concat_axis=0, til...  36.8 us
    pallas_call x2, Pallas kernels, sent_part(): pl.pallas_call(sent_kernel, out_shape=(jax.ShapeDtypeStruct((rows, hidden...  20.3 us
    pallas_call x2, Pallas kernels, factor(): pl.pallas_call(factor_kernel, out_shape=pltpu.HBM((rows, hidden), jnp.flo...  15.9 us
    pallas_call x3, Pallas kernels, pick(): pl.pallas_call(lambda *refs: pick_kernel(step, *refs), out_shape=jax.Shap...  12.9 us
    ppermute x2, starting transfers between devices, combine(): lax.ppermute(result, 'section', [(i, (i - 1) % n_section) for i in range(...  9.7 us
    pallas_call x2, Pallas kernels, kept_part(): pl.pallas_call(kept_kernel, out_shape=jax.ShapeDtypeStruct((halves, rows,...  7.48 us
    ppermute x5, waiting for transfers between devices, swap_cores(): return lax.ppermute(value, 'core', [(0, 1), (1, 0)])  7.39 us
  transfers between devices with their start and end apart: 12, of which 9 were waited for; matrix products, arithmetic and copies ran while one was open for 0% of the time, Pallas kernels for 16%

profile of v3, /device:TPU:8, one launch (start us, length us, event | category | flops | bytes accessed | tf_op | source)
XLA Modules:
  0.0 238.7 jit_solution(3819869839841164431)
XLA Ops:
  0.0 4.6 %pick.4 = bf16[2,4,2,72,1536]{4,3,2,1,0:T(8,128)(2,1)} custom-call(s32[2]{0:T(128)} %bitcast.82, s32[2,2,128]{2,1,0:T(2,128)} %bitcast.79, bf16[2,128,768]{2,1,0:T(8,128)(2,1)} %bitcast.75, bf16[1,128,768]{2,1,0:T(8,128)(2,1)} %refs_3_.1), custom_call_target="tpu_custom_call" | custom-call | tf_op jit(solution)/shard_map/pick/pallas_call | solution.py:213
  4.6 7.4 %all-to-all-start = ((bf16[16,72,1536]{2,1,0:T(8,128)(2,1)}), bf16[16,72,1536]{2,1,0:T(8,128)(2,1)S(1)}, u32[]{:S(2)}, u32[]{:S(2)}) async-start(bf16[16,72,1536]{2,1,0:T(8,128)(2,1)} %bitcast.70), calls=%async_computation | async-start | bytes 7077888 | tf_op jit(solution)/shard_map/all_to_all | solution.py:263
  12.0 4.2 %pick.3 = bf16[2,4,2,72,768]{4,3,2,1,0:T(8,128)(2,1)} custom-call(s32[2]{0:T(128)} %bitcast.83, s32[2,2,128]{2,1,0:T(2,128)} %bitcast.80, bf16[2,128,768]{2,1,0:T(8,128)(2,1)} %bitcast.76), custom_call_target="tpu_custom_call" | custom-call | tf_op jit(solution)/shard_map/pick/pallas_call | solution.py:213
  16.2 41.6 %all-to-all-done = bf16[16,72,1536]{2,1,0:T(8,128)(2,1)S(1)} async-done(((bf16[16,72,1536]{2,1,0:T(8,128)(2,1)}), bf16[16,72,1536]{2,1,0:T(8,128)(2,1)S(1)}, u32[]{:S(2)}, u32[]{:S(2)}) %all-to-all-start) | async-done | bytes 3538976 | tf_op jit(solution)/shard_map/all_to_all | solution.py:263
  57.8 0.0 collective-permute-start
  57.8 11.9 %all-to-all-start.1 = ((bf16[16,72,768]{2,1,0:T(8,128)(2,1)}), bf16[16,72,768]{2,1,0:T(8,128)(2,1)}, u32[]{:S(2)}, u32[]{:S(2)}) async-start(bf16[16,72,768]{2,1,0:T(8,128)(2,1)} %bitcast.73), calls=%async_computation.1 | async-start | bytes 3538944 | tf_op jit(solution)/shard_map/all_to_all | solution.py:263
  69.7 0.0 collective-permute-done.other_ref
  69.7 8.0 %factor.2.factor_ref = f32[576,1024]{1,0:T(8,128)} custom-call(s32[1]{0:T(128)} %bitcast.6.core_ref, bf16[2,576,1536]{2,1,0:T(8,128)(2,1)S(1)} %bitcast.58, bf16[2,576,1536]{2,1,0:T(8,128)(2,1)} %collective-permute-done.other_ref, bf16[3072,1024]{1,0:T(8,128)(2,1)} %bitcast.62), custom_call_target="tpu_custom_call" | custom-call | flops 3623878656 | bytes 12189696 | tf_op jit(solution)/shard_map/factor/pallas_call | solution.py:47
  77.7 10.5 %sent_part.2 = (bf16[576,1024]{1,0:T(8,128)(2,1)S(1)}, bf16[2,576,768]{2,1,0:T(8,128)(2,1)S(1)}) custom-call(s32[1]{0:T(128)} %bitcast.6.core_ref, bf16[2,576,1536]{2,1,0:T(8,128)(2,1)S(1)} %bitcast.59, bf16[2,576,1536]{2,1,0:T(8,128)(2,1)} %collective-permute-done.other_ref, bf16[1024,3072]{1,0:T(8,128)(2,1)} %bitcast.68, f32[576,1024]{1,0:T(8,128)} %factor.2.factor_ref, ...), custom_call_target="tpu_custom_call" | custom-call | flops 2359296 | bytes 2359296 | tf_op jit(solution)/shard_map/sent_part/pallas_call | solution.py:111
  88.2 0.0 copy-start
  88.2 1.2 copy-done
  89.4 0.0 copy-start.1
  89.4 3.8 %kept_part.2 = bf16[2,576,768]{2,1,0:T(8,128)(2,1)S(1)} custom-call(s32[1]{0:T(128)} %bitcast.6.core_ref, bf16[576,1024]{1,0:T(8,128)(2,1)S(1)} %get-tuple-element.21.grad_pre_ref, bf16[3072,1024]{1,0:T(8,128)(2,1)} %bitcast.64), custom_call_target="tpu_custom_call" | custom-call | flops 1811939328 | bytes 4325376 | tf_op jit(solution)/shard_map/kept_part/pallas_call | solution.py:150
  93.2 2.5 %all-to-all-done.1 = bf16[16,72,768]{2,1,0:T(8,128)(2,1)} async-done(((bf16[16,72,768]{2,1,0:T(8,128)(2,1)}), bf16[16,72,768]{2,1,0:T(8,128)(2,1)}, u32[]{:S(2)}, u32[]{:S(2)}) %all-to-all-start.1) | async-done | bytes 1769504 | tf_op jit(solution)/shard_map/all_to_all | solution.py:263
  95.7 0.0 copy-done.1
  95.7 0.0 collective-permute-start.1
  95.7 3.7 %collective-permute-done.1 = bf16[2,576,768]{2,1,0:T(8,128)(2,1)S(1)} collective-permute-done((bf16[2,576,768]{2,1,0:T(8,128)(2,1)S(1)}, bf16[2,576,768]{2,1,0:T(8,128)(2,1)S(1)}, u32[]{:S(2)}, u32[]{:S(2)}) %collective-permute-start.1) | collective-permute-done | bytes 1769504 | tf_op jit(solution)/shard_map/ppermute | solution.py:260
  99.4 1.7 add_convert_fusion.1
  101.1 0.0 copy-start.6
  101.1 0.0 copy-start.5
  101.1 0.0 copy-start.7
  101.1 6.0 %all-to-all-start.2 = ((bf16[16,72,768]{2,1,0:T(8,128)(2,1)}), bf16[16,72,768]{2,1,0:T(8,128)(2,1)S(1)}, u32[]{:S(2)}, u32[]{:S(2)}) async-start(bf16[16,72,768]{2,1,0:T(8,128)(2,1)} %bitcast.18), calls=%async_computation.2 | async-start | bytes 3538944 | tf_op jit(solution)/shard_map/all_to_all | solution.py:263
  107.1 0.0 copy-done.6
  107.1 0.0 copy-start.2
  107.1 0.6 fusion.18
  111.5 0.0 copy-done.5
  111.6 0.0 copy-done.7
  111.6 0.1 fusion.3
  111.7 20.8 %all-to-all-done.2 = bf16[16,72,768]{2,1,0:T(8,128)(2,1)S(1)} async-done(((bf16[16,72,768]{2,1,0:T(8,128)(2,1)}), bf16[16,72,768]{2,1,0:T(8,128)(2,1)S(1)}, u32[]{:S(2)}, u32[]{:S(2)}) %all-to-all-start.2) | async-done | bytes 1769504 | tf_op jit(solution)/shard_map/all_to_all | solution.py:263
  132.5 0.2 convert_reduce_fusion.1
  132.8 0.0 copy-done.2
  132.8 0.8 fusion.1
  133.6 5.9 %collective-permute-start.2 = (bf16[128,768]{1,0:T(8,128)(2,1)S(1)}, bf16[128,768]{1,0:T(8,128)(2,1)S(1)}, u32[]{:S(2)}, u32[]{:S(2)}) collective-permute-start(bf16[128,768]{1,0:T(8,128)(2,1)S(1)} %fusion.1), channel_id=1, source_target_pairs={{0,224},{32,0},{64,32},{96,64},{128,96},{160,128},{192,160},{224,1... | collective-permute-start | bytes 589832 | tf_op jit(solution)/shard_map/ppermute | solution.py:281
  139.6 3.2 %collective-permute-done.2 = bf16[128,768]{1,0:T(8,128)(2,1)S(1)} collective-permute-done((bf16[128,768]{1,0:T(8,128)(2,1)S(1)}, bf16[128,768]{1,0:T(8,128)(2,1)S(1)}, u32[]{:S(2)}, u32[]{:S(2)}) %collective-permute-start.2) | collective-permute-done | bytes 196640 | tf_op jit(solution)/shard_map/ppermute | solution.py:281
  142.8 0.0 copy-start.3
  142.8 0.7 copy-done.3
  143.4 4.1 %pick.5 = bf16[2,4,2,72,768]{4,3,2,1,0:T(8,128)(2,1)} custom-call(s32[2]{0:T(128)} %bitcast.84, s32[2,2,128]{2,1,0:T(2,128)} %bitcast.81, bf16[1,128,768]{2,1,0:T(8,128)(2,1)} %bitcast.77), custom_call_target="tpu_custom_call" | custom-call | tf_op jit(solution)/shard_map/pick/pallas_call | solution.py:213
  147.5 0.0 collective-permute-start.3
  147.5 5.0 %all-to-all-start.3 = ((bf16[16,72,768]{2,1,0:T(8,128)(2,1)}), bf16[16,72,768]{2,1,0:T(8,128)(2,1)S(1)}, u32[]{:S(2)}, u32[]{:S(2)}) async-start(bf16[16,72,768]{2,1,0:T(8,128)(2,1)} %bitcast.71), calls=%async_computation.3 | async-start | bytes 3538944 | tf_op jit(solution)/shard_map/all_to_all | solution.py:263
  152.5 0.0 collective-permute-done.3.other_ref
  152.5 7.9 %factor.3.factor_ref = f32[576,1024]{1,0:T(8,128)} custom-call(s32[1]{0:T(128)} %bitcast.6.core_ref, bf16[2,576,768]{2,1,0:T(8,128)(2,1)} %bitcast.17.mine_ref, bf16[2,576,768]{2,1,0:T(8,128)(2,1)S(1)} %collective-permute-done.3.other_ref, bf16[3072,1024]{1,0:T(8,128)(2,1)} %bitcast.65), custom_call_target="tpu_custom_call" | custom-call | flops 3623878656 | bytes 12189696 | tf_op jit(solution)/shard_map/factor/pallas_call | solution.py:47
  160.4 17.9 %all-to-all-done.3 = bf16[16,72,768]{2,1,0:T(8,128)(2,1)S(1)} async-done(((bf16[16,72,768]{2,1,0:T(8,128)(2,1)}), bf16[16,72,768]{2,1,0:T(8,128)(2,1)S(1)}, u32[]{:S(2)}, u32[]{:S(2)}) %all-to-all-start.3) | async-done | bytes 1769504 | tf_op jit(solution)/shard_map/all_to_all | solution.py:263
  178.3 0.0 collective-permute-start.4
  178.3 3.7 %collective-permute-done.4.other_ref = bf16[2,576,768]{2,1,0:T(8,128)(2,1)S(1)} collective-permute-done((bf16[2,576,768]{2,1,0:T(8,128)(2,1)S(1)}, bf16[2,576,768]{2,1,0:T(8,128)(2,1)S(1)}, u32[]{:S(2)}, u32[]{:S(2)}) %collective-permute-start.4) | collective-permute-done | bytes 1769504 | tf_op jit(solution)/shard_map/ppermute | solution.py:260
  182.0 9.8 %sent_part.3 = (bf16[576,1024]{1,0:T(8,128)(2,1)S(1)}, bf16[2,576,768]{2,1,0:T(8,128)(2,1)S(1)}) custom-call(s32[1]{0:T(128)} %bitcast.6.core_ref, bf16[2,576,768]{2,1,0:T(8,128)(2,1)S(1)} %bitcast.61, bf16[2,576,768]{2,1,0:T(8,128)(2,1)S(1)} %collective-permute-done.4.other_ref, bf16[1024,3072]{1,0:T(8,128)(2,1)} %bitcast.69, ...), custom_call_target="tpu_custom_call" | custom-call | flops 2359296 | bytes 2359296 | tf_op jit(solution)/shard_map/sent_part/pallas_call | solution.py:111
  191.9 0.2 collective-permute-start.5
  192.1 3.7 %kept_part.3 = bf16[2,576,768]{2,1,0:T(8,128)(2,1)S(1)} custom-call(s32[1]{0:T(128)} %bitcast.6.core_ref, bf16[576,1024]{1,0:T(8,128)(2,1)S(1)} %get-tuple-element.29.grad_pre_ref, bf16[3072,1024]{1,0:T(8,128)(2,1)} %bitcast.67), custom_call_target="tpu_custom_call" | custom-call | flops 1811939328 | bytes 4325376 | tf_op jit(solution)/shard_map/kept_part/pallas_call | solution.py:150
  195.8 0.0 collective-permute-done.5
  195.8 1.7 add_convert_fusion
  197.5 6.5 %all-to-all-start.4 = ((bf16[16,72,768]{2,1,0:T(8,128)(2,1)}), bf16[16,72,768]{2,1,0:T(8,128)(2,1)S(1)}, u32[]{:S(2)}, u32[]{:S(2)}) async-start(bf16[16,72,768]{2,1,0:T(8,128)(2,1)} %bitcast.29), calls=%async_computation.4 | async-start | bytes 3538944 | tf_op jit(solution)/shard_map/all_to_all | solution.py:263
  204.0 0.0 copy-start.4
  204.1 0.1 fusion.2
  204.2 25.8 %all-to-all-done.4 = bf16[16,72,768]{2,1,0:T(8,128)(2,1)S(1)} async-done(((bf16[16,72,768]{2,1,0:T(8,128)(2,1)}), bf16[16,72,768]{2,1,0:T(8,128)(2,1)S(1)}, u32[]{:S(2)}, u32[]{:S(2)}) %all-to-all-start.4) | async-done | bytes 1769504 | tf_op jit(solution)/shard_map/all_to_all | solution.py:263
  230.0 0.2 convert_reduce_fusion
  230.2 0.0 copy-done.4
  230.3 0.8 add_convert_fusion.2
  231.1 3.8 %collective-permute-start.6 = (bf16[128,768]{1,0:T(8,128)(2,1)S(1)}, bf16[128,768]{1,0:T(8,128)(2,1)S(1)}, u32[]{:S(2)}, u32[]{:S(2)}) collective-permute-start(bf16[128,768]{1,0:T(8,128)(2,1)S(1)} %add_convert_fusion.2), channel_id=1, source_target_pairs={{0,224},{32,0},{64,32},{96,64},{128,96},{160,128},{192,160},{224,1... | collective-permute-start | bytes 589832 | tf_op jit(solution)/shard_map/ppermute | solution.py:281
  234.9 3.2 %collective-permute-done.6 = bf16[128,768]{1,0:T(8,128)(2,1)S(1)} collective-permute-done((bf16[128,768]{1,0:T(8,128)(2,1)S(1)}, bf16[128,768]{1,0:T(8,128)(2,1)S(1)}, u32[]{:S(2)}, u32[]{:S(2)}) %collective-permute-start.6) | collective-permute-done | bytes 196640 | tf_op jit(solution)/shard_map/ppermute | solution.py:281
  238.1 0.7 copy.9
  (6 shorter events, 0.1 us)
Async XLA Ops:
  4.6 53.1 %all-to-all-start = ((bf16[16,72,1536]{2,1,0:T(8,128)(2,1)}), bf16[16,72,1536]{2,1,0:T(8,128)(2,1)S(1)}, u32[]{:S(2)}, u32[]{:S(2)}) async-start(bf16[16,72,1536]{2,1,0:T(8,128)(2,1)} %bitcast.70), calls=%async_computation | async-start | bytes 7077888 | tf_op jit(solution)/shard_map/all_to_all | solution.py:263
  57.8 11.9 %collective-permute-start = (bf16[2,576,1536]{2,1,0:T(8,128)(2,1)S(1)}, bf16[2,576,1536]{2,1,0:T(8,128)(2,1)}, u32[]{:S(2)}, u32[]{:S(2)}) collective-permute-start(bf16[2,576,1536]{2,1,0:T(8,128)(2,1)S(1)} %bitcast.57), channel_id=1, source_target_pairs={{0,1},{1,0},{2,3},{3,2},{4,5},{5,4},{6,7},{7,6},{8,9},{9,8},{10,11... | collective-permute-start | bytes 10616840 | tf_op jit(solution)/shard_map/ppermute | solution.py:260
  57.8 37.9 %all-to-all-start.1 = ((bf16[16,72,768]{2,1,0:T(8,128)(2,1)}), bf16[16,72,768]{2,1,0:T(8,128)(2,1)}, u32[]{:S(2)}, u32[]{:S(2)}) async-start(bf16[16,72,768]{2,1,0:T(8,128)(2,1)} %bitcast.73), calls=%async_computation.1 | async-start | bytes 3538944 | tf_op jit(solution)/shard_map/all_to_all | solution.py:263
  88.2 1.2 copy-start
  89.4 6.4 %copy-start.1 = (bf16[2,576,768]{2,1,0:T(8,128)(2,1)S(1)}, bf16[2,576,768]{2,1,0:T(8,128)(2,1)}, u32[]{:S(2)}) copy-start(bf16[2,576,768]{2,1,0:T(8,128)(2,1)} %copy-done) | copy-start | bytes 5308420
  95.7 3.7 %collective-permute-start.1 = (bf16[2,576,768]{2,1,0:T(8,128)(2,1)S(1)}, bf16[2,576,768]{2,1,0:T(8,128)(2,1)S(1)}, u32[]{:S(2)}, u32[]{:S(2)}) collective-permute-start(bf16[2,576,768]{2,1,0:T(8,128)(2,1)S(1)} %copy-done.1), channel_id=1, source_target_pairs={{0,1},{1,0},{2,3},{3,2},{4,5},{5,4},{6,7},{7,6},{8,9},{9,8},{10,11... | collective-permute-start | bytes 5308424 | tf_op jit(solution)/shard_map/ppermute | solution.py:260
  101.1 6.0 %copy-start.6 = (s32[1,2]{1,0:T(1,128)S(1)}, s32[1,2]{1,0:T(1,128)}, u32[]{:S(2)}) copy-start(s32[1,2]{1,0:T(1,128)} %param.11) | copy-start | bytes 28
  101.1 10.4 %copy-start.5 = (s32[1,2,128,2]{2,3,1,0:T(2,128)S(1)}, s32[1,2,128,2]{2,3,1,0:T(2,128)}, u32[]{:S(2)}) copy-start(s32[1,2,128,2]{2,3,1,0:T(2,128)} %param.9) | copy-start | bytes 6148
  101.1 10.4 %copy-start.7 = (f32[1,2,128,2]{2,3,1,0:T(2,128)S(1)}, f32[1,2,128,2]{2,3,1,0:T(2,128)}, u32[]{:S(2)}) copy-start(f32[1,2,128,2]{2,3,1,0:T(2,128)} %param.10) | copy-start | bytes 6148
  101.1 31.4 %all-to-all-start.2 = ((bf16[16,72,768]{2,1,0:T(8,128)(2,1)}), bf16[16,72,768]{2,1,0:T(8,128)(2,1)S(1)}, u32[]{:S(2)}, u32[]{:S(2)}) async-start(bf16[16,72,768]{2,1,0:T(8,128)(2,1)} %bitcast.18), calls=%async_computation.2 | async-start | bytes 3538944 | tf_op jit(solution)/shard_map/all_to_all | solution.py:263
  107.1 25.7 %copy-start.2 = (bf16[1,128,768]{2,1,0:T(8,128)(2,1)S(1)}, bf16[1,128,768]{2,1,0:T(8,128)(2,1)}, u32[]{:S(2)}) copy-start(bf16[1,128,768]{2,1,0:T(8,128)(2,1)} %refs_3_.1) | copy-start | bytes 589828
  133.6 9.1 %collective-permute-start.2 = (bf16[128,768]{1,0:T(8,128)(2,1)S(1)}, bf16[128,768]{1,0:T(8,128)(2,1)S(1)}, u32[]{:S(2)}, u32[]{:S(2)}) collective-permute-start(bf16[128,768]{1,0:T(8,128)(2,1)S(1)} %fusion.1), channel_id=1, source_target_pairs={{0,224},{32,0},{64,32},{96,64},{128,96},{160,128},{192,160},{224,1... | collective-permute-start | bytes 589832 | tf_op jit(solution)/shard_map/ppermute | solution.py:281
  142.8 0.7 copy-start.3
  147.5 5.0 %collective-permute-start.3 = (bf16[2,576,768]{2,1,0:T(8,128)(2,1)}, bf16[2,576,768]{2,1,0:T(8,128)(2,1)S(1)}, u32[]{:S(2)}, u32[]{:S(2)}) collective-permute-start(bf16[2,576,768]{2,1,0:T(8,128)(2,1)} %bitcast.17.mine_ref), channel_id=1, source_target_pairs={{0,1},{1,0},{2,3},{3,2},{4,5},{5,4},{6,7},{7,6},{8,9},{9,8},{10,11... | collective-permute-start | bytes 5308424 | tf_op jit(solution)/shard_map/ppermute | solution.py:260
  147.5 30.8 %all-to-all-start.3 = ((bf16[16,72,768]{2,1,0:T(8,128)(2,1)}), bf16[16,72,768]{2,1,0:T(8,128)(2,1)S(1)}, u32[]{:S(2)}, u32[]{:S(2)}) async-start(bf16[16,72,768]{2,1,0:T(8,128)(2,1)} %bitcast.71), calls=%async_computation.3 | async-start | bytes 3538944 | tf_op jit(solution)/shard_map/all_to_all | solution.py:263
  178.3 3.7 %collective-permute-start.4 = (bf16[2,576,768]{2,1,0:T(8,128)(2,1)S(1)}, bf16[2,576,768]{2,1,0:T(8,128)(2,1)S(1)}, u32[]{:S(2)}, u32[]{:S(2)}) collective-permute-start(bf16[2,576,768]{2,1,0:T(8,128)(2,1)S(1)} %bitcast.60), channel_id=1, source_target_pairs={{0,1},{1,0},{2,3},{3,2},{4,5},{5,4},{6,7},{7,6},{8,9},{9,8},{10,11... | collective-permute-start | bytes 5308424 | tf_op jit(solution)/shard_map/ppermute | solution.py:260
  191.9 3.9 %collective-permute-start.5 = (bf16[2,576,768]{2,1,0:T(8,128)(2,1)S(1)}, bf16[2,576,768]{2,1,0:T(8,128)(2,1)S(1)}, u32[]{:S(2)}, u32[]{:S(2)}) collective-permute-start(bf16[2,576,768]{2,1,0:T(8,128)(2,1)S(1)} %get-tuple-element.30), channel_id=1, source_target_pairs={{0,1},{1,0},{2,3},{3,2},{4,5},{5,4},{6,7},{7,6},{8,9},{9,8},{10,11... | collective-permute-start | bytes 5308424 | tf_op jit(solution)/shard_map/ppermute | solution.py:260
  197.5 32.5 %all-to-all-start.4 = ((bf16[16,72,768]{2,1,0:T(8,128)(2,1)}), bf16[16,72,768]{2,1,0:T(8,128)(2,1)S(1)}, u32[]{:S(2)}, u32[]{:S(2)}) async-start(bf16[16,72,768]{2,1,0:T(8,128)(2,1)} %bitcast.29), calls=%async_computation.4 | async-start | bytes 3538944 | tf_op jit(solution)/shard_map/all_to_all | solution.py:263
  204.0 26.2 %copy-start.4 = (bf16[128,768]{1,0:T(8,128)(2,1)S(1)}, bf16[128,768]{1,0:T(8,128)(2,1)}, u32[]{:S(2)}) copy-start(bf16[128,768]{1,0:T(8,128)(2,1)} %copy-done.3) | copy-start | bytes 589828
  231.1 7.0 %collective-permute-start.6 = (bf16[128,768]{1,0:T(8,128)(2,1)S(1)}, bf16[128,768]{1,0:T(8,128)(2,1)S(1)}, u32[]{:S(2)}, u32[]{:S(2)}) collective-permute-start(bf16[128,768]{1,0:T(8,128)(2,1)S(1)} %add_convert_fusion.2), channel_id=1, source_target_pairs={{0,224},{32,0},{64,32},{96,64},{128,96},{160,128},{192,160},{224,1... | collective-permute-start | bytes 589832 | tf_op jit(solution)/shard_map/ppermute | solution.py:281

commit v4 on v3

v4 whole, which is shorter than its diff:
```python
import jax
import jax.numpy as jnp
from jax import lax
from jax.experimental import pallas as pl
from jax.experimental.pallas import tpu as pltpu
from jax.sharding import Mesh, PartitionSpec as P

EXPERTS = 4
CAPACITY = 72
HIDDEN_BLOCK = 256
VMEM_LIMIT = 32 * 1024 * 1024


def together(*values):
    return lax.optimization_barrier(values)


def contract_last(left, right):
    return lax.dot_general(
        left, right, (((1,), (1,)), ((), ())), preferred_element_type=jnp.float32
    )


def quarter_copies(core, mine, other, column, weight, by_rows, rows_buf, weight_buf, semaphores):
    quarter = rows_buf.shape[2]
    copies = []
    for number in range(rows_buf.shape[0]):
        xhi = number % mine.shape[0]
        swapped = number // mine.shape[0]
        first = pl.multiple_of((2 * xhi + (1 - core if swapped else core)) * quarter, quarter)
        part = pl.ds(first, quarter)
        source = other if swapped else mine
        copies.append(
            (
                pltpu.make_async_copy(
                    source.at[xhi, :, pl.ds(column * quarter, quarter)],
                    rows_buf.at[number],
                    semaphores.at[2 * number],
                ),
                pltpu.make_async_copy(
                    weight.at[part, :] if by_rows else weight.at[:, part],
                    weight_buf.at[number],
                    semaphores.at[2 * number + 1],
                ),
            )
        )
    return copies


def hidden_blocks(hidden):
    return [slice(start, start + HIDDEN_BLOCK) for start in range(0, hidden, HIDDEN_BLOCK)]


def factor_kernel(
    column, core_ref, mine, other, up, out, rows_buf, up_buf, acc, semaphores, out_semaphores
):
    copies = quarter_copies(
        core_ref[0], mine, other, column, up, True, rows_buf, up_buf, semaphores
    )
    for pair in copies:
        for copy in pair:
            copy.start()
    last = len(copies) - 1
    blocks = hidden_blocks(acc.shape[1])
    sent = []
    for number, pair in enumerate(copies):
        for copy in pair:
            copy.wait()
        for index, block in enumerate(blocks):
            part = jnp.dot(
                rows_buf[number], up_buf[number, :, block], preferred_element_type=jnp.float32
            )
            if number:
                part = acc[:, block] + part
            if number < last:
                acc[:, block] = part
                continue
            sigma = jax.nn.sigmoid(part)
            acc[:, block] = sigma * (1.0 + part * (1.0 - sigma))
            sent.append(
                pltpu.make_async_copy(
                    acc.at[:, block], out.at[:, block], out_semaphores.at[index]
                )
            )
            sent[-1].start()
    for copy in sent:
        copy.wait()


def own_copies(kernel, name, out, scratch, core, *operands):
    anywhere = pl.BlockSpec(memory_space=pltpu.HBM)
    return pl.pallas_call(
        kernel,
        out_shape=out,
        in_specs=[pl.BlockSpec(memory_space=pltpu.SMEM)] + [anywhere] * len(operands),
        out_specs=jax.tree.map(lambda _: anywhere, out),
        scratch_shapes=scratch,
        compiler_params=pltpu.CompilerParams(vmem_limit_bytes=VMEM_LIMIT),
        cost_estimate=pl.CostEstimate(flops=1000, transcendentals=0, bytes_accessed=1000),
        name=name,
    )(core, *operands)


def factor(core, saved, up):
    mine, other, column = saved
    halves, rows = mine.shape[:2]
    width, hidden = up.shape
    pieces = 2 * halves
    quarter = width // pieces
    return own_copies(
        lambda *refs: factor_kernel(column, *refs),
        "factor",
        jax.ShapeDtypeStruct((rows, hidden), jnp.float32),
        [
            pltpu.VMEM((pieces, rows, quarter), jnp.bfloat16),
            pltpu.VMEM((pieces, quarter, hidden), jnp.bfloat16),
            pltpu.VMEM((rows, hidden), jnp.float32),
            pltpu.SemaphoreType.DMA((2 * pieces,)),
            pltpu.SemaphoreType.DMA((hidden // HIDDEN_BLOCK,)),
        ],
        core,
        mine,
        other,
        up,
    )


def sent_kernel(
    column,
    core_ref,
    mine,
    other,
    down,
    factors,
    up,
    grad_pre_out,
    send_out,
    rows_buf,
    down_buf,
    acc,
    factor_buf,
    up_buf,
    grad_pre,
    send,
    semaphores,
    late_semaphores,
):
    core = core_ref[0]
    halves, _, quarter = send.shape
    copies = quarter_copies(
        core, mine, other, column, down, False, rows_buf, down_buf, semaphores
    )
    factor_copy = pltpu.make_async_copy(factors, factor_buf, late_semaphores.at[0])
    up_copies = [
        pltpu.make_async_copy(
            up.at[pl.ds(pl.multiple_of((2 * half + 1 - core) * quarter, quarter), quarter), :],
            up_buf.at[half],
            late_semaphores.at[1 + half],
        )
        for half in range(halves)
    ]
    for pair in copies:
        for copy in pair:
            copy.start()
    factor_copy.start()
    for copy in up_copies:
        copy.start()
    last = len(copies) - 1
    blocks = hidden_blocks(acc.shape[1])
    for number, pair in enumerate(copies):
        for copy in pair:
            copy.wait()
        if number == last:
            factor_copy.wait()
        for block in blocks:
            part = contract_last(rows_buf[number], down_buf[number, block, :])
            if number:
                part = acc[:, block] + part
            if number < last:
                acc[:, block] = part
            else:
                grad_pre[:, block] = (part * factor_buf[:, block]).astype(jnp.bfloat16)
    sent = [pltpu.make_async_copy(grad_pre, grad_pre_out, late_semaphores.at[1 + halves])]
    sent[0].start()
    for half in range(halves):
        up_copies[half].wait()
        send[half] = contract_last(grad_pre[...], up_buf[half]).astype(jnp.bfloat16)
        sent.append(
            pltpu.make_async_copy(
                send.at[half], send_out.at[half], late_semaphores.at[2 + halves + half]
            )
        )
        sent[-1].start()
    for copy in sent:
        copy.wait()


def sent_part(core, grads, down, factors, up):
    mine, other, column = grads
    halves, rows = mine.shape[:2]
    hidden, width = down.shape
    pieces = 2 * halves
    quarter = width // pieces
    return own_copies(
        lambda *refs: sent_kernel(column, *refs),
        "sent_part",
        (
            jax.ShapeDtypeStruct((rows, hidden), jnp.bfloat16),
            jax.ShapeDtypeStruct((halves, rows, quarter), jnp.bfloat16),
        ),
        [
            pltpu.VMEM((pieces, rows, quarter), jnp.bfloat16),
            pltpu.VMEM((pieces, hidden, quarter), jnp.bfloat16),
            pltpu.VMEM((rows, hidden), jnp.float32),
            pltpu.VMEM((rows, hidden), jnp.float32),
            pltpu.VMEM((halves, quarter, hidden), jnp.bfloat16),
            pltpu.VMEM((rows, hidden), jnp.bfloat16),
            pltpu.VMEM((halves, rows, quarter), jnp.bfloat16),
            pltpu.SemaphoreType.DMA((2 * pieces,)),
            pltpu.SemaphoreType.DMA((2 + 2 * halves,)),
        ],
        core,
        mine,
        other,
        down,
        factors,
        up,
    )


def kept_kernel(core_ref, grad_pre_ref, up_ref, keep_ref):
    keep_ref[0] = contract_last(grad_pre_ref[...], up_ref[...]).astype(jnp.bfloat16)


def kept_part(core, grad_pre, up):
    rows, hidden = grad_pre.shape
    quarter = up.shape[0] // 4
    halves = 2
    return pl.pallas_call(
        kept_kernel,
        out_shape=jax.ShapeDtypeStruct((halves, rows, quarter), jnp.bfloat16),
        grid_spec=pltpu.PrefetchScalarGridSpec(
            num_scalar_prefetch=1,
            grid=(halves,),
            in_specs=[
                pl.BlockSpec((rows, hidden), lambda i, c: (0, 0)),
                pl.BlockSpec((quarter, hidden), lambda i, c: (2 * i + c[0], 0)),
            ],
            out_specs=pl.BlockSpec((1, rows, quarter), lambda i, c: (i, 0, 0)),
        ),
        compiler_params=pltpu.CompilerParams(
            dimension_semantics=("arbitrary",), vmem_limit_bytes=VMEM_LIMIT
        ),
        cost_estimate=pl.CostEstimate(
            flops=2 * rows * hidden * halves * quarter,
            transcendentals=0,
            bytes_accessed=2 * hidden * (rows + halves * quarter),
        ),
        name="kept_part",
    )(core, grad_pre, up)


def pick_kernel(plan_ref, routes_ref, *refs):
    del plan_ref
    values, (out, buffer, semaphores) = refs[:-3], refs[-3:]
    rows = routes_ref.shape[2]
    expert = lax.broadcasted_iota(jnp.int32, (16, rows), 0)
    named = routes_ref[0]
    chosen = named[0:1] == expert
    for choice in range(1, named.shape[0]):
        chosen = chosen | (named[choice : choice + 1] == expert)
    earlier = (
        lax.broadcasted_iota(jnp.int32, (rows, rows), 0)
        < lax.broadcasted_iota(jnp.int32, (rows, rows), 1)
    ).astype(jnp.float32)
    before = jnp.dot(
        chosen.astype(jnp.float32).astype(jnp.bfloat16),
        earlier.astype(jnp.bfloat16),
        preferred_element_type=jnp.float32,
    )
    place = jnp.where(chosen, before, -1.0).astype(jnp.int32)
    slot = lax.broadcasted_iota(jnp.int32, (CAPACITY, rows), 0)
    copies = []
    for j in range(EXPERTS):
        select = (place[j : j + 1] == slot).astype(jnp.float32).astype(jnp.bfloat16)
        start = 0
        for value_ref in values:
            width = value_ref.shape[2]
            buffer[j, :, start : start + width] = jnp.dot(
                select, value_ref[0], preferred_element_type=jnp.float32
            ).astype(jnp.bfloat16)
            start += width
        for i in range(out.shape[0]):
            for k in range(out.shape[2]):
                copy = pltpu.make_async_copy(
                    buffer.at[j], out.at[i, j, k], semaphores.at[len(copies)]
                )
                copy.start()
                copies.append(copy)
    for copy in copies:
        copy.wait()


def pick(step, plan, routes, values, n_xhi, per_expert):
    width = sum(value.shape[2] for value, _ in values)
    specs = [pl.BlockSpec((1,) + routes.shape[1:], lambda i, p: (p[step], 0, 0))]
    for value, planned in values:
        if planned:
            specs.append(pl.BlockSpec((1,) + value.shape[1:], lambda i, p: (p[step], 0, 0)))
        else:
            specs.append(pl.BlockSpec((1,) + value.shape[1:], lambda i, p: (0, 0, 0)))
    out = pl.pallas_call(
        pick_kernel,
        out_shape=jax.ShapeDtypeStruct(
            (n_xhi, EXPERTS, per_expert, CAPACITY, width), jnp.bfloat16
        ),
        grid_spec=pltpu.PrefetchScalarGridSpec(
            num_scalar_prefetch=1,
            grid=(1,),
            in_specs=specs,
            out_specs=pl.BlockSpec(memory_space=pltpu.HBM),
            scratch_shapes=[
                pltpu.VMEM((EXPERTS, CAPACITY, width), jnp.bfloat16),
                pltpu.SemaphoreType.DMA((n_xhi * EXPERTS * per_expert,)),
            ],
        ),
        compiler_params=pltpu.CompilerParams(dimension_semantics=("arbitrary",)),
        name="pick",
    )(plan, routes, *[value for value, _ in values])
    return out.reshape(n_xhi * EXPERTS * per_expert, CAPACITY, width)


def slots(route_now, share_now):
    rows = route_now.shape[0]
    named = route_now.T[None] == jnp.arange(EXPERTS, dtype=jnp.int32)[:, None, None]
    chosen = jnp.any(named, axis=1)
    mix = jnp.sum(jnp.where(named, share_now.T[None], 0.0), axis=1)
    token = jnp.arange(rows, dtype=jnp.int32)
    earlier = (token[:, None] < token[None, :]).astype(jnp.bfloat16)
    before = jnp.dot(
        chosen.astype(jnp.bfloat16), earlier, preferred_element_type=jnp.float32
    ).astype(jnp.int32)
    place = jnp.where(chosen, before, -1)
    hit = place[:, None, :] == jnp.arange(CAPACITY, dtype=jnp.int32)[None, :, None]
    mixing = jnp.where(hit, mix[:, None, :], 0.0).reshape(EXPERTS * CAPACITY, rows)
    return mixing


def per_device(grad_in, saved_input, routes, route_weights, plan, up_weight, down_weight):
    n_expert = lax.axis_size("expert")
    n_xhi = lax.axis_size("xhi")
    n_section = lax.axis_size("section")
    per_expert = n_expert // EXPERTS
    peers = n_xhi * n_expert
    rows, quarter = grad_in.shape[1:]
    up_local = pltpu.with_memory_space_constraint(up_weight[0], pltpu.HBM)
    down_local = pltpu.with_memory_space_constraint(down_weight[0], pltpu.HBM)
    core = lax.axis_index("core").astype(jnp.int32).reshape(1)

    def swap_cores(value):
        return lax.ppermute(value, "core", [(0, 1), (1, 0)])

    def exchange(value):
        return lax.all_to_all(value, ("xhi", "expert"), split_axis=0, concat_axis=0, tiled=True)

    def deliver(sent):
        return exchange(sent).reshape(n_xhi, n_expert * CAPACITY, sent.shape[2])

    def combine(current, mixing, arrived):
        summed = jnp.sum(
            arrived.reshape(n_xhi, EXPERTS, per_expert, CAPACITY, quarter).astype(jnp.float32),
            axis=(0, 2),
        )
        moe_term = lax.dot_general(
            mixing,
            summed.reshape(EXPERTS * CAPACITY, quarter),
            (((0,), (0,)), ((), ())),
            precision=lax.Precision.HIGHEST,
            preferred_element_type=jnp.float32,
        )
        result = (current.astype(jnp.float32) + moe_term).astype(jnp.bfloat16)
        return lax.ppermute(
            result, "section", [(i, (i - 1) % n_section) for i in range(n_section)]
        )

    def outgoing(send, keep):
        return (
            keep.astype(jnp.float32) + swap_cores(send).astype(jnp.float32)
        ).astype(jnp.bfloat16).reshape(peers, CAPACITY, quarter)

    micros = plan[0]
    routes_by_choice = routes[0].transpose(0, 2, 1)
    saved_all = saved_input[0]
    current = grad_in[0]
    ticks = micros.shape[0]

    def mixing_of(tick):
        route_now = lax.dynamic_index_in_dim(routes[0], micros[tick], 0, keepdims=False)
        share_now = lax.dynamic_index_in_dim(route_weights[0], micros[tick], 0, keepdims=False)
        return slots(route_now, share_now)

    def pick_rows(tick, *values):
        return pick(tick, micros, routes_by_choice, values, n_xhi, per_expert)

    rows_in = deliver(pick_rows(0, (saved_all, True), (current[None], False)))
    later = None
    for tick in range(ticks):
        if tick == 0:
            both, swapped = rows_in, None
            if ticks > 1:
                saved_sent, both = together(pick_rows(1, (saved_all, True)), both)
                later = deliver(saved_sent)
            swapped = swap_cores(both)
            saved, grads = (both, swapped, 0), (both, swapped, 1)
            factors = factor(core, saved, up_local)
        else:
            grad_sent, later = together(pick_rows(tick, (current[None], False)), later)
            grad_rows = deliver(grad_sent)
            factors = factor(core, (later, swap_cores(later), 0), up_local)
            grad_rows, factors = together(grad_rows, factors)
            grads = (grad_rows, swap_cores(grad_rows), 0)
        grad_pre, send = sent_part(core, grads, down_local, factors, up_local)
        keep = kept_part(core, grad_pre, up_local)
        if tick + 1 < ticks:
            send, later, keep = together(send, later, keep)
        partial_rows = (
            keep.astype(jnp.float32) + swap_cores(send).astype(jnp.float32)
        ).astype(jnp.bfloat16)
        arrived = exchange(partial_rows.reshape(peers, CAPACITY, quarter))
        current = combine(current, mixing_of(tick), arrived)
    return current[None]


def solution(mesh):
    sections, experts, parts = (mesh.shape[name] for name in ("section", "expert", "mp"))
    refined = Mesh(
        mesh.devices.reshape(sections, experts, parts // 2, 2),
        ("section", "expert", "xhi", "core"),
    )
    mp = ("xhi", "core")
    placed = (
        P("section", "expert", mp),
        P("section", None, "expert", mp),
        P("section", None, "expert", None),
        P("section", None, "expert", None),
        P("section", None),
        P("section", None, ("expert", "xhi", "core")),
        P("section", ("expert", "xhi", "core"), None),
    )
    return jax.shard_map(
        per_device,
        mesh=refined,
        in_specs=placed,
        out_specs=P("section", "expert", mp),
        check_vma=False,
    )
```

time: 240 us -> 239 us (level)
  Pallas kernels: 56.6 us -> 52.9 us
  local copies, waits for them, and re-layouts: 3.19 us -> 5.94 us
    pallas_call x7, Pallas kernels: 49.1 us -> 45.4 us  [the longest x4 34.9 us: own_copies(): pl.pallas_call(kernel, out_shape=out, in_specs=[pl.BlockSpec(memory_space...]
    unnamed x17 -> x21, local copies, waits for them, and re-layouts: 2.58 us -> 5.33 us
  transfers between devices with their start and end apart: 12 -> 12, of which waited for: 9 -> 9; matrix products, arithmetic and copies ran while one was open for 0% -> 0% of each run, Pallas kernels for 16% -> 15%
where the time goes in v4:
time: 239 us; the launch traced here: 238 us
  waiting for transfers between devices  122 us (51%)
  Pallas kernels  52.9 us (22%)
  starting transfers between devices  47.7 us (20%)
  local copies, waits for them, and re-layouts  5.94 us (2%)
  between operations  4.08 us (2%)
  other arithmetic  3.94 us (2%)
    all_to_all x5, waiting for transfers between devices, exchange(): lax.all_to_all(value, ('xhi', 'expert'), split_axis=0, concat_axis=0, til...  108 us
    all_to_all x5, starting transfers between devices, exchange(): lax.all_to_all(value, ('xhi', 'expert'), split_axis=0, concat_axis=0, til...  37.4 us
    pallas_call x4, Pallas kernels, own_copies(): pl.pallas_call(kernel, out_shape=out, in_specs=[pl.BlockSpec(memory_space...  34.9 us
    pallas_call x3, Pallas kernels, pick(): pl.pallas_call(pick_kernel, out_shape=jax.ShapeDtypeStruct((n_xhi, EXPERT...  10.5 us
    ppermute x2, starting transfers between devices, combine(): lax.ppermute(result, 'section', [(i, (i - 1) % n_section) for i in range(...  9.73 us
    ppermute x5, waiting for transfers between devices, swap_cores(): return lax.ppermute(value, 'core', [(0, 1), (1, 0)])  7.6 us
    pallas_call x2, Pallas kernels, kept_part(): pl.pallas_call(kept_kernel, out_shape=jax.ShapeDtypeStruct((halves, rows,...  7.48 us
    ppermute x2, waiting for transfers between devices, combine(): lax.ppermute(result, 'section', [(i, (i - 1) % n_section) for i in range(...  6.38 us
  transfers between devices with their start and end apart: 12, of which 9 were waited for; matrix products, arithmetic and copies ran while one was open for 0% of the time, Pallas kernels for 15%

profile of v4, /device:TPU:8, one launch (start us, length us, event | category | flops | bytes accessed | tf_op | source)
XLA Modules:
  0.0 238.4 jit_solution(100711057595688217)
XLA Ops:
  0.0 3.9 %pick.4 = bf16[2,4,2,72,1536]{4,3,2,1,0:T(8,128)(2,1)} custom-call(s32[2]{0:T(128)} %bitcast.80, s32[2,2,128]{2,1,0:T(2,128)} %bitcast.77, bf16[2,128,768]{2,1,0:T(8,128)(2,1)} %bitcast.73, bf16[1,128,768]{2,1,0:T(8,128)(2,1)} %refs_1_.1), custom_call_target="tpu_custom_call" | custom-call | tf_op jit(solution)/shard_map/pick/pallas_call | solution.py:312
  3.9 7.4 %all-to-all-start = ((bf16[16,72,1536]{2,1,0:T(8,128)(2,1)}), bf16[16,72,1536]{2,1,0:T(8,128)(2,1)S(1)}, u32[]{:S(2)}, u32[]{:S(2)}) async-start(bf16[16,72,1536]{2,1,0:T(8,128)(2,1)} %bitcast.68), calls=%async_computation | async-start | bytes 7077888 | tf_op jit(solution)/shard_map/all_to_all | solution.py:364
  11.3 3.3 %pick.3 = bf16[2,4,2,72,768]{4,3,2,1,0:T(8,128)(2,1)} custom-call(s32[2]{0:T(128)} %bitcast.81, s32[2,2,128]{2,1,0:T(2,128)} %bitcast.78, bf16[2,128,768]{2,1,0:T(8,128)(2,1)} %bitcast.74), custom_call_target="tpu_custom_call" | custom-call | tf_op jit(solution)/shard_map/pick/pallas_call | solution.py:312
  14.7 42.4 %all-to-all-done = bf16[16,72,1536]{2,1,0:T(8,128)(2,1)S(1)} async-done(((bf16[16,72,1536]{2,1,0:T(8,128)(2,1)}), bf16[16,72,1536]{2,1,0:T(8,128)(2,1)S(1)}, u32[]{:S(2)}, u32[]{:S(2)}) %all-to-all-start) | async-done | bytes 3538976 | tf_op jit(solution)/shard_map/all_to_all | solution.py:364
  57.1 0.0 collective-permute-start
  57.1 11.9 %all-to-all-start.1 = ((bf16[16,72,768]{2,1,0:T(8,128)(2,1)}), bf16[16,72,768]{2,1,0:T(8,128)(2,1)}, u32[]{:S(2)}, u32[]{:S(2)}) async-start(bf16[16,72,768]{2,1,0:T(8,128)(2,1)} %bitcast.71), calls=%async_computation.1 | async-start | bytes 3538944 | tf_op jit(solution)/shard_map/all_to_all | solution.py:364
  69.0 0.0 collective-permute-done.refs_2_
  69.0 7.9 %factor.2.refs_4_ = f32[576,1024]{1,0:T(8,128)S(1)} custom-call(s32[1]{0:T(128)} %bitcast.6.refs_0_.core_ref, bf16[2,576,1536]{2,1,0:T(8,128)(2,1)S(1)} %bitcast.58, bf16[2,576,1536]{2,1,0:T(8,128)(2,1)} %collective-permute-done.refs_2_, bf16[3072,1024]{1,0:T(8,128)(2,1)} %bitcast.60), custom_call_target="tpu_custom_call" | custom-call | flops 1000 | bytes 1000 | tf_op jit(solution)/shard_map/factor/pallas_call | solution.py:92
  76.9 9.5 %sent_part.2 = (bf16[576,1024]{1,0:T(8,128)(2,1)S(1)}, bf16[2,576,768]{2,1,0:T(8,128)(2,1)S(1)}) custom-call(s32[1]{0:T(128)} %bitcast.6.refs_0_.core_ref, bf16[2,576,1536]{2,1,0:T(8,128)(2,1)S(1)} %bitcast.59, bf16[2,576,1536]{2,1,0:T(8,128)(2,1)} %collective-permute-done.refs_2_, bf16[1024,3072]{1,0:T(8,128)(2,1)} %bitcast.66, ...), custom_call_target="tpu_custom_call" | custom-call | flops 1000 | bytes 1000 | tf_op jit(solution)/shard_map/sent_part/pallas_call | solution.py:92
  86.4 0.0 copy-start.2
  86.4 1.2 copy-done.2
  87.7 0.0 copy-start.3
  87.7 3.8 %kept_part.2 = bf16[2,576,768]{2,1,0:T(8,128)(2,1)S(1)} custom-call(s32[1]{0:T(128)} %bitcast.6.refs_0_.core_ref, bf16[576,1024]{1,0:T(8,128)(2,1)S(1)} %get-tuple-element.21.grad_pre_ref, bf16[3072,1024]{1,0:T(8,128)(2,1)} %bitcast.62), custom_call_target="tpu_custom_call" | custom-call | flops 1811939328 | bytes 4325376 | tf_op jit(solution)/shard_map/kept_part/pallas_call | solution.py:239
  91.5 3.6 %all-to-all-done.1 = bf16[16,72,768]{2,1,0:T(8,128)(2,1)} async-done(((bf16[16,72,768]{2,1,0:T(8,128)(2,1)}), bf16[16,72,768]{2,1,0:T(8,128)(2,1)}, u32[]{:S(2)}, u32[]{:S(2)}) %all-to-all-start.1) | async-done | bytes 1769504 | tf_op jit(solution)/shard_map/all_to_all | solution.py:364
  95.0 0.0 copy-done.3
  95.0 0.0 collective-permute-start.1
  95.0 3.7 %collective-permute-done.1 = bf16[2,576,768]{2,1,0:T(8,128)(2,1)S(1)} collective-permute-done((bf16[2,576,768]{2,1,0:T(8,128)(2,1)S(1)}, bf16[2,576,768]{2,1,0:T(8,128)(2,1)S(1)}, u32[]{:S(2)}, u32[]{:S(2)}) %collective-permute-start.1) | collective-permute-done | bytes 1769504 | tf_op jit(solution)/shard_map/ppermute | solution.py:361
  98.7 1.7 add_convert_fusion.1
  100.4 0.0 copy-start.8
  100.4 0.0 copy-start.7
  100.4 0.0 copy-start.9
  100.4 6.0 %all-to-all-start.2 = ((bf16[16,72,768]{2,1,0:T(8,128)(2,1)}), bf16[16,72,768]{2,1,0:T(8,128)(2,1)S(1)}, u32[]{:S(2)}, u32[]{:S(2)}) async-start(bf16[16,72,768]{2,1,0:T(8,128)(2,1)} %bitcast.18), calls=%async_computation.2 | async-start | bytes 3538944 | tf_op jit(solution)/shard_map/all_to_all | solution.py:364
  106.4 0.0 copy-done.8
  106.4 0.0 copy-start.4
  106.4 0.6 fusion.18
  110.9 0.0 copy-done.7
  110.9 0.0 copy-done.9
  110.9 0.1 fusion.3
  111.1 20.8 %all-to-all-done.2 = bf16[16,72,768]{2,1,0:T(8,128)(2,1)S(1)} async-done(((bf16[16,72,768]{2,1,0:T(8,128)(2,1)}), bf16[16,72,768]{2,1,0:T(8,128)(2,1)S(1)}, u32[]{:S(2)}, u32[]{:S(2)}) %all-to-all-start.2) | async-done | bytes 1769504 | tf_op jit(solution)/shard_map/all_to_all | solution.py:364
  131.9 0.2 convert_reduce_fusion.1
  132.1 0.0 copy-done.4
  132.1 0.8 fusion.1
  133.0 5.9 %collective-permute-start.2 = (bf16[128,768]{1,0:T(8,128)(2,1)S(1)}, bf16[128,768]{1,0:T(8,128)(2,1)S(1)}, u32[]{:S(2)}, u32[]{:S(2)}) collective-permute-start(bf16[128,768]{1,0:T(8,128)(2,1)S(1)} %fusion.1), channel_id=1, source_target_pairs={{0,224},{32,0},{64,32},{96,64},{128,96},{160,128},{192,160},{224,1... | collective-permute-start | bytes 589832 | tf_op jit(solution)/shard_map/ppermute | solution.py:382
  138.9 3.2 %collective-permute-done.2 = bf16[128,768]{1,0:T(8,128)(2,1)S(1)} collective-permute-done((bf16[128,768]{1,0:T(8,128)(2,1)S(1)}, bf16[128,768]{1,0:T(8,128)(2,1)S(1)}, u32[]{:S(2)}, u32[]{:S(2)}) %collective-permute-start.2) | collective-permute-done | bytes 196640 | tf_op jit(solution)/shard_map/ppermute | solution.py:382
  142.1 0.0 copy-start.5
  142.1 0.7 copy-done.5
  142.8 3.2 %pick.5 = bf16[2,4,2,72,768]{4,3,2,1,0:T(8,128)(2,1)} custom-call(s32[2]{0:T(128)} %bitcast.82, s32[2,2,128]{2,1,0:T(2,128)} %bitcast.79, bf16[1,128,768]{2,1,0:T(8,128)(2,1)} %bitcast.75), custom_call_target="tpu_custom_call" | custom-call | tf_op jit(solution)/shard_map/pick/pallas_call | solution.py:312
  146.0 0.1 collective-permute-start.3
  146.1 5.6 %all-to-all-start.3 = ((bf16[16,72,768]{2,1,0:T(8,128)(2,1)}), bf16[16,72,768]{2,1,0:T(8,128)(2,1)}, u32[]{:S(2)}, u32[]{:S(2)}) async-start(bf16[16,72,768]{2,1,0:T(8,128)(2,1)} %bitcast.69), calls=%async_computation.3 | async-start | bytes 3538944 | tf_op jit(solution)/shard_map/all_to_all | solution.py:364
  151.7 0.0 collective-permute-done.3.refs_2_
  151.8 0.0 copy-start
  151.8 1.2 copy-done
  153.0 0.0 copy-start.1
  153.0 1.5 copy-done.1
  154.5 7.8 %factor.3.refs_4_ = f32[576,1024]{1,0:T(8,128)S(1)} custom-call(s32[1]{0:T(128)} %bitcast.6.refs_0_.core_ref, bf16[2,576,768]{2,1,0:T(8,128)(2,1)} %bitcast.17.refs_1_, bf16[2,576,768]{2,1,0:T(8,128)(2,1)S(1)} %copy-done.1, bf16[3072,1024]{1,0:T(8,128)(2,1)} %bitcast.63), custom_call_target="tpu_custom_call" | custom-call | flops 1000 | bytes 1000 | tf_op jit(solution)/shard_map/factor/pallas_call | solution.py:92
  162.3 15.4 %all-to-all-done.3 = bf16[16,72,768]{2,1,0:T(8,128)(2,1)} async-done(((bf16[16,72,768]{2,1,0:T(8,128)(2,1)}), bf16[16,72,768]{2,1,0:T(8,128)(2,1)}, u32[]{:S(2)}, u32[]{:S(2)}) %all-to-all-start.3) | async-done | bytes 1769504 | tf_op jit(solution)/shard_map/all_to_all | solution.py:364
  177.7 0.0 collective-permute-start.4
  177.7 3.9 %collective-permute-done.4.refs_2_ = bf16[2,576,768]{2,1,0:T(8,128)(2,1)S(1)} collective-permute-done((bf16[2,576,768]{2,1,0:T(8,128)(2,1)}, bf16[2,576,768]{2,1,0:T(8,128)(2,1)S(1)}, u32[]{:S(2)}, u32[]{:S(2)}) %collective-permute-start.4) | collective-permute-done | bytes 1769504 | tf_op jit(solution)/shard_map/ppermute | solution.py:361
  181.6 9.7 %sent_part.3 = (bf16[576,1024]{1,0:T(8,128)(2,1)S(1)}, bf16[2,576,768]{2,1,0:T(8,128)(2,1)S(1)}) custom-call(s32[1]{0:T(128)} %bitcast.6.refs_0_.core_ref, bf16[2,576,768]{2,1,0:T(8,128)(2,1)} %bitcast.28.refs_1_, bf16[2,576,768]{2,1,0:T(8,128)(2,1)S(1)} %collective-permute-done.4.refs_2_, bf16[1024,3072]{1,0:T(8,128)(2,1)} %bitcast.67, ...), custom_call_target="tpu_custom_call" | custom-call | flops 1000 | bytes 1000 | tf_op jit(solution)/shard_map/sent_part/pallas_call | solution.py:92
  191.3 0.4 collective-permute-start.5
  191.7 3.7 %kept_part.3 = bf16[2,576,768]{2,1,0:T(8,128)(2,1)S(1)} custom-call(s32[1]{0:T(128)} %bitcast.6.refs_0_.core_ref, bf16[576,1024]{1,0:T(8,128)(2,1)S(1)} %get-tuple-element.29.grad_pre_ref, bf16[3072,1024]{1,0:T(8,128)(2,1)} %bitcast.65), custom_call_target="tpu_custom_call" | custom-call | flops 1811939328 | bytes 4325376 | tf_op jit(solution)/shard_map/kept_part/pallas_call | solution.py:239
  195.4 0.0 collective-permute-done.5
  195.4 1.7 add_convert_fusion
  197.1 6.5 %all-to-all-start.4 = ((bf16[16,72,768]{2,1,0:T(8,128)(2,1)}), bf16[16,72,768]{2,1,0:T(8,128)(2,1)S(1)}, u32[]{:S(2)}, u32[]{:S(2)}) async-start(bf16[16,72,768]{2,1,0:T(8,128)(2,1)} %bitcast.29), calls=%async_computation.4 | async-start | bytes 3538944 | tf_op jit(solution)/shard_map/all_to_all | solution.py:364
  203.6 0.0 copy-start.6
  203.7 0.1 fusion.2
  203.8 25.8 %all-to-all-done.4 = bf16[16,72,768]{2,1,0:T(8,128)(2,1)S(1)} async-done(((bf16[16,72,768]{2,1,0:T(8,128)(2,1)}), bf16[16,72,768]{2,1,0:T(8,128)(2,1)S(1)}, u32[]{:S(2)}, u32[]{:S(2)}) %all-to-all-start.4) | async-done | bytes 1769504 | tf_op jit(solution)/shard_map/all_to_all | solution.py:364
  229.7 0.2 convert_reduce_fusion
  229.9 0.0 copy-done.6
  229.9 0.8 add_convert_fusion.2
  230.8 3.8 %collective-permute-start.6 = (bf16[128,768]{1,0:T(8,128)(2,1)S(1)}, bf16[128,768]{1,0:T(8,128)(2,1)S(1)}, u32[]{:S(2)}, u32[]{:S(2)}) collective-permute-start(bf16[128,768]{1,0:T(8,128)(2,1)S(1)} %add_convert_fusion.2), channel_id=1, source_target_pairs={{0,224},{32,0},{64,32},{96,64},{128,96},{160,128},{192,160},{224,1... | collective-permute-start | bytes 589832 | tf_op jit(solution)/shard_map/ppermute | solution.py:382
  234.6 3.2 %collective-permute-done.6 = bf16[128,768]{1,0:T(8,128)(2,1)S(1)} collective-permute-done((bf16[128,768]{1,0:T(8,128)(2,1)S(1)}, bf16[128,768]{1,0:T(8,128)(2,1)S(1)}, u32[]{:S(2)}, u32[]{:S(2)}) %collective-permute-start.6) | collective-permute-done | bytes 196640 | tf_op jit(solution)/shard_map/ppermute | solution.py:382
  237.8 0.7 copy.9
  (6 shorter events, 0.1 us)
Async XLA Ops:
  3.9 53.2 %all-to-all-start = ((bf16[16,72,1536]{2,1,0:T(8,128)(2,1)}), bf16[16,72,1536]{2,1,0:T(8,128)(2,1)S(1)}, u32[]{:S(2)}, u32[]{:S(2)}) async-start(bf16[16,72,1536]{2,1,0:T(8,128)(2,1)} %bitcast.68), calls=%async_computation | async-start | bytes 7077888 | tf_op jit(solution)/shard_map/all_to_all | solution.py:364
  57.1 11.9 %collective-permute-start = (bf16[2,576,1536]{2,1,0:T(8,128)(2,1)S(1)}, bf16[2,576,1536]{2,1,0:T(8,128)(2,1)}, u32[]{:S(2)}, u32[]{:S(2)}) collective-permute-start(bf16[2,576,1536]{2,1,0:T(8,128)(2,1)S(1)} %bitcast.57), channel_id=1, source_target_pairs={{0,1},{1,0},{2,3},{3,2},{4,5},{5,4},{6,7},{7,6},{8,9},{9,8},{10,11... | collective-permute-start | bytes 10616840 | tf_op jit(solution)/shard_map/ppermute | solution.py:361
  57.1 37.9 %all-to-all-start.1 = ((bf16[16,72,768]{2,1,0:T(8,128)(2,1)}), bf16[16,72,768]{2,1,0:T(8,128)(2,1)}, u32[]{:S(2)}, u32[]{:S(2)}) async-start(bf16[16,72,768]{2,1,0:T(8,128)(2,1)} %bitcast.71), calls=%async_computation.1 | async-start | bytes 3538944 | tf_op jit(solution)/shard_map/all_to_all | solution.py:364
  86.4 1.2 copy-start.2
  87.7 7.4 %copy-start.3 = (bf16[2,576,768]{2,1,0:T(8,128)(2,1)S(1)}, bf16[2,576,768]{2,1,0:T(8,128)(2,1)}, u32[]{:S(2)}) copy-start(bf16[2,576,768]{2,1,0:T(8,128)(2,1)} %copy-done.2) | copy-start | bytes 5308420
  95.0 3.7 %collective-permute-start.1 = (bf16[2,576,768]{2,1,0:T(8,128)(2,1)S(1)}, bf16[2,576,768]{2,1,0:T(8,128)(2,1)S(1)}, u32[]{:S(2)}, u32[]{:S(2)}) collective-permute-start(bf16[2,576,768]{2,1,0:T(8,128)(2,1)S(1)} %copy-done.3), channel_id=1, source_target_pairs={{0,1},{1,0},{2,3},{3,2},{4,5},{5,4},{6,7},{7,6},{8,9},{9,8},{10,11... | collective-permute-start | bytes 5308424 | tf_op jit(solution)/shard_map/ppermute | solution.py:361
  100.4 6.0 %copy-start.8 = (s32[1,2]{1,0:T(1,128)S(1)}, s32[1,2]{1,0:T(1,128)}, u32[]{:S(2)}) copy-start(s32[1,2]{1,0:T(1,128)} %param.11) | copy-start | bytes 28
  100.4 10.4 %copy-start.7 = (s32[1,2,128,2]{2,3,1,0:T(2,128)S(1)}, s32[1,2,128,2]{2,3,1,0:T(2,128)}, u32[]{:S(2)}) copy-start(s32[1,2,128,2]{2,3,1,0:T(2,128)} %param.9) | copy-start | bytes 6148
  100.4 10.4 %copy-start.9 = (f32[1,2,128,2]{2,3,1,0:T(2,128)S(1)}, f32[1,2,128,2]{2,3,1,0:T(2,128)}, u32[]{:S(2)}) copy-start(f32[1,2,128,2]{2,3,1,0:T(2,128)} %param.10) | copy-start | bytes 6148
  100.4 31.4 %all-to-all-start.2 = ((bf16[16,72,768]{2,1,0:T(8,128)(2,1)}), bf16[16,72,768]{2,1,0:T(8,128)(2,1)S(1)}, u32[]{:S(2)}, u32[]{:S(2)}) async-start(bf16[16,72,768]{2,1,0:T(8,128)(2,1)} %bitcast.18), calls=%async_computation.2 | async-start | bytes 3538944 | tf_op jit(solution)/shard_map/all_to_all | solution.py:364
  106.4 25.7 %copy-start.4 = (bf16[1,128,768]{2,1,0:T(8,128)(2,1)S(1)}, bf16[1,128,768]{2,1,0:T(8,128)(2,1)}, u32[]{:S(2)}) copy-start(bf16[1,128,768]{2,1,0:T(8,128)(2,1)} %refs_1_.1) | copy-start | bytes 589828
  133.0 9.1 %collective-permute-start.2 = (bf16[128,768]{1,0:T(8,128)(2,1)S(1)}, bf16[128,768]{1,0:T(8,128)(2,1)S(1)}, u32[]{:S(2)}, u32[]{:S(2)}) collective-permute-start(bf16[128,768]{1,0:T(8,128)(2,1)S(1)} %fusion.1), channel_id=1, source_target_pairs={{0,224},{32,0},{64,32},{96,64},{128,96},{160,128},{192,160},{224,1... | collective-permute-start | bytes 589832 | tf_op jit(solution)/shard_map/ppermute | solution.py:382
  142.1 0.7 copy-start.5
  146.0 5.7 %collective-permute-start.3 = (bf16[2,576,768]{2,1,0:T(8,128)(2,1)}, bf16[2,576,768]{2,1,0:T(8,128)(2,1)S(1)}, u32[]{:S(2)}, u32[]{:S(2)}) collective-permute-start(bf16[2,576,768]{2,1,0:T(8,128)(2,1)} %bitcast.17.refs_1_), channel_id=1, source_target_pairs={{0,1},{1,0},{2,3},{3,2},{4,5},{5,4},{6,7},{7,6},{8,9},{9,8},{10,11... | collective-permute-start | bytes 5308424 | tf_op jit(solution)/shard_map/ppermute | solution.py:361
  146.1 31.6 %all-to-all-start.3 = ((bf16[16,72,768]{2,1,0:T(8,128)(2,1)}), bf16[16,72,768]{2,1,0:T(8,128)(2,1)}, u32[]{:S(2)}, u32[]{:S(2)}) async-start(bf16[16,72,768]{2,1,0:T(8,128)(2,1)} %bitcast.69), calls=%async_computation.3 | async-start | bytes 3538944 | tf_op jit(solution)/shard_map/all_to_all | solution.py:364
  151.8 1.3 copy-start
  153.0 1.5 copy-start.1
  177.7 3.9 %collective-permute-start.4 = (bf16[2,576,768]{2,1,0:T(8,128)(2,1)}, bf16[2,576,768]{2,1,0:T(8,128)(2,1)S(1)}, u32[]{:S(2)}, u32[]{:S(2)}) collective-permute-start(bf16[2,576,768]{2,1,0:T(8,128)(2,1)} %bitcast.28.refs_1_), channel_id=1, source_target_pairs={{0,1},{1,0},{2,3},{3,2},{4,5},{5,4},{6,7},{7,6},{8,9},{9,8},{10,11... | collective-permute-start | bytes 5308424 | tf_op jit(solution)/shard_map/ppermute | solution.py:361
  191.3 4.1 %collective-permute-start.5 = (bf16[2,576,768]{2,1,0:T(8,128)(2,1)S(1)}, bf16[2,576,768]{2,1,0:T(8,128)(2,1)S(1)}, u32[]{:S(2)}, u32[]{:S(2)}) collective-permute-start(bf16[2,576,768]{2,1,0:T(8,128)(2,1)S(1)} %get-tuple-element.30), channel_id=1, source_target_pairs={{0,1},{1,0},{2,3},{3,2},{4,5},{5,4},{6,7},{7,6},{8,9},{9,8},{10,11... | collective-permute-start | bytes 5308424 | tf_op jit(solution)/shard_map/ppermute | solution.py:361
  197.1 32.5 %all-to-all-start.4 = ((bf16[16,72,768]{2,1,0:T(8,128)(2,1)}), bf16[16,72,768]{2,1,0:T(8,128)(2,1)S(1)}, u32[]{:S(2)}, u32[]{:S(2)}) async-start(bf16[16,72,768]{2,1,0:T(8,128)(2,1)} %bitcast.29), calls=%async_computation.4 | async-start | bytes 3538944 | tf_op jit(solution)/shard_map/all_to_all | solution.py:364
  203.6 26.3 %copy-start.6 = (bf16[128,768]{1,0:T(8,128)(2,1)S(1)}, bf16[128,768]{1,0:T(8,128)(2,1)}, u32[]{:S(2)}) copy-start(bf16[128,768]{1,0:T(8,128)(2,1)} %copy-done.5) | copy-start | bytes 589828
  230.8 7.0 %collective-permute-start.6 = (bf16[128,768]{1,0:T(8,128)(2,1)S(1)}, bf16[128,768]{1,0:T(8,128)(2,1)S(1)}, u32[]{:S(2)}, u32[]{:S(2)}) collective-permute-start(bf16[128,768]{1,0:T(8,128)(2,1)S(1)} %add_convert_fusion.2), channel_id=1, source_target_pairs={{0,224},{32,0},{64,32},{96,64},{128,96},{160,128},{192,160},{224,1... | collective-permute-start | bytes 589832 | tf_op jit(solution)/shard_map/ppermute | solution.py:382

commit v5 on v4

--- a/solution.py
+++ b/solution.py
@@ -127,14 +127,15 @@
 
 def sent_kernel(
     column,
+    complete,
     core_ref,
     mine,
     other,
     down,
     factors,
     up,
-    grad_pre_out,
-    send_out,
+    first_out,
+    second_out,
     rows_buf,
     down_buf,
     acc,
@@ -146,18 +147,21 @@
     late_semaphores,
 ):
     core = core_ref[0]
-    halves, _, quarter = send.shape
+    halves = mine.shape[0]
+    results, _, quarter = send.shape
     copies = quarter_copies(
         core, mine, other, column, down, False, rows_buf, down_buf, semaphores
     )
+    firsts = [
+        pl.multiple_of((2 * (n % halves) + (1 - core if n < halves else core)) * quarter, quarter)
+        for n in range(results)
+    ]
     factor_copy = pltpu.make_async_copy(factors, factor_buf, late_semaphores.at[0])
     up_copies = [
         pltpu.make_async_copy(
-            up.at[pl.ds(pl.multiple_of((2 * half + 1 - core) * quarter, quarter), quarter), :],
-            up_buf.at[half],
-            late_semaphores.at[1 + half],
-        )
-        for half in range(halves)
+            up.at[pl.ds(firsts[n], quarter), :], up_buf.at[n], late_semaphores.at[1 + n]
+        )
+        for n in range(results)
     ]
     for pair in copies:
         for copy in pair:
@@ -180,14 +184,19 @@
                 acc[:, block] = part
             else:
                 grad_pre[:, block] = (part * factor_buf[:, block]).astype(jnp.bfloat16)
-    sent = [pltpu.make_async_copy(grad_pre, grad_pre_out, late_semaphores.at[1 + halves])]
-    sent[0].start()
-    for half in range(halves):
-        up_copies[half].wait()
-        send[half] = contract_last(grad_pre[...], up_buf[half]).astype(jnp.bfloat16)
+    sent = []
+    if not complete:
+        sent.append(
+            pltpu.make_async_copy(grad_pre, first_out, late_semaphores.at[1 + 2 * results])
+        )
+        sent[-1].start()
+    for n in range(results):
+        up_copies[n].wait()
+        send[n] = contract_last(grad_pre[...], up_buf[n]).astype(jnp.bfloat16)
+        target = first_out if complete and n < halves else second_out
         sent.append(
             pltpu.make_async_copy(
-                send.at[half], send_out.at[half], late_semaphores.at[2 + halves + half]
+                send.at[n], target.at[n % halves], late_semaphores.at[1 + results + n]
             )
         )
         sent[-1].start()
@@ -195,29 +204,32 @@
         copy.wait()
 
 
-def sent_part(core, grads, down, factors, up):
+def sent_part(core, grads, down, factors, up, complete):
     mine, other, column = grads
     halves, rows = mine.shape[:2]
     hidden, width = down.shape
     pieces = 2 * halves
     quarter = width // pieces
+    results = pieces if complete else halves
+    part = jax.ShapeDtypeStruct((halves, rows, quarter), jnp.bfloat16)
+    if complete:
+        kept = pltpu.HBM((halves, rows, quarter), jnp.bfloat16)
+    else:
+        kept = jax.ShapeDtypeStruct((rows, hidden), jnp.bfloat16)
     return own_copies(
-        lambda *refs: sent_kernel(column, *refs),
-        "sent_part",
-        (
-            jax.ShapeDtypeStruct((rows, hidden), jnp.bfloat16),
-            jax.ShapeDtypeStruct((halves, rows, quarter), jnp.bfloat16),
-        ),
+        lambda *refs: sent_kernel(column, complete, *refs),
+        "branch" if complete else "sent_part",
+        (part, kept) if complete else (kept, part),
         [
             pltpu.VMEM((pieces, rows, quarter), jnp.bfloat16),
             pltpu.VMEM((pieces, hidden, quarter), jnp.bfloat16),
             pltpu.VMEM((rows, hidden), jnp.float32),
             pltpu.VMEM((rows, hidden), jnp.float32),
-            pltpu.VMEM((halves, quarter, hidden), jnp.bfloat16),
+            pltpu.VMEM((results, quarter, hidden), jnp.bfloat16),
             pltpu.VMEM((rows, hidden), jnp.bfloat16),
-            pltpu.VMEM((halves, rows, quarter), jnp.bfloat16),
+            pltpu.VMEM((results, rows, quarter), jnp.bfloat16),
             pltpu.SemaphoreType.DMA((2 * pieces,)),
-            pltpu.SemaphoreType.DMA((2 + 2 * halves,)),
+            pltpu.SemaphoreType.DMA((2 + 2 * results,)),
         ],
         core,
         mine,
@@ -330,6 +342,21 @@
     return out.reshape(n_xhi * EXPERTS * per_expert, CAPACITY, width)
 
 
+def landed(value):
+    anywhere = pl.BlockSpec(memory_space=pltpu.HBM)
+    return pl.pallas_call(
+        lambda value_ref, same_ref: None,
+        out_shape=jax.ShapeDtypeStruct(value.shape, value.dtype),
+        in_specs=[anywhere],
+        out_specs=anywhere,
+        input_output_aliases={0: 0},
+        cost_estimate=pl.CostEstimate(
+            flops=10**11, transcendentals=0, bytes_accessed=10**8
+        ),
+        name="landed",
+    )(value)
+
+
 def slots(route_now, share_now):
     rows = route_now.shape[0]
     named = route_now.T[None] == jnp.arange(EXPERTS, dtype=jnp.int32)[:, None, None]
@@ -419,13 +446,17 @@
             factors = factor(core, (later, swap_cores(later), 0), up_local)
             grad_rows, factors = together(grad_rows, factors)
             grads = (grad_rows, swap_cores(grad_rows), 0)
-        grad_pre, send = sent_part(core, grads, down_local, factors, up_local)
-        keep = kept_part(core, grad_pre, up_local)
+        complete = tick + 1 < ticks
+        made = sent_part(core, grads, down_local, factors, up_local, complete)
+        if complete:
+            send, keep = made
+        else:
+            grad_pre, send = made
+            keep = kept_part(core, grad_pre, up_local)
+        got = swap_cores(send)
         if tick + 1 < ticks:
-            send, later, keep = together(send, later, keep)
-        partial_rows = (
-            keep.astype(jnp.float32) + swap_cores(send).astype(jnp.float32)
-        ).astype(jnp.bfloat16)
+            keep, later = together(keep, landed(later))
+        partial_rows = (keep.astype(jnp.float32) + got.astype(jnp.float32)).astype(jnp.bfloat16)
         arrived = exchange(partial_rows.reshape(peers, CAPACITY, quarter))
         current = combine(current, mixing_of(tick), arrived)
     return current[None]

time: 239 us -> 235 us (0.983)
  waiting for transfers between devices: 122 us -> 119 us
    pallas_call x2 -> x1, Pallas kernels: 7.48 us -> 3.67 us  [kept_part(): pl.pallas_call(kept_kernel, out_shape=jax.ShapeDtypeStruct((halves, rows,...]
    ppermute x5, waiting for transfers between devices: 7.6 us -> 3.91 us  [swap_cores(): return lax.ppermute(value, 'core', [(0, 1), (1, 0)])]
    pallas_call x4, Pallas kernels: 34.9 us -> 38.1 us  [own_copies(): pl.pallas_call(kernel, out_shape=out, in_specs=[pl.BlockSpec(memory_space...]
    unnamed x21 -> x19, local copies, waits for them, and re-layouts: 5.33 us -> 5.53 us
  transfers between devices with their start and end apart: 12 -> 12, of which waited for: 9 -> 8; matrix products, arithmetic and copies ran while one was open for 0% -> 0% of each run, Pallas kernels for 15% -> 15%
where the time goes in v5:
time: 235 us
  waiting for transfers between devices  119 us (51%)
  Pallas kernels  52.2 us (22%)
  starting transfers between devices  47.9 us (20%)
  local copies, waits for them, and re-layouts  6.13 us (3%)
  between operations  3.99 us (2%)
  other arithmetic  3.87 us (2%)
    all_to_all x5, waiting for transfers between devices, exchange(): lax.all_to_all(value, ('xhi', 'expert'), split_axis=0, concat_axis=0, til...  108 us
    pallas_call x4, Pallas kernels, own_copies(): pl.pallas_call(kernel, out_shape=out, in_specs=[pl.BlockSpec(memory_space...  38.1 us
    all_to_all x5, starting transfers between devices, exchange(): lax.all_to_all(value, ('xhi', 'expert'), split_axis=0, concat_axis=0, til...  37.4 us
    pallas_call x3, Pallas kernels, pick(): pl.pallas_call(pick_kernel, out_shape=jax.ShapeDtypeStruct((n_xhi, EXPERT...  10.5 us
    ppermute x2, starting transfers between devices, combine(): lax.ppermute(result, 'section', [(i, (i - 1) % n_section) for i in range(...  9.7 us
    ppermute x2, waiting for transfers between devices, combine(): lax.ppermute(result, 'section', [(i, (i - 1) % n_section) for i in range(...  6.38 us
    unnamed x19, local copies, waits for them, and re-layouts  5.53 us
  transfers between devices with their start and end apart: 12, of which 8 were waited for; matrix products, arithmetic and copies ran while one was open for 0% of the time, Pallas kernels for 15%

profile of v5, /device:TPU:8, one launch (start us, length us, event | category | flops | bytes accessed | tf_op | source)
XLA Modules:
  0.0 234.6 jit_solution(4756094983969406042)
XLA Ops:
  0.0 3.9 %pick.4 = bf16[2,4,2,72,1536]{4,3,2,1,0:T(8,128)(2,1)} custom-call(s32[2]{0:T(128)} %bitcast.79, s32[2,2,128]{2,1,0:T(2,128)} %bitcast.76, bf16[2,128,768]{2,1,0:T(8,128)(2,1)} %bitcast.72, bf16[1,128,768]{2,1,0:T(8,128)(2,1)} %refs_1_.1), custom_call_target="tpu_custom_call" | custom-call | tf_op jit(solution)/shard_map/pick/pallas_call | solution.py:324
  4.0 7.4 %all-to-all-start = ((bf16[16,72,1536]{2,1,0:T(8,128)(2,1)}), bf16[16,72,1536]{2,1,0:T(8,128)(2,1)S(1)}, u32[]{:S(2)}, u32[]{:S(2)}) async-start(bf16[16,72,1536]{2,1,0:T(8,128)(2,1)} %bitcast.67), calls=%async_computation | async-start | bytes 7077888 | tf_op jit(solution)/shard_map/all_to_all | solution.py:391
  11.4 3.3 %pick.3 = bf16[2,4,2,72,768]{4,3,2,1,0:T(8,128)(2,1)} custom-call(s32[2]{0:T(128)} %bitcast.80, s32[2,2,128]{2,1,0:T(2,128)} %bitcast.77, bf16[2,128,768]{2,1,0:T(8,128)(2,1)} %bitcast.73), custom_call_target="tpu_custom_call" | custom-call | tf_op jit(solution)/shard_map/pick/pallas_call | solution.py:324
  14.6 42.5 %all-to-all-done = bf16[16,72,1536]{2,1,0:T(8,128)(2,1)S(1)} async-done(((bf16[16,72,1536]{2,1,0:T(8,128)(2,1)}), bf16[16,72,1536]{2,1,0:T(8,128)(2,1)S(1)}, u32[]{:S(2)}, u32[]{:S(2)}) %all-to-all-start) | async-done | bytes 3538976 | tf_op jit(solution)/shard_map/all_to_all | solution.py:391
  57.1 0.0 collective-permute-start
  57.1 11.9 %all-to-all-start.1 = ((bf16[16,72,768]{2,1,0:T(8,128)(2,1)}), bf16[16,72,768]{2,1,0:T(8,128)(2,1)}, u32[]{:S(2)}, u32[]{:S(2)}) async-start(bf16[16,72,768]{2,1,0:T(8,128)(2,1)} %bitcast.70), calls=%async_computation.1 | async-start | bytes 3538944 | tf_op jit(solution)/shard_map/all_to_all | solution.py:391
  69.0 0.0 collective-permute-done.refs_2_
  69.0 7.9 %factor.2.refs_4_ = f32[576,1024]{1,0:T(8,128)S(1)} custom-call(s32[1]{0:T(128)} %bitcast.6.refs_0_.core_ref, bf16[2,576,1536]{2,1,0:T(8,128)(2,1)S(1)} %bitcast.58, bf16[2,576,1536]{2,1,0:T(8,128)(2,1)} %collective-permute-done.refs_2_, bf16[3072,1024]{1,0:T(8,128)(2,1)} %bitcast.60), custom_call_target="tpu_custom_call" | custom-call | flops 1000 | bytes 1000 | tf_op jit(solution)/shard_map/factor/pallas_call | solution.py:92
  76.9 12.7 %branch.1 = (bf16[2,576,768]{2,1,0:T(8,128)(2,1)}, bf16[2,576,768]{2,1,0:T(8,128)(2,1)}) custom-call(s32[1]{0:T(128)} %bitcast.6.refs_0_.core_ref, bf16[2,576,1536]{2,1,0:T(8,128)(2,1)S(1)} %bitcast.59, bf16[2,576,1536]{2,1,0:T(8,128)(2,1)} %collective-permute-done.refs_2_, bf16[1024,3072]{1,0:T(8,128)(2,1)} %bitcast.65, f32[576,1024]{1,0:T(8,128)S(1)} %factor.2.refs_4_, ...), custom_call_target="tpu_custom_call" | custom-call | flops 1000 | bytes 1000 | tf_op jit(solution)/shard_map/branch/pallas_call | solution.py:92
  89.6 0.3 collective-permute-start.1
  89.9 5.2 %all-to-all-done.1 = bf16[16,72,768]{2,1,0:T(8,128)(2,1)} async-done(((bf16[16,72,768]{2,1,0:T(8,128)(2,1)}), bf16[16,72,768]{2,1,0:T(8,128)(2,1)}, u32[]{:S(2)}, u32[]{:S(2)}) %all-to-all-start.1) | async-done | bytes 1769504 | tf_op jit(solution)/shard_map/all_to_all | solution.py:391
  95.0 0.0 copy-start.2
  95.0 0.0 collective-permute-done.1
  95.1 1.5 copy-done.2
  96.5 1.6 add_convert_fusion.1
  98.2 0.0 copy-start.7
  98.2 0.0 copy-start.6
  98.2 0.0 copy-start.8
  98.2 6.0 %all-to-all-start.2 = ((bf16[16,72,768]{2,1,0:T(8,128)(2,1)}), bf16[16,72,768]{2,1,0:T(8,128)(2,1)S(1)}, u32[]{:S(2)}, u32[]{:S(2)}) async-start(bf16[16,72,768]{2,1,0:T(8,128)(2,1)} %bitcast.18), calls=%async_computation.2 | async-start | bytes 3538944 | tf_op jit(solution)/shard_map/all_to_all | solution.py:391
  104.1 0.0 copy-done.7
  104.1 0.0 copy-start.3
  104.2 0.6 fusion.18
  108.5 0.0 copy-done.6
  108.5 0.0 copy-done.8
  108.6 0.1 fusion.3
  108.7 19.4 %all-to-all-done.2 = bf16[16,72,768]{2,1,0:T(8,128)(2,1)S(1)} async-done(((bf16[16,72,768]{2,1,0:T(8,128)(2,1)}), bf16[16,72,768]{2,1,0:T(8,128)(2,1)S(1)}, u32[]{:S(2)}, u32[]{:S(2)}) %all-to-all-start.2) | async-done | bytes 1769504 | tf_op jit(solution)/shard_map/all_to_all | solution.py:391
  128.1 0.2 convert_reduce_fusion.1
  128.3 0.0 copy-done.3
  128.3 0.8 fusion.1
  129.2 5.9 %collective-permute-start.2 = (bf16[128,768]{1,0:T(8,128)(2,1)S(1)}, bf16[128,768]{1,0:T(8,128)(2,1)S(1)}, u32[]{:S(2)}, u32[]{:S(2)}) collective-permute-start(bf16[128,768]{1,0:T(8,128)(2,1)S(1)} %fusion.1), channel_id=1, source_target_pairs={{0,224},{32,0},{64,32},{96,64},{128,96},{160,128},{192,160},{224,1... | collective-permute-start | bytes 589832 | tf_op jit(solution)/shard_map/ppermute | solution.py:409
  135.1 3.2 %collective-permute-done.2 = bf16[128,768]{1,0:T(8,128)(2,1)S(1)} collective-permute-done((bf16[128,768]{1,0:T(8,128)(2,1)S(1)}, bf16[128,768]{1,0:T(8,128)(2,1)S(1)}, u32[]{:S(2)}, u32[]{:S(2)}) %collective-permute-start.2) | collective-permute-done | bytes 196640 | tf_op jit(solution)/shard_map/ppermute | solution.py:409
  138.3 0.0 copy-start.4
  138.3 0.7 copy-done.4
  139.0 3.2 %pick.5 = bf16[2,4,2,72,768]{4,3,2,1,0:T(8,128)(2,1)} custom-call(s32[2]{0:T(128)} %bitcast.81, s32[2,2,128]{2,1,0:T(2,128)} %bitcast.78, bf16[1,128,768]{2,1,0:T(8,128)(2,1)} %bitcast.74), custom_call_target="tpu_custom_call" | custom-call | tf_op jit(solution)/shard_map/pick/pallas_call | solution.py:324
  142.3 0.1 collective-permute-start.3
  142.4 5.6 %all-to-all-start.3 = ((bf16[16,72,768]{2,1,0:T(8,128)(2,1)}), bf16[16,72,768]{2,1,0:T(8,128)(2,1)}, u32[]{:S(2)}, u32[]{:S(2)}) async-start(bf16[16,72,768]{2,1,0:T(8,128)(2,1)} %bitcast.68), calls=%async_computation.3 | async-start | bytes 3538944 | tf_op jit(solution)/shard_map/all_to_all | solution.py:391
  148.0 0.0 collective-permute-done.3.refs_2_
  148.0 0.0 copy-start
  148.0 1.2 copy-done
  149.2 0.0 copy-start.1
  149.2 1.5 copy-done.1
  150.7 7.8 %factor.3.refs_4_ = f32[576,1024]{1,0:T(8,128)S(1)} custom-call(s32[1]{0:T(128)} %bitcast.6.refs_0_.core_ref, bf16[2,576,768]{2,1,0:T(8,128)(2,1)} %landed.1.refs_1_, bf16[2,576,768]{2,1,0:T(8,128)(2,1)S(1)} %copy-done.1, bf16[3072,1024]{1,0:T(8,128)(2,1)} %bitcast.62), custom_call_target="tpu_custom_call" | custom-call | flops 1000 | bytes 1000 | tf_op jit(solution)/shard_map/factor/pallas_call | solution.py:92
  158.5 15.4 %all-to-all-done.3 = bf16[16,72,768]{2,1,0:T(8,128)(2,1)} async-done(((bf16[16,72,768]{2,1,0:T(8,128)(2,1)}), bf16[16,72,768]{2,1,0:T(8,128)(2,1)}, u32[]{:S(2)}, u32[]{:S(2)}) %all-to-all-start.3) | async-done | bytes 1769504 | tf_op jit(solution)/shard_map/all_to_all | solution.py:391
  173.9 0.0 collective-permute-start.4
  173.9 3.9 %collective-permute-done.4.refs_2_ = bf16[2,576,768]{2,1,0:T(8,128)(2,1)S(1)} collective-permute-done((bf16[2,576,768]{2,1,0:T(8,128)(2,1)}, bf16[2,576,768]{2,1,0:T(8,128)(2,1)S(1)}, u32[]{:S(2)}, u32[]{:S(2)}) %collective-permute-start.4) | collective-permute-done | bytes 1769504 | tf_op jit(solution)/shard_map/ppermute | solution.py:388
  177.8 9.7 %sent_part.1 = (bf16[576,1024]{1,0:T(8,128)(2,1)S(1)}, bf16[2,576,768]{2,1,0:T(8,128)(2,1)S(1)}) custom-call(s32[1]{0:T(128)} %bitcast.6.refs_0_.core_ref, bf16[2,576,768]{2,1,0:T(8,128)(2,1)} %bitcast.28.refs_1_, bf16[2,576,768]{2,1,0:T(8,128)(2,1)S(1)} %collective-permute-done.4.refs_2_, bf16[1024,3072]{1,0:T(8,128)(2,1)} %bitcast.66, ...), custom_call_target="tpu_custom_call" | custom-call | flops 1000 | bytes 1000 | tf_op jit(solution)/shard_map/sent_part/pallas_call | solution.py:92
  187.5 0.4 collective-permute-start.5
  188.0 3.7 %kept_part.1 = bf16[2,576,768]{2,1,0:T(8,128)(2,1)S(1)} custom-call(s32[1]{0:T(128)} %bitcast.6.refs_0_.core_ref, bf16[576,1024]{1,0:T(8,128)(2,1)S(1)} %get-tuple-element.27.grad_pre_ref, bf16[3072,1024]{1,0:T(8,128)(2,1)} %bitcast.64), custom_call_target="tpu_custom_call" | custom-call | flops 1811939328 | bytes 4325376 | tf_op jit(solution)/shard_map/kept_part/pallas_call | solution.py:251
  191.7 0.0 collective-permute-done.5
  191.7 1.7 add_convert_fusion
  193.4 6.5 %all-to-all-start.4 = ((bf16[16,72,768]{2,1,0:T(8,128)(2,1)}), bf16[16,72,768]{2,1,0:T(8,128)(2,1)S(1)}, u32[]{:S(2)}, u32[]{:S(2)}) async-start(bf16[16,72,768]{2,1,0:T(8,128)(2,1)} %bitcast.29), calls=%async_computation.4 | async-start | bytes 3538944 | tf_op jit(solution)/shard_map/all_to_all | solution.py:391
  199.9 0.0 copy-start.5
  199.9 0.1 fusion.2
  200.0 25.8 %all-to-all-done.4 = bf16[16,72,768]{2,1,0:T(8,128)(2,1)S(1)} async-done(((bf16[16,72,768]{2,1,0:T(8,128)(2,1)}), bf16[16,72,768]{2,1,0:T(8,128)(2,1)S(1)}, u32[]{:S(2)}, u32[]{:S(2)}) %all-to-all-start.4) | async-done | bytes 1769504 | tf_op jit(solution)/shard_map/all_to_all | solution.py:391
  225.9 0.2 convert_reduce_fusion
  226.1 0.0 copy-done.5
  226.1 0.8 add_convert_fusion.2
  227.0 3.8 %collective-permute-start.6 = (bf16[128,768]{1,0:T(8,128)(2,1)S(1)}, bf16[128,768]{1,0:T(8,128)(2,1)S(1)}, u32[]{:S(2)}, u32[]{:S(2)}) collective-permute-start(bf16[128,768]{1,0:T(8,128)(2,1)S(1)} %add_convert_fusion.2), channel_id=1, source_target_pairs={{0,224},{32,0},{64,32},{96,64},{128,96},{160,128},{192,160},{224,1... | collective-permute-start | bytes 589832 | tf_op jit(solution)/shard_map/ppermute | solution.py:409
  230.8 3.2 %collective-permute-done.6 = bf16[128,768]{1,0:T(8,128)(2,1)S(1)} collective-permute-done((bf16[128,768]{1,0:T(8,128)(2,1)S(1)}, bf16[128,768]{1,0:T(8,128)(2,1)S(1)}, u32[]{:S(2)}, u32[]{:S(2)}) %collective-permute-start.6) | collective-permute-done | bytes 196640 | tf_op jit(solution)/shard_map/ppermute | solution.py:409
  233.9 0.7 copy.11
  (7 shorter events, 0.1 us)
Async XLA Ops:
  4.0 53.2 %all-to-all-start = ((bf16[16,72,1536]{2,1,0:T(8,128)(2,1)}), bf16[16,72,1536]{2,1,0:T(8,128)(2,1)S(1)}, u32[]{:S(2)}, u32[]{:S(2)}) async-start(bf16[16,72,1536]{2,1,0:T(8,128)(2,1)} %bitcast.67), calls=%async_computation | async-start | bytes 7077888 | tf_op jit(solution)/shard_map/all_to_all | solution.py:391
  57.1 11.9 %collective-permute-start = (bf16[2,576,1536]{2,1,0:T(8,128)(2,1)S(1)}, bf16[2,576,1536]{2,1,0:T(8,128)(2,1)}, u32[]{:S(2)}, u32[]{:S(2)}) collective-permute-start(bf16[2,576,1536]{2,1,0:T(8,128)(2,1)S(1)} %bitcast.57), channel_id=1, source_target_pairs={{0,1},{1,0},{2,3},{3,2},{4,5},{5,4},{6,7},{7,6},{8,9},{9,8},{10,11... | collective-permute-start | bytes 10616840 | tf_op jit(solution)/shard_map/ppermute | solution.py:388
  57.1 37.9 %all-to-all-start.1 = ((bf16[16,72,768]{2,1,0:T(8,128)(2,1)}), bf16[16,72,768]{2,1,0:T(8,128)(2,1)}, u32[]{:S(2)}, u32[]{:S(2)}) async-start(bf16[16,72,768]{2,1,0:T(8,128)(2,1)} %bitcast.70), calls=%async_computation.1 | async-start | bytes 3538944 | tf_op jit(solution)/shard_map/all_to_all | solution.py:391
  89.6 5.5 %collective-permute-start.1 = (bf16[2,576,768]{2,1,0:T(8,128)(2,1)}, bf16[2,576,768]{2,1,0:T(8,128)(2,1)S(1)}, u32[]{:S(2)}, u32[]{:S(2)}) collective-permute-start(bf16[2,576,768]{2,1,0:T(8,128)(2,1)} %get-tuple-element.21), channel_id=1, source_target_pairs={{0,1},{1,0},{2,3},{3,2},{4,5},{5,4},{6,7},{7,6},{8,9},{9,8},{10,11... | collective-permute-start | bytes 5308424 | tf_op jit(solution)/shard_map/ppermute | solution.py:388
  95.0 1.5 copy-start.2
  98.2 6.0 %copy-start.7 = (s32[1,2]{1,0:T(1,128)S(1)}, s32[1,2]{1,0:T(1,128)}, u32[]{:S(2)}) copy-start(s32[1,2]{1,0:T(1,128)} %param.11) | copy-start | bytes 28
  98.2 10.3 %copy-start.6 = (s32[1,2,128,2]{2,3,1,0:T(2,128)S(1)}, s32[1,2,128,2]{2,3,1,0:T(2,128)}, u32[]{:S(2)}) copy-start(s32[1,2,128,2]{2,3,1,0:T(2,128)} %param.9) | copy-start | bytes 6148
  98.2 10.4 %copy-start.8 = (f32[1,2,128,2]{2,3,1,0:T(2,128)S(1)}, f32[1,2,128,2]{2,3,1,0:T(2,128)}, u32[]{:S(2)}) copy-start(f32[1,2,128,2]{2,3,1,0:T(2,128)} %param.10) | copy-start | bytes 6148
  98.2 29.9 %all-to-all-start.2 = ((bf16[16,72,768]{2,1,0:T(8,128)(2,1)}), bf16[16,72,768]{2,1,0:T(8,128)(2,1)S(1)}, u32[]{:S(2)}, u32[]{:S(2)}) async-start(bf16[16,72,768]{2,1,0:T(8,128)(2,1)} %bitcast.18), calls=%async_computation.2 | async-start | bytes 3538944 | tf_op jit(solution)/shard_map/all_to_all | solution.py:391
  104.1 24.2 %copy-start.3 = (bf16[1,128,768]{2,1,0:T(8,128)(2,1)S(1)}, bf16[1,128,768]{2,1,0:T(8,128)(2,1)}, u32[]{:S(2)}) copy-start(bf16[1,128,768]{2,1,0:T(8,128)(2,1)} %refs_1_.1) | copy-start | bytes 589828
  129.2 9.1 %collective-permute-start.2 = (bf16[128,768]{1,0:T(8,128)(2,1)S(1)}, bf16[128,768]{1,0:T(8,128)(2,1)S(1)}, u32[]{:S(2)}, u32[]{:S(2)}) collective-permute-start(bf16[128,768]{1,0:T(8,128)(2,1)S(1)} %fusion.1), channel_id=1, source_target_pairs={{0,224},{32,0},{64,32},{96,64},{128,96},{160,128},{192,160},{224,1... | collective-permute-start | bytes 589832 | tf_op jit(solution)/shard_map/ppermute | solution.py:409
  138.3 0.7 copy-start.4
  142.3 5.7 %collective-permute-start.3 = (bf16[2,576,768]{2,1,0:T(8,128)(2,1)}, bf16[2,576,768]{2,1,0:T(8,128)(2,1)S(1)}, u32[]{:S(2)}, u32[]{:S(2)}) collective-permute-start(bf16[2,576,768]{2,1,0:T(8,128)(2,1)} %landed.1.refs_1_), channel_id=1, source_target_pairs={{0,1},{1,0},{2,3},{3,2},{4,5},{5,4},{6,7},{7,6},{8,9},{9,8},{10,11... | collective-permute-start | bytes 5308424 | tf_op jit(solution)/shard_map/ppermute | solution.py:388
  142.4 31.6 %all-to-all-start.3 = ((bf16[16,72,768]{2,1,0:T(8,128)(2,1)}), bf16[16,72,768]{2,1,0:T(8,128)(2,1)}, u32[]{:S(2)}, u32[]{:S(2)}) async-start(bf16[16,72,768]{2,1,0:T(8,128)(2,1)} %bitcast.68), calls=%async_computation.3 | async-start | bytes 3538944 | tf_op jit(solution)/shard_map/all_to_all | solution.py:391
  148.0 1.2 copy-start
  149.2 1.5 copy-start.1
  173.9 3.9 %collective-permute-start.4 = (bf16[2,576,768]{2,1,0:T(8,128)(2,1)}, bf16[2,576,768]{2,1,0:T(8,128)(2,1)S(1)}, u32[]{:S(2)}, u32[]{:S(2)}) collective-permute-start(bf16[2,576,768]{2,1,0:T(8,128)(2,1)} %bitcast.28.refs_1_), channel_id=1, source_target_pairs={{0,1},{1,0},{2,3},{3,2},{4,5},{5,4},{6,7},{7,6},{8,9},{9,8},{10,11... | collective-permute-start | bytes 5308424 | tf_op jit(solution)/shard_map/ppermute | solution.py:388
  187.5 4.1 %collective-permute-start.5 = (bf16[2,576,768]{2,1,0:T(8,128)(2,1)S(1)}, bf16[2,576,768]{2,1,0:T(8,128)(2,1)S(1)}, u32[]{:S(2)}, u32[]{:S(2)}) collective-permute-start(bf16[2,576,768]{2,1,0:T(8,128)(2,1)S(1)} %get-tuple-element.28), channel_id=1, source_target_pairs={{0,1},{1,0},{2,3},{3,2},{4,5},{5,4},{6,7},{7,6},{8,9},{9,8},{10,11... | collective-permute-start | bytes 5308424 | tf_op jit(solution)/shard_map/ppermute | solution.py:388
  193.4 32.5 %all-to-all-start.4 = ((bf16[16,72,768]{2,1,0:T(8,128)(2,1)}), bf16[16,72,768]{2,1,0:T(8,128)(2,1)S(1)}, u32[]{:S(2)}, u32[]{:S(2)}) async-start(bf16[16,72,768]{2,1,0:T(8,128)(2,1)} %bitcast.29), calls=%async_computation.4 | async-start | bytes 3538944 | tf_op jit(solution)/shard_map/all_to_all | solution.py:391
  199.9 26.3 %copy-start.5 = (bf16[128,768]{1,0:T(8,128)(2,1)S(1)}, bf16[128,768]{1,0:T(8,128)(2,1)}, u32[]{:S(2)}) copy-start(bf16[128,768]{1,0:T(8,128)(2,1)} %copy-done.4) | copy-start | bytes 589828
  227.0 7.0 %collective-permute-start.6 = (bf16[128,768]{1,0:T(8,128)(2,1)S(1)}, bf16[128,768]{1,0:T(8,128)(2,1)S(1)}, u32[]{:S(2)}, u32[]{:S(2)}) collective-permute-start(bf16[128,768]{1,0:T(8,128)(2,1)S(1)} %add_convert_fusion.2), channel_id=1, source_target_pairs={{0,224},{32,0},{64,32},{96,64},{128,96},{160,128},{192,160},{224,1... | collective-permute-start | bytes 589832 | tf_op jit(solution)/shard_map/ppermute | solution.py:409

commit v6 on v5

v6 whole, which is shorter than its diff:
```python
import jax
import jax.numpy as jnp
from jax import lax
from jax.experimental import pallas as pl
from jax.experimental.pallas import tpu as pltpu
from jax.sharding import Mesh, PartitionSpec as P

EXPERTS = 4
CAPACITY = 72
HIDDEN_BLOCK = 256
VMEM_LIMIT = 18 * 1024 * 1024


def together(*values):
    return lax.optimization_barrier(values)


def contract_last(left, right):
    return lax.dot_general(
        left, right, (((1,), (1,)), ((), ())), preferred_element_type=jnp.float32
    )


HBM_SPEC = pl.BlockSpec(memory_space=pltpu.HBM)
VMEM_SPEC = pl.BlockSpec(memory_space=pltpu.VMEM)


def local_kernel(kernel, name, core, far, near, outs, scratch, flops=1000):
    return pl.pallas_call(
        kernel,
        out_shape=tuple(shape for shape, _ in outs),
        in_specs=[pl.BlockSpec(memory_space=pltpu.SMEM)]
        + [HBM_SPEC] * len(far)
        + [VMEM_SPEC] * len(near),
        out_specs=tuple(place for _, place in outs),
        scratch_shapes=scratch,
        compiler_params=pltpu.CompilerParams(vmem_limit_bytes=VMEM_LIMIT),
        cost_estimate=pl.CostEstimate(flops=flops, transcendentals=0, bytes_accessed=1000),
        name=name,
    )(core, *far, *near)


def stage_kernel(up, down, up_out, down_out, semaphores):
    pieces = semaphores.shape[0] // 2
    copies = []
    for source, target in ((up, up_out), (down, down_out)):
        step = source.shape[0] // pieces
        for piece in range(pieces):
            part = pl.ds(piece * step, step)
            copies.append(
                pltpu.make_async_copy(
                    source.at[part], target.at[part], semaphores.at[len(copies)]
                )
            )
            copies[-1].start()
    for copy in copies:
        copy.wait()


def stage(up, down, name):
    return pl.pallas_call(
        stage_kernel,
        out_shape=(pltpu.VMEM(up.shape, up.dtype), pltpu.VMEM(down.shape, down.dtype)),
        in_specs=[HBM_SPEC, HBM_SPEC],
        out_specs=(VMEM_SPEC, VMEM_SPEC),
        scratch_shapes=[pltpu.SemaphoreType.DMA((8,))],
        compiler_params=pltpu.CompilerParams(vmem_limit_bytes=1024 * 1024),
        cost_estimate=pl.CostEstimate(flops=1000, transcendentals=0, bytes_accessed=1000),
        name=name,
    )(up, down)


def row_copies(sources, column, rows_buf, semaphores):
    quarter = rows_buf.shape[2]
    halves = sources[0].shape[0]
    copies = [
        pltpu.make_async_copy(
            source.at[xhi, :, pl.ds(column * quarter, quarter)],
            rows_buf.at[n * halves + xhi],
            semaphores.at[n * halves + xhi],
        )
        for n, source in enumerate(sources)
        for xhi in range(halves)
    ]
    for copy in copies:
        copy.start()
    return copies


def first_feature(number, halves, core, quarter):
    side = core if number < halves else 1 - core
    return pl.multiple_of((2 * (number % halves) + side) * quarter, quarter)


def hidden_blocks(hidden):
    return [slice(start, start + HIDDEN_BLOCK) for start in range(0, hidden, HIDDEN_BLOCK)]


def factor_kernel(column, core_ref, mine, other, up, out, rows_buf, semaphores):
    copies = row_copies((mine, other), column, rows_buf, semaphores)
    pieces, _, quarter = rows_buf.shape
    for copy in copies:
        copy.wait()
    for block in hidden_blocks(up.shape[1]):
        pre = None
        for number in range(pieces):
            first = first_feature(number, pieces // 2, core_ref[0], quarter)
            part = jnp.dot(
                rows_buf[number],
                up[pl.ds(first, quarter), block],
                preferred_element_type=jnp.float32,
            )
            pre = part if pre is None else pre + part
        sigma = jax.nn.sigmoid(pre)
        out[:, block] = sigma * (1.0 + pre * (1.0 - sigma))


def factor(core, saved, up):
    mine, other, column = saved
    halves, rows = mine.shape[:2]
    width, hidden = up.shape
    pieces = 2 * halves
    return local_kernel(
        lambda *refs: factor_kernel(column, *refs),
        "factor",
        core,
        [mine, other],
        [up],
        [(pltpu.VMEM((rows, hidden), jnp.float32), VMEM_SPEC)],
        [
            pltpu.VMEM((pieces, rows, width // pieces), jnp.bfloat16),
            pltpu.SemaphoreType.DMA((pieces,)),
        ],
    )[0]


def add_act(rows_buf, numbers, core, down, block):
    act = None
    halves = down.shape[1] // rows_buf.shape[2] // 2
    for slot, number in enumerate(numbers):
        first = first_feature(number, halves, core, rows_buf.shape[2])
        part = contract_last(rows_buf[slot], down[block, pl.ds(first, rows_buf.shape[2])])
        act = part if act is None else act + part
    return act


def branch_parts(numbers, core, grad_pre, up, results, targets, semaphores):
    quarter = results.shape[2]
    halves = up.shape[0] // quarter // 2
    sent = []
    for slot, number in enumerate(numbers):
        first = first_feature(number, halves, core, quarter)
        results[slot] = contract_last(
            grad_pre[...], up[pl.ds(first, quarter), :]
        ).astype(jnp.bfloat16)
        copy = pltpu.make_async_copy(results.at[slot], targets[slot], semaphores.at[slot])
        copy.start()
        sent.append(copy)
    for copy in sent:
        copy.wait()


def branch_kernel(
    column, core_ref, mine, other, up, down, factors, send, keep, rows_buf, grad_pre, results,
    semaphores, out_semaphores,
):
    copies = row_copies((mine, other), column, rows_buf, semaphores)
    pieces = rows_buf.shape[0]
    halves = pieces // 2
    for copy in copies:
        copy.wait()
    for block in hidden_blocks(down.shape[0]):
        act = add_act(rows_buf, range(pieces), core_ref[0], down, block)
        grad_pre[:, block] = (act * factors[:, block]).astype(jnp.bfloat16)
    numbers = [halves + n for n in range(halves)] + list(range(halves))
    targets = [send.at[n] for n in range(halves)] + [keep.at[n] for n in range(halves)]
    branch_parts(numbers, core_ref[0], grad_pre, up, results, targets, out_semaphores)


def branch(core, grads, up, down, factors):
    mine, other, column = grads
    halves, rows = mine.shape[:2]
    hidden, width = down.shape
    pieces = 2 * halves
    quarter = width // pieces
    part = (halves, rows, quarter)
    return local_kernel(
        lambda *refs: branch_kernel(column, *refs),
        "branch",
        core,
        [mine, other],
        [up, down, factors],
        [
            (jax.ShapeDtypeStruct(part, jnp.bfloat16), HBM_SPEC),
            (pltpu.HBM(part, jnp.bfloat16), HBM_SPEC),
        ],
        [
            pltpu.VMEM((pieces, rows, quarter), jnp.bfloat16),
            pltpu.VMEM((rows, hidden), jnp.bfloat16),
            pltpu.VMEM((pieces, rows, quarter), jnp.bfloat16),
            pltpu.SemaphoreType.DMA((pieces,)),
            pltpu.SemaphoreType.DMA((pieces,)),
        ],
    )


def own_act_kernel(core_ref, mine, down, out, rows_buf, semaphores):
    for copy in row_copies((mine,), 0, rows_buf, semaphores):
        copy.wait()
    for block in hidden_blocks(down.shape[0]):
        out[:, block] = add_act(rows_buf, range(rows_buf.shape[0]), core_ref[0], down, block)


def own_act(core, mine, down):
    halves, rows, quarter = mine.shape
    return local_kernel(
        own_act_kernel,
        "own_act",
        core,
        [mine],
        [down],
        [(pltpu.VMEM((rows, down.shape[0]), jnp.float32), VMEM_SPEC)],
        [
            pltpu.VMEM((halves, rows, quarter), jnp.bfloat16),
            pltpu.SemaphoreType.DMA((halves,)),
        ],
    )[0]


def sent_kernel(
    core_ref, other, up, down, own, factors, grad_pre, send, rows_buf, results, semaphores,
    out_semaphores,
):
    halves = rows_buf.shape[0]
    late = [halves + n for n in range(halves)]
    for copy in row_copies((other,), 0, rows_buf, semaphores):
        copy.wait()
    for block in hidden_blocks(down.shape[0]):
        act = own[:, block] + add_act(rows_buf, late, core_ref[0], down, block)
        grad_pre[:, block] = (act * factors[:, block]).astype(jnp.bfloat16)
    targets = [send.at[n] for n in range(halves)]
    branch_parts(late, core_ref[0], grad_pre, up, results, targets, out_semaphores)


def sent_part(core, other, up, down, own, factors):
    halves, rows, quarter = other.shape
    return local_kernel(
        sent_kernel,
        "sent_part",
        core,
        [other],
        [up, down, own, factors],
        [
            (pltpu.VMEM((rows, down.shape[0]), jnp.bfloat16), VMEM_SPEC),
            (jax.ShapeDtypeStruct(other.shape, jnp.bfloat16), HBM_SPEC),
        ],
        [
            pltpu.VMEM((halves, rows, quarter), jnp.bfloat16),
            pltpu.VMEM((halves, rows, quarter), jnp.bfloat16),
            pltpu.SemaphoreType.DMA((halves,)),
            pltpu.SemaphoreType.DMA((halves,)),
        ],
    )


def kept_kernel(core_ref, up, grad_pre, keep, results, semaphores):
    halves = keep.shape[0]
    targets = [keep.at[n] for n in range(halves)]
    branch_parts(range(halves), core_ref[0], grad_pre, up, results, targets, semaphores)


def kept_part(core, up, grad_pre, part):
    return local_kernel(
        kept_kernel,
        "kept_part",
        core,
        [],
        [up, grad_pre],
        [(jax.ShapeDtypeStruct(part, jnp.bfloat16), HBM_SPEC)],
        [pltpu.VMEM(part, jnp.bfloat16), pltpu.SemaphoreType.DMA((part[0],))],
        flops=10**10,
    )[0]


def pick_kernel(plan_ref, routes_ref, *refs):
    del plan_ref
    values, (out, buffer, semaphores) = refs[:-3], refs[-3:]
    rows = routes_ref.shape[2]
    expert = lax.broadcasted_iota(jnp.int32, (16, rows), 0)
    named = routes_ref[0]
    chosen = named[0:1] == expert
    for choice in range(1, named.shape[0]):
        chosen = chosen | (named[choice : choice + 1] == expert)
    earlier = (
        lax.broadcasted_iota(jnp.int32, (rows, rows), 0)
        < lax.broadcasted_iota(jnp.int32, (rows, rows), 1)
    ).astype(jnp.float32)
    before = jnp.dot(
        chosen.astype(jnp.float32).astype(jnp.bfloat16),
        earlier.astype(jnp.bfloat16),
        preferred_element_type=jnp.float32,
    )
    place = jnp.where(chosen, before, -1.0).astype(jnp.int32)
    slot = lax.broadcasted_iota(jnp.int32, (CAPACITY, rows), 0)
    copies = []
    for j in range(EXPERTS):
        select = (place[j : j + 1] == slot).astype(jnp.float32).astype(jnp.bfloat16)
        start = 0
        for value_ref in values:
            width = value_ref.shape[2]
            buffer[j, :, start : start + width] = jnp.dot(
                select, value_ref[0], preferred_element_type=jnp.float32
            ).astype(jnp.bfloat16)
            start += width
        for i in range(out.shape[0]):
            for k in range(out.shape[2]):
                copy = pltpu.make_async_copy(
                    buffer.at[j], out.at[i, j, k], semaphores.at[len(copies)]
                )
                copy.start()
                copies.append(copy)
    for copy in copies:
        copy.wait()


def pick(step, plan, routes, values, n_xhi, per_expert):
    width = sum(value.shape[2] for value, _ in values)
    specs = [pl.BlockSpec((1,) + routes.shape[1:], lambda i, p: (p[step], 0, 0))]
    for value, planned in values:
        if planned:
            specs.append(pl.BlockSpec((1,) + value.shape[1:], lambda i, p: (p[step], 0, 0)))
        else:
            specs.append(pl.BlockSpec((1,) + value.shape[1:], lambda i, p: (0, 0, 0)))
    out = pl.pallas_call(
        pick_kernel,
        out_shape=jax.ShapeDtypeStruct(
            (n_xhi, EXPERTS, per_expert, CAPACITY, width), jnp.bfloat16
        ),
        grid_spec=pltpu.PrefetchScalarGridSpec(
            num_scalar_prefetch=1,
            grid=(1,),
            in_specs=specs,
            out_specs=pl.BlockSpec(memory_space=pltpu.HBM),
            scratch_shapes=[
                pltpu.VMEM((EXPERTS, CAPACITY, width), jnp.bfloat16),
                pltpu.SemaphoreType.DMA((n_xhi * EXPERTS * per_expert,)),
            ],
        ),
        compiler_params=pltpu.CompilerParams(dimension_semantics=("arbitrary",)),
        name="pick",
    )(plan, routes, *[value for value, _ in values])
    return out.reshape(n_xhi * EXPERTS * per_expert, CAPACITY, width)


def landed(value):
    anywhere = pl.BlockSpec(memory_space=pltpu.HBM)
    return pl.pallas_call(
        lambda value_ref, same_ref: None,
        out_shape=jax.ShapeDtypeStruct(value.shape, value.dtype),
        in_specs=[anywhere],
        out_specs=anywhere,
        input_output_aliases={0: 0},
        cost_estimate=pl.CostEstimate(
            flops=10**11, transcendentals=0, bytes_accessed=10**8
        ),
        name="landed",
    )(value)


def slots(route_now, share_now):
    rows = route_now.shape[0]
    named = route_now.T[None] == jnp.arange(EXPERTS, dtype=jnp.int32)[:, None, None]
    chosen = jnp.any(named, axis=1)
    mix = jnp.sum(jnp.where(named, share_now.T[None], 0.0), axis=1)
    token = jnp.arange(rows, dtype=jnp.int32)
    earlier = (token[:, None] < token[None, :]).astype(jnp.bfloat16)
    before = jnp.dot(
        chosen.astype(jnp.bfloat16), earlier, preferred_element_type=jnp.float32
    ).astype(jnp.int32)
    place = jnp.where(chosen, before, -1)
    hit = place[:, None, :] == jnp.arange(CAPACITY, dtype=jnp.int32)[None, :, None]
    mixing = jnp.where(hit, mix[:, None, :], 0.0).reshape(EXPERTS * CAPACITY, rows)
    return hit, mixing


def per_device(grad_in, saved_input, routes, route_weights, plan, up_weight, down_weight):
    n_expert = lax.axis_size("expert")
    n_xhi = lax.axis_size("xhi")
    n_section = lax.axis_size("section")
    per_expert = n_expert // EXPERTS
    peers = n_xhi * n_expert
    rows, quarter = grad_in.shape[1:]
    up_local = pltpu.with_memory_space_constraint(up_weight[0], pltpu.HBM)
    down_local = pltpu.with_memory_space_constraint(down_weight[0], pltpu.HBM)
    core = lax.axis_index("core").astype(jnp.int32).reshape(1)

    def swap_cores(value):
        return lax.ppermute(value, "core", [(0, 1), (1, 0)])

    def exchange(value):
        return lax.all_to_all(value, ("xhi", "expert"), split_axis=0, concat_axis=0, tiled=True)

    def deliver(sent):
        return exchange(sent).reshape(n_xhi, n_expert * CAPACITY, sent.shape[2])

    def combine(current, mixing, arrived):
        summed = jnp.sum(
            arrived.reshape(n_xhi, EXPERTS, per_expert, CAPACITY, quarter).astype(jnp.float32),
            axis=(0, 2),
        )
        moe_term = lax.dot_general(
            mixing,
            summed.reshape(EXPERTS * CAPACITY, quarter),
            (((0,), (0,)), ((), ())),
            precision=lax.Precision.HIGHEST,
            preferred_element_type=jnp.float32,
        )
        result = (current.astype(jnp.float32) + moe_term).astype(jnp.bfloat16)
        return lax.ppermute(
            result, "section", [(i, (i - 1) % n_section) for i in range(n_section)]
        )

    def outgoing(send, keep):
        return (
            keep.astype(jnp.float32) + swap_cores(send).astype(jnp.float32)
        ).astype(jnp.bfloat16).reshape(peers, CAPACITY, quarter)

    micros = plan[0]
    routes_by_choice = routes[0].transpose(0, 2, 1)
    saved_all = saved_input[0]
    current = grad_in[0]
    ticks = micros.shape[0]

    def slots_of(tick):
        route_now = lax.dynamic_index_in_dim(routes[0], micros[tick], 0, keepdims=False)
        share_now = lax.dynamic_index_in_dim(route_weights[0], micros[tick], 0, keepdims=False)
        return slots(route_now, share_now)

    def pick_rows(tick, *values):
        return pick(tick, micros, routes_by_choice, values, n_xhi, per_expert)

    both = deliver(pick_rows(0, (saved_all, True), (current[None], False)))
    up_near, down_near = stage(up_local, down_local, "stage_first")
    both, up_near, down_near = together(both, up_near, down_near)
    later = None
    if ticks > 1:
        saved_sent, both = together(pick_rows(1, (saved_all, True)), both)
        later = deliver(saved_sent)
    swapped = swap_cores(both)
    factors = factor(core, (both, swapped, 0), up_near)
    send, keep = branch(core, (both, swapped, 1), up_near, down_near, factors)
    for tick in range(ticks):
        got = swap_cores(send)
        if tick + 1 < ticks:
            keep, later = together(keep, landed(later))
        partial_rows = (keep.astype(jnp.float32) + got.astype(jnp.float32)).astype(jnp.bfloat16)
        arrived = exchange(partial_rows.reshape(peers, CAPACITY, quarter))
        _, mixing = slots_of(tick)
        if tick + 1 == ticks:
            return combine(current, mixing, arrived)[None]
        later_swapped = swap_cores(later)
        hit, _ = slots_of(tick + 1)
        picks = jnp.broadcast_to(
            hit[None, :, None], (n_xhi, EXPERTS, per_expert, CAPACITY, rows)
        ).reshape(peers * CAPACITY, rows)
        arrived, later_swapped, picks = together(arrived, later_swapped, picks)
        current = combine(current, mixing, arrived)
        grad_sent = jnp.dot(
            picks.astype(jnp.bfloat16), current, preferred_element_type=jnp.float32
        ).astype(jnp.bfloat16)
        grad_sent, later, later_swapped = together(
            grad_sent.reshape(peers, CAPACITY, quarter), later, later_swapped
        )
        grad_rows = deliver(grad_sent)
        up_near, down_near = stage(up_local, down_local, "stage_next")
        factors = factor(core, (later, later_swapped, 0), up_near)
        grad_rows, factors, down_near = together(grad_rows, factors, down_near)
        swapped = swap_cores(grad_rows)
        own = own_act(core, grad_rows, down_near)
        grad_pre, send = sent_part(core, swapped, up_near, down_near, own, factors)
        keep = kept_part(core, up_near, grad_pre, send.shape)


def solution(mesh):
    sections, experts, parts = (mesh.shape[name] for name in ("section", "expert", "mp"))
    refined = Mesh(
        mesh.devices.reshape(sections, experts, parts // 2, 2),
        ("section", "expert", "xhi", "core"),
    )
    mp = ("xhi", "core")
    placed = (
        P("section", "expert", mp),
        P("section", None, "expert", mp),
        P("section", None, "expert", None),
        P("section", None, "expert", None),
        P("section", None),
        P("section", None, ("expert", "xhi", "core")),
        P("section", ("expert", "xhi", "core"), None),
    )
    return jax.shard_map(
        per_device,
        mesh=refined,
        in_specs=placed,
        out_specs=P("section", "expert", mp),
        check_vma=False,
    )
```

time: 235 us -> 227 us (0.966)
  waiting for transfers between devices: 119 us -> 94.5 us
  local copies, waits for them, and re-layouts: 6.13 us -> 19.7 us
  matrix products: 1.97 us -> 4.38 us
    all_to_all x5, waiting for transfers between devices: 108 us -> 88 us  [exchange(): lax.all_to_all(value, ('xhi', 'expert'), split_axis=0, concat_axis=0, til...]
    unnamed x19 -> x33, local copies, waits for them, and re-layouts: 5.53 us -> 18.2 us
    ppermute x5, waiting for transfers between devices: 3.91 us -> 0.12 us  [swap_cores(): return lax.ppermute(value, 'core', [(0, 1), (1, 0)])]
    pallas_call x3 -> x2, Pallas kernels: 10.5 us -> 7.27 us  [pick(): pl.pallas_call(pick_kernel, out_shape=jax.ShapeDtypeStruct((n_xhi, EXPERT...]
    pallas_call x5 -> x8, Pallas kernels: 41.7 us -> 43.2 us  [the longest x6 33.7 us: local_kernel(): pl.pallas_call(kernel, out_shape=tuple((shape for shape, _ in outs)), in_...]
  transfers between devices with their start and end apart: 12 -> 12, of which waited for: 8 -> 8; matrix products, arithmetic and copies ran while one was open for 0% -> 2% of each run, Pallas kernels for 15% -> 18%
where the time goes in v6:
time: 227 us; the launch traced here: 226 us
  waiting for transfers between devices  94.5 us (42%)
  Pallas kernels  50.5 us (22%)
  starting transfers between devices  47.1 us (21%)
  local copies, waits for them, and re-layouts  19.7 us (9%)
  other arithmetic  5.98 us (3%)
  matrix products  4.38 us (2%)
  between operations  4.08 us (2%)
    all_to_all x5, waiting for transfers between devices, exchange(): lax.all_to_all(value, ('xhi', 'expert'), split_axis=0, concat_axis=0, til...  88 us
    all_to_all x5, starting transfers between devices, exchange(): lax.all_to_all(value, ('xhi', 'expert'), split_axis=0, concat_axis=0, til...  37 us
    pallas_call x6, Pallas kernels, local_kernel(): pl.pallas_call(kernel, out_shape=tuple((shape for shape, _ in outs)), in_...  33.7 us
    unnamed x33, local copies, waits for them, and re-layouts  18.2 us
    pallas_call x2, Pallas kernels, stage(): pl.pallas_call(stage_kernel, out_shape=(pltpu.VMEM(up.shape, up.dtype), p...  9.52 us
    ppermute x2, starting transfers between devices, combine(): lax.ppermute(result, 'section', [(i, (i - 1) % n_section) for i in range(...  9.13 us
    pallas_call x2, Pallas kernels, pick(): pl.pallas_call(pick_kernel, out_shape=jax.ShapeDtypeStruct((n_xhi, EXPERT...  7.27 us
    ppermute x2, waiting for transfers between devices, combine(): lax.ppermute(result, 'section', [(i, (i - 1) % n_section) for i in range(...  6.38 us
  transfers between devices with their start and end apart: 12, of which 8 were waited for; matrix products, arithmetic and copies ran while one was open for 2% of the time, Pallas kernels for 18%

profile of v6, /device:TPU:8, one launch (start us, length us, event | category | flops | bytes accessed | tf_op | source)
XLA Modules:
  0.0 226.2 jit_solution(10030811081080227759)
XLA Ops:
  0.0 4.0 %pick.3 = bf16[2,4,2,72,1536]{4,3,2,1,0:T(8,128)(2,1)} custom-call(s32[2]{0:T(128)} %bitcast.77, s32[2,2,128]{2,1,0:T(2,128)} %bitcast.75, bf16[2,128,768]{2,1,0:T(8,128)(2,1)} %bitcast.71, bf16[1,128,768]{2,1,0:T(8,128)(2,1)} %refs_1_.1), custom_call_target="tpu_custom_call" | custom-call | tf_op jit(solution)/shard_map/pick/pallas_call | solution.py:334
  4.0 7.4 %all-to-all-start = ((bf16[16,72,1536]{2,1,0:T(8,128)(2,1)}), bf16[16,72,1536]{2,1,0:T(8,128)(2,1)S(1)}, u32[]{:S(2)}, u32[]{:S(2)}) async-start(bf16[16,72,1536]{2,1,0:T(8,128)(2,1)} %bitcast.66), calls=%async_computation | async-start | bytes 7077888 | tf_op jit(solution)/shard_map/all_to_all | solution.py:401
  11.4 4.7 %stage_first.1 = (bf16[3072,1024]{1,0:T(8,128)(2,1)S(1)}, bf16[1024,3072]{1,0:T(8,128)(2,1)S(1)}) custom-call(bf16[3072,1024]{1,0:T(8,128)(2,1)} %bitcast.62, bf16[1024,3072]{1,0:T(8,128)(2,1)} %bitcast.64), custom_call_target="tpu_custom_call" | custom-call | flops 1000 | bytes 1000 | tf_op jit(solution)/shard_map/stage_first/pallas_call | solution.py:61
  16.1 0.0 copy-start.2
  16.1 2.6 %copy-done.2 = bf16[3072,1024]{1,0:T(8,128)(2,1)} copy-done((bf16[3072,1024]{1,0:T(8,128)(2,1)}, bf16[3072,1024]{1,0:T(8,128)(2,1)S(1)}, u32[]{:S(2)}) %copy-start.2) | copy-done | bytes 6291480
  18.7 2.6 %copy-done.6 = bf16[1024,3072]{1,0:T(8,128)(2,1)} copy-done((bf16[1024,3072]{1,0:T(8,128)(2,1)}, bf16[1024,3072]{1,0:T(8,128)(2,1)S(1)}, u32[]{:S(2)}) %copy-start.6) | copy-done | bytes 6291480
  21.3 3.3 %pick.2 = bf16[2,4,2,72,768]{4,3,2,1,0:T(8,128)(2,1)} custom-call(s32[2]{0:T(128)} %bitcast.78, s32[2,2,128]{2,1,0:T(2,128)} %bitcast.76, bf16[2,128,768]{2,1,0:T(8,128)(2,1)} %bitcast.72), custom_call_target="tpu_custom_call" | custom-call | tf_op jit(solution)/shard_map/pick/pallas_call | solution.py:334
  24.6 32.5 %all-to-all-done = bf16[16,72,1536]{2,1,0:T(8,128)(2,1)S(1)} async-done(((bf16[16,72,1536]{2,1,0:T(8,128)(2,1)}), bf16[16,72,1536]{2,1,0:T(8,128)(2,1)S(1)}, u32[]{:S(2)}, u32[]{:S(2)}) %all-to-all-start) | async-done | bytes 3538976 | tf_op jit(solution)/shard_map/all_to_all | solution.py:401
  57.1 0.0 collective-permute-start
  57.1 11.9 %all-to-all-start.1 = ((bf16[16,72,768]{2,1,0:T(8,128)(2,1)}), bf16[16,72,768]{2,1,0:T(8,128)(2,1)}, u32[]{:S(2)}, u32[]{:S(2)}) async-start(bf16[16,72,768]{2,1,0:T(8,128)(2,1)} %bitcast.68), calls=%async_computation.1 | async-start | bytes 3538944 | tf_op jit(solution)/shard_map/all_to_all | solution.py:401
  69.1 0.0 collective-permute-done.refs_2_
  69.1 0.0 copy-start.3
  69.1 2.8 %copy-done.3 = bf16[3072,1024]{1,0:T(8,128)(2,1)S(1)} copy-done((bf16[3072,1024]{1,0:T(8,128)(2,1)S(1)}, bf16[3072,1024]{1,0:T(8,128)(2,1)}, u32[]{:S(2)}) %copy-start.3) | copy-done | bytes 6291480
  71.8 5.8 %factor.2.refs_5_ = f32[576,1024]{1,0:T(8,128)S(1)} custom-call(s32[1]{0:T(128)} %bitcast.6.refs_0_.core_ref, bf16[2,576,1536]{2,1,0:T(8,128)(2,1)S(1)} %bitcast.60, bf16[2,576,1536]{2,1,0:T(8,128)(2,1)} %collective-permute-done.refs_2_, bf16[3072,1024]{1,0:T(8,128)(2,1)S(1)} %copy-done.3), custom_call_target="tpu_custom_call" | custom-call | flops 1000 | bytes 1000 | tf_op jit(solution)/shard_map/factor/pallas_call | solution.py:29
  77.6 0.0 copy-done.7
  77.6 10.1 %branch.1 = (bf16[2,576,768]{2,1,0:T(8,128)(2,1)}, bf16[2,576,768]{2,1,0:T(8,128)(2,1)}) custom-call(s32[1]{0:T(128)} %bitcast.6.refs_0_.core_ref, bf16[2,576,1536]{2,1,0:T(8,128)(2,1)S(1)} %bitcast.61, bf16[2,576,1536]{2,1,0:T(8,128)(2,1)} %collective-permute-done.refs_2_, bf16[3072,1024]{1,0:T(8,128)(2,1)S(1)} %copy-done.3, ...), custom_call_target="tpu_custom_call" | custom-call | flops 1000 | bytes 1000 | tf_op jit(solution)/shard_map/branch/pallas_call | solution.py:29
  87.8 0.1 collective-permute-start.1
  87.9 7.2 %all-to-all-done.1 = bf16[16,72,768]{2,1,0:T(8,128)(2,1)} async-done(((bf16[16,72,768]{2,1,0:T(8,128)(2,1)}), bf16[16,72,768]{2,1,0:T(8,128)(2,1)}, u32[]{:S(2)}, u32[]{:S(2)}) %all-to-all-start.1) | async-done | bytes 1769504 | tf_op jit(solution)/shard_map/all_to_all | solution.py:401
  95.1 0.0 collective-permute-start.2
  95.1 0.0 collective-permute-done.1
  95.1 1.5 copy-done.10
  96.5 3.1 %add_convert_fusion.1 = bf16[2,576,768]{2,1,0:T(8,128)(2,1)} fusion(bf16[2,576,768]{2,1,0:T(8,128)(2,1)} %collective-permute-done.1, bf16[2,576,768]{2,1,0:T(8,128)(2,1)S(1)} %copy-done.10), kind=kLoop, calls=%fused_computation.3 | loop fusion | flops 3538944 | bytes 5308416 | tf_op jit(solution)/shard_map/convert_element_type | solution.py:456
  99.7 6.0 %all-to-all-start.2 = ((bf16[16,72,768]{2,1,0:T(8,128)(2,1)}), bf16[16,72,768]{2,1,0:T(8,128)(2,1)S(1)}, u32[]{:S(2)}, u32[]{:S(2)}) async-start(bf16[16,72,768]{2,1,0:T(8,128)(2,1)} %bitcast.70), calls=%async_computation.2 | async-start | bytes 3538944 | tf_op jit(solution)/shard_map/all_to_all | solution.py:401
  105.6 0.0 copy-done.13
  105.6 0.6 fusion.17
  110.1 0.0 copy-done.12
  110.1 0.0 copy-done.15
  110.2 0.1 fusion.2
  110.3 0.7 fusion.3
  111.0 0.6 iota_compare_fusion
  111.7 0.0 collective-permute-done.2.refs_2_
  111.7 17.9 %all-to-all-done.2 = bf16[16,72,768]{2,1,0:T(8,128)(2,1)S(1)} async-done(((bf16[16,72,768]{2,1,0:T(8,128)(2,1)}), bf16[16,72,768]{2,1,0:T(8,128)(2,1)S(1)}, u32[]{:S(2)}, u32[]{:S(2)}) %all-to-all-start.2) | async-done | bytes 1769504 | tf_op jit(solution)/shard_map/all_to_all | solution.py:401
  129.6 0.8 broadcast_in_dim.78
  130.4 0.2 convert_reduce_fusion.1
  130.7 0.0 copy-done.11
  130.7 0.0 copy-done.14
  130.7 0.9 fusion.1
  131.6 0.0 copy-done.8
  131.6 5.9 %collective-permute-start.3 = (bf16[128,768]{1,0:T(8,128)(2,1)S(1)}, bf16[128,768]{1,0:T(8,128)(2,1)S(1)}, u32[]{:S(2)}, u32[]{:S(2)}) collective-permute-start(bf16[128,768]{1,0:T(8,128)(2,1)S(1)} %fusion.1), channel_id=1, source_target_pairs={{0,224},{32,0},{64,32},{96,64},{128,96},{160,128},{192,160},{224,1... | collective-permute-start | bytes 589832 | tf_op jit(solution)/shard_map/ppermute | solution.py:419
  137.5 3.2 %collective-permute-done.3 = bf16[128,768]{1,0:T(8,128)(2,1)S(1)} collective-permute-done((bf16[128,768]{1,0:T(8,128)(2,1)S(1)}, bf16[128,768]{1,0:T(8,128)(2,1)S(1)}, u32[]{:S(2)}, u32[]{:S(2)}) %collective-permute-start.3) | collective-permute-done | bytes 196640 | tf_op jit(solution)/shard_map/ppermute | solution.py:419
  140.7 1.8 convolution_convert_fusion
  142.5 5.6 %all-to-all-start.3 = ((bf16[16,72,768]{2,1,0:T(8,128)(2,1)}), bf16[16,72,768]{2,1,0:T(8,128)(2,1)}, u32[]{:S(2)}, u32[]{:S(2)}) async-start(bf16[16,72,768]{2,1,0:T(8,128)(2,1)} %bitcast.27), calls=%async_computation.3 | async-start | bytes 3538944 | tf_op jit(solution)/shard_map/all_to_all | solution.py:401
  148.1 4.8 %stage_next.1 = (bf16[3072,1024]{1,0:T(8,128)(2,1)S(1)}, bf16[1024,3072]{1,0:T(8,128)(2,1)S(1)}) custom-call(bf16[3072,1024]{1,0:T(8,128)(2,1)} %bitcast.63, bf16[1024,3072]{1,0:T(8,128)(2,1)} %bitcast.65), custom_call_target="tpu_custom_call" | custom-call | flops 1000 | bytes 1000 | tf_op jit(solution)/shard_map/stage_next/pallas_call | solution.py:61
  153.0 2.6 %copy-done.4 = bf16[1024,3072]{1,0:T(8,128)(2,1)} copy-done((bf16[1024,3072]{1,0:T(8,128)(2,1)}, bf16[1024,3072]{1,0:T(8,128)(2,1)S(1)}, u32[]{:S(2)}) %copy-start.4) | copy-done | bytes 6291480
  155.6 5.5 %factor.3.factors = f32[576,1024]{1,0:T(8,128)S(1)} custom-call(s32[1]{0:T(128)} %bitcast.6.refs_0_.core_ref, bf16[2,576,768]{2,1,0:T(8,128)(2,1)} %landed.1.refs_1_, bf16[2,576,768]{2,1,0:T(8,128)(2,1)S(1)} %copy-done.9, bf16[3072,1024]{1,0:T(8,128)(2,1)S(1)} %get-tuple-element.41.refs_3_.up), custom_call_target="tpu_custom_call" | custom-call | flops 1000 | bytes 1000 | tf_op jit(solution)/shard_map/factor/pallas_call | solution.py:29
  161.2 2.6 %copy-done = bf16[3072,1024]{1,0:T(8,128)(2,1)} copy-done((bf16[3072,1024]{1,0:T(8,128)(2,1)}, bf16[3072,1024]{1,0:T(8,128)(2,1)S(1)}, u32[]{:S(2)}) %copy-start) | copy-done | bytes 6291480
  163.8 4.4 %all-to-all-done.3 = bf16[16,72,768]{2,1,0:T(8,128)(2,1)} async-done(((bf16[16,72,768]{2,1,0:T(8,128)(2,1)}), bf16[16,72,768]{2,1,0:T(8,128)(2,1)}, u32[]{:S(2)}, u32[]{:S(2)}) %all-to-all-start.3) | async-done | bytes 1769504 | tf_op jit(solution)/shard_map/all_to_all | solution.py:401
  168.1 0.0 collective-permute-start.4
  168.1 2.8 %copy-done.5 = bf16[1024,3072]{1,0:T(8,128)(2,1)S(1)} copy-done((bf16[1024,3072]{1,0:T(8,128)(2,1)S(1)}, bf16[1024,3072]{1,0:T(8,128)(2,1)}, u32[]{:S(2)}) %copy-start.5) | copy-done | bytes 6291480
  170.9 3.6 %own_act.1.own = f32[576,1024]{1,0:T(8,128)S(1)} custom-call(s32[1]{0:T(128)} %bitcast.6.refs_0_.core_ref, bf16[2,576,768]{2,1,0:T(8,128)(2,1)} %bitcast.28.mine, bf16[1024,3072]{1,0:T(8,128)(2,1)S(1)} %copy-done.5), custom_call_target="tpu_custom_call" | custom-call | flops 1000 | bytes 1000 | tf_op jit(solution)/shard_map/own_act/pallas_call | solution.py:29
  174.5 0.0 collective-permute-done.4.other
  174.6 0.0 copy-done.1
  174.6 5.5 %sent_part.1 = (bf16[576,1024]{1,0:T(8,128)(2,1)S(1)}, bf16[2,576,768]{2,1,0:T(8,128)(2,1)S(1)}) custom-call(s32[1]{0:T(128)} %bitcast.6.refs_0_.core_ref, bf16[2,576,768]{2,1,0:T(8,128)(2,1)S(1)} %collective-permute-done.4.other, bf16[3072,1024]{1,0:T(8,128)(2,1)S(1)} %copy-done.1, bf16[1024,3072]{1,0:T(8,128)(2,1)S(1)} %copy-done.5, ...), custom_call_target="tpu_custom_call" | custom-call | flops 1000 | bytes 1000 | tf_op jit(solution)/shard_map/sent_part/pallas_call | solution.py:29
  180.0 0.8 collective-permute-start.5
  180.8 3.2 %kept_part.1 = bf16[2,576,768]{2,1,0:T(8,128)(2,1)S(1)} custom-call(s32[1]{0:T(128)} %bitcast.6.refs_0_.core_ref, bf16[3072,1024]{1,0:T(8,128)(2,1)S(1)} %copy-done.1, bf16[576,1024]{1,0:T(8,128)(2,1)S(1)} %get-tuple-element.51.grad_pre), custom_call_target="tpu_custom_call" | custom-call | flops 10000000000 | bytes 1000 | tf_op jit(solution)/shard_map/kept_part/pallas_call | solution.py:29
  184.1 0.1 collective-permute-done.5
  184.2 1.7 add_convert_fusion
  185.9 6.1 %all-to-all-start.4 = ((bf16[16,72,768]{2,1,0:T(8,128)(2,1)}), bf16[16,72,768]{2,1,0:T(8,128)(2,1)S(1)}, u32[]{:S(2)}, u32[]{:S(2)}) async-start(bf16[16,72,768]{2,1,0:T(8,128)(2,1)} %bitcast.29), calls=%async_computation.4 | async-start | bytes 3538944 | tf_op jit(solution)/shard_map/all_to_all | solution.py:401
  192.0 26.0 %all-to-all-done.4 = bf16[16,72,768]{2,1,0:T(8,128)(2,1)S(1)} async-done(((bf16[16,72,768]{2,1,0:T(8,128)(2,1)}), bf16[16,72,768]{2,1,0:T(8,128)(2,1)S(1)}, u32[]{:S(2)}, u32[]{:S(2)}) %all-to-all-start.4) | async-done | bytes 1769504 | tf_op jit(solution)/shard_map/all_to_all | solution.py:401
  218.0 0.2 convert_reduce_fusion
  218.2 0.8 add_convert_fusion.2
  219.1 3.2 %collective-permute-start.6 = (bf16[128,768]{1,0:T(8,128)(2,1)S(1)}, bf16[128,768]{1,0:T(8,128)(2,1)S(1)}, u32[]{:S(2)}, u32[]{:S(2)}) collective-permute-start(bf16[128,768]{1,0:T(8,128)(2,1)S(1)} %add_convert_fusion.2), channel_id=1, source_target_pairs={{0,224},{32,0},{64,32},{96,64},{128,96},{160,128},{192,160},{224,1... | collective-permute-start | bytes 589832 | tf_op jit(solution)/shard_map/ppermute | solution.py:419
  222.3 3.2 %collective-permute-done.6 = bf16[128,768]{1,0:T(8,128)(2,1)S(1)} collective-permute-done((bf16[128,768]{1,0:T(8,128)(2,1)S(1)}, bf16[128,768]{1,0:T(8,128)(2,1)S(1)}, u32[]{:S(2)}, u32[]{:S(2)}) %collective-permute-start.6) | collective-permute-done | bytes 196640 | tf_op jit(solution)/shard_map/ppermute | solution.py:419
  225.5 0.7 copy.11
  (21 shorter events, 0.1 us)
Async XLA Ops:
  4.0 53.2 %all-to-all-start = ((bf16[16,72,1536]{2,1,0:T(8,128)(2,1)}), bf16[16,72,1536]{2,1,0:T(8,128)(2,1)S(1)}, u32[]{:S(2)}, u32[]{:S(2)}) async-start(bf16[16,72,1536]{2,1,0:T(8,128)(2,1)} %bitcast.66), calls=%async_computation | async-start | bytes 7077888 | tf_op jit(solution)/shard_map/all_to_all | solution.py:401
  16.1 2.7 %copy-start.2 = (bf16[3072,1024]{1,0:T(8,128)(2,1)}, bf16[3072,1024]{1,0:T(8,128)(2,1)S(1)}, u32[]{:S(2)}) copy-start(bf16[3072,1024]{1,0:T(8,128)(2,1)S(1)} %get-tuple-element.33.refs_3_) | copy-start | bytes 18874372
  18.7 2.6 %copy-start.6 = (bf16[1024,3072]{1,0:T(8,128)(2,1)}, bf16[1024,3072]{1,0:T(8,128)(2,1)S(1)}, u32[]{:S(2)}) copy-start(bf16[1024,3072]{1,0:T(8,128)(2,1)S(1)} %get-tuple-element.34.refs_4_) | copy-start | bytes 18874372
  57.1 11.9 %collective-permute-start = (bf16[2,576,1536]{2,1,0:T(8,128)(2,1)S(1)}, bf16[2,576,1536]{2,1,0:T(8,128)(2,1)}, u32[]{:S(2)}, u32[]{:S(2)}) collective-permute-start(bf16[2,576,1536]{2,1,0:T(8,128)(2,1)S(1)} %bitcast.59), channel_id=1, source_target_pairs={{0,1},{1,0},{2,3},{3,2},{4,5},{5,4},{6,7},{7,6},{8,9},{9,8},{10,11... | collective-permute-start | bytes 10616840 | tf_op jit(solution)/shard_map/ppermute | solution.py:398
  57.1 37.9 %all-to-all-start.1 = ((bf16[16,72,768]{2,1,0:T(8,128)(2,1)}), bf16[16,72,768]{2,1,0:T(8,128)(2,1)}, u32[]{:S(2)}, u32[]{:S(2)}) async-start(bf16[16,72,768]{2,1,0:T(8,128)(2,1)} %bitcast.68), calls=%async_computation.1 | async-start | bytes 3538944 | tf_op jit(solution)/shard_map/all_to_all | solution.py:401
  69.1 2.8 %copy-start.3 = (bf16[3072,1024]{1,0:T(8,128)(2,1)S(1)}, bf16[3072,1024]{1,0:T(8,128)(2,1)}, u32[]{:S(2)}) copy-start(bf16[3072,1024]{1,0:T(8,128)(2,1)} %copy-done.2) | copy-start | bytes 18874372
  71.8 5.8 %copy-start.7 = (bf16[1024,3072]{1,0:T(8,128)(2,1)S(1)}, bf16[1024,3072]{1,0:T(8,128)(2,1)}, u32[]{:S(2)}) copy-start(bf16[1024,3072]{1,0:T(8,128)(2,1)} %copy-done.6) | copy-start | bytes 18874372
  87.8 7.3 %collective-permute-start.1 = (bf16[2,576,768]{2,1,0:T(8,128)(2,1)}, bf16[2,576,768]{2,1,0:T(8,128)(2,1)}, u32[]{:S(2)}, u32[]{:S(2)}) collective-permute-start(bf16[2,576,768]{2,1,0:T(8,128)(2,1)} %get-tuple-element.38), channel_id=1, source_target_pairs={{0,1},{1,0},{2,3},{3,2},{4,5},{5,4},{6,7},{7,6},{8,9},{9,8},{10,11... | collective-permute-start | bytes 5308424 | tf_op jit(solution)/shard_map/ppermute | solution.py:398
  95.1 1.5 copy-start.10
  95.1 16.6 %collective-permute-start.2 = (bf16[2,576,768]{2,1,0:T(8,128)(2,1)}, bf16[2,576,768]{2,1,0:T(8,128)(2,1)S(1)}, u32[]{:S(2)}, u32[]{:S(2)}) collective-permute-start(bf16[2,576,768]{2,1,0:T(8,128)(2,1)} %landed.1.refs_1_), channel_id=1, source_target_pairs={{0,1},{1,0},{2,3},{3,2},{4,5},{5,4},{6,7},{7,6},{8,9},{9,8},{10,11... | collective-permute-start | bytes 5308424 | tf_op jit(solution)/shard_map/ppermute | solution.py:398
  99.7 6.0 %copy-start.13 = (s32[1,2]{1,0:T(1,128)S(1)}, s32[1,2]{1,0:T(1,128)}, u32[]{:S(2)}) copy-start(s32[1,2]{1,0:T(1,128)} %param.11) | copy-start | bytes 28
  99.7 10.4 %copy-start.12 = (s32[1,2,128,2]{2,3,1,0:T(2,128)S(1)}, s32[1,2,128,2]{2,3,1,0:T(2,128)}, u32[]{:S(2)}) copy-start(s32[1,2,128,2]{2,3,1,0:T(2,128)} %param.9) | copy-start | bytes 6148
  99.7 10.4 %copy-start.15 = (f32[1,2,128,2]{2,3,1,0:T(2,128)S(1)}, f32[1,2,128,2]{2,3,1,0:T(2,128)}, u32[]{:S(2)}) copy-start(f32[1,2,128,2]{2,3,1,0:T(2,128)} %param.10) | copy-start | bytes 6148
  99.7 29.9 %all-to-all-start.2 = ((bf16[16,72,768]{2,1,0:T(8,128)(2,1)}), bf16[16,72,768]{2,1,0:T(8,128)(2,1)S(1)}, u32[]{:S(2)}, u32[]{:S(2)}) async-start(bf16[16,72,768]{2,1,0:T(8,128)(2,1)} %bitcast.70), calls=%async_computation.2 | async-start | bytes 3538944 | tf_op jit(solution)/shard_map/all_to_all | solution.py:401
  111.7 19.9 %copy-start.8 = (bf16[2,576,768]{2,1,0:T(8,128)(2,1)}, bf16[2,576,768]{2,1,0:T(8,128)(2,1)S(1)}, u32[]{:S(2)}) copy-start(bf16[2,576,768]{2,1,0:T(8,128)(2,1)S(1)} %collective-permute-done.2.refs_2_) | copy-start | bytes 5308420
  129.6 1.1 copy-start.11
  129.6 1.1 copy-start.14
  131.6 9.1 %collective-permute-start.3 = (bf16[128,768]{1,0:T(8,128)(2,1)S(1)}, bf16[128,768]{1,0:T(8,128)(2,1)S(1)}, u32[]{:S(2)}, u32[]{:S(2)}) collective-permute-start(bf16[128,768]{1,0:T(8,128)(2,1)S(1)} %fusion.1), channel_id=1, source_target_pairs={{0,224},{32,0},{64,32},{96,64},{128,96},{160,128},{192,160},{224,1... | collective-permute-start | bytes 589832 | tf_op jit(solution)/shard_map/ppermute | solution.py:419
  142.5 25.6 %all-to-all-start.3 = ((bf16[16,72,768]{2,1,0:T(8,128)(2,1)}), bf16[16,72,768]{2,1,0:T(8,128)(2,1)}, u32[]{:S(2)}, u32[]{:S(2)}) async-start(bf16[16,72,768]{2,1,0:T(8,128)(2,1)} %bitcast.27), calls=%async_computation.3 | async-start | bytes 3538944 | tf_op jit(solution)/shard_map/all_to_all | solution.py:401
  148.1 7.5 %copy-start.9 = (bf16[2,576,768]{2,1,0:T(8,128)(2,1)S(1)}, bf16[2,576,768]{2,1,0:T(8,128)(2,1)}, u32[]{:S(2)}) copy-start(bf16[2,576,768]{2,1,0:T(8,128)(2,1)} %copy-done.8) | copy-start | bytes 5308420
  153.0 2.7 %copy-start.4 = (bf16[1024,3072]{1,0:T(8,128)(2,1)}, bf16[1024,3072]{1,0:T(8,128)(2,1)S(1)}, u32[]{:S(2)}) copy-start(bf16[1024,3072]{1,0:T(8,128)(2,1)S(1)} %get-tuple-element.49.down) | copy-start | bytes 18874372
  161.1 2.6 %copy-start = (bf16[3072,1024]{1,0:T(8,128)(2,1)}, bf16[3072,1024]{1,0:T(8,128)(2,1)S(1)}, u32[]{:S(2)}) copy-start(bf16[3072,1024]{1,0:T(8,128)(2,1)S(1)} %get-tuple-element.41.refs_3_.up) | copy-start | bytes 18874372
  168.1 6.4 %collective-permute-start.4 = (bf16[2,576,768]{2,1,0:T(8,128)(2,1)}, bf16[2,576,768]{2,1,0:T(8,128)(2,1)S(1)}, u32[]{:S(2)}, u32[]{:S(2)}) collective-permute-start(bf16[2,576,768]{2,1,0:T(8,128)(2,1)} %bitcast.28.mine), channel_id=1, source_target_pairs={{0,1},{1,0},{2,3},{3,2},{4,5},{5,4},{6,7},{7,6},{8,9},{9,8},{10,11... | collective-permute-start | bytes 5308424 | tf_op jit(solution)/shard_map/ppermute | solution.py:398
  168.1 2.8 %copy-start.5 = (bf16[1024,3072]{1,0:T(8,128)(2,1)S(1)}, bf16[1024,3072]{1,0:T(8,128)(2,1)}, u32[]{:S(2)}) copy-start(bf16[1024,3072]{1,0:T(8,128)(2,1)} %copy-done.4) | copy-start | bytes 18874372
  170.9 3.7 %copy-start.1 = (bf16[3072,1024]{1,0:T(8,128)(2,1)S(1)}, bf16[3072,1024]{1,0:T(8,128)(2,1)}, u32[]{:S(2)}) copy-start(bf16[3072,1024]{1,0:T(8,128)(2,1)} %copy-done) | copy-start | bytes 18874372
  180.0 4.1 %collective-permute-start.5 = (bf16[2,576,768]{2,1,0:T(8,128)(2,1)S(1)}, bf16[2,576,768]{2,1,0:T(8,128)(2,1)S(1)}, u32[]{:S(2)}, u32[]{:S(2)}) collective-permute-start(bf16[2,576,768]{2,1,0:T(8,128)(2,1)S(1)} %get-tuple-element.52), channel_id=1, source_target_pairs={{0,1},{1,0},{2,3},{3,2},{4,5},{5,4},{6,7},{7,6},{8,9},{9,8},{10,11... | collective-permute-start | bytes 5308424 | tf_op jit(solution)/shard_map/ppermute | solution.py:398
  185.9 32.1 %all-to-all-start.4 = ((bf16[16,72,768]{2,1,0:T(8,128)(2,1)}), bf16[16,72,768]{2,1,0:T(8,128)(2,1)S(1)}, u32[]{:S(2)}, u32[]{:S(2)}) async-start(bf16[16,72,768]{2,1,0:T(8,128)(2,1)} %bitcast.29), calls=%async_computation.4 | async-start | bytes 3538944 | tf_op jit(solution)/shard_map/all_to_all | solution.py:401
  219.1 6.4 %collective-permute-start.6 = (bf16[128,768]{1,0:T(8,128)(2,1)S(1)}, bf16[128,768]{1,0:T(8,128)(2,1)S(1)}, u32[]{:S(2)}, u32[]{:S(2)}) collective-permute-start(bf16[128,768]{1,0:T(8,128)(2,1)S(1)} %add_convert_fusion.2), channel_id=1, source_target_pairs={{0,224},{32,0},{64,32},{96,64},{128,96},{160,128},{192,160},{224,1... | collective-permute-start | bytes 589832 | tf_op jit(solution)/shard_map/ppermute | solution.py:419

commit v7 on v6

--- a/solution.py
+++ b/solution.py
@@ -8,7 +8,7 @@
 EXPERTS = 4
 CAPACITY = 72
 HIDDEN_BLOCK = 256
-VMEM_LIMIT = 18 * 1024 * 1024
+VMEM_LIMIT = 22 * 1024 * 1024
 
 
 def together(*values):
@@ -38,36 +38,6 @@
         cost_estimate=pl.CostEstimate(flops=flops, transcendentals=0, bytes_accessed=1000),
         name=name,
     )(core, *far, *near)
-
-
-def stage_kernel(up, down, up_out, down_out, semaphores):
-    pieces = semaphores.shape[0] // 2
-    copies = []
-    for source, target in ((up, up_out), (down, down_out)):
-        step = source.shape[0] // pieces
-        for piece in range(pieces):
-            part = pl.ds(piece * step, step)
-            copies.append(
-                pltpu.make_async_copy(
-                    source.at[part], target.at[part], semaphores.at[len(copies)]
-                )
-            )
-            copies[-1].start()
-    for copy in copies:
-        copy.wait()
-
-
-def stage(up, down, name):
-    return pl.pallas_call(
-        stage_kernel,
-        out_shape=(pltpu.VMEM(up.shape, up.dtype), pltpu.VMEM(down.shape, down.dtype)),
-        in_specs=[HBM_SPEC, HBM_SPEC],
-        out_specs=(VMEM_SPEC, VMEM_SPEC),
-        scratch_shapes=[pltpu.SemaphoreType.DMA((8,))],
-        compiler_params=pltpu.CompilerParams(vmem_limit_bytes=1024 * 1024),
-        cost_estimate=pl.CostEstimate(flops=1000, transcendentals=0, bytes_accessed=1000),
-        name=name,
-    )(up, down)
 
 
 def row_copies(sources, column, rows_buf, semaphores):
@@ -96,23 +66,30 @@
     return [slice(start, start + HIDDEN_BLOCK) for start in range(0, hidden, HIDDEN_BLOCK)]
 
 
-def factor_kernel(column, core_ref, mine, other, up, out, rows_buf, semaphores):
+def factor_kernel(column, core_ref, mine, other, up, out, rows_buf, up_buf, semaphores):
+    pieces, _, quarter = rows_buf.shape
     copies = row_copies((mine, other), column, rows_buf, semaphores)
-    pieces, _, quarter = rows_buf.shape
-    for copy in copies:
-        copy.wait()
-    for block in hidden_blocks(up.shape[1]):
-        pre = None
-        for number in range(pieces):
-            first = first_feature(number, pieces // 2, core_ref[0], quarter)
+    for number in range(pieces):
+        first = first_feature(number, pieces // 2, core_ref[0], quarter)
+        copies.append(
+            pltpu.make_async_copy(
+                up.at[pl.ds(first, quarter), :], up_buf.at[number], semaphores.at[pieces + number]
+            )
+        )
+        copies[-1].start()
+    for number in range(pieces):
+        copies[number].wait()
+        copies[pieces + number].wait()
+        for block in hidden_blocks(up.shape[1]):
             part = jnp.dot(
-                rows_buf[number],
-                up[pl.ds(first, quarter), block],
-                preferred_element_type=jnp.float32,
+                rows_buf[number], up_buf[number, :, block], preferred_element_type=jnp.float32
             )
-            pre = part if pre is None else pre + part
-        sigma = jax.nn.sigmoid(pre)
-        out[:, block] = sigma * (1.0 + pre * (1.0 - sigma))
+            if number:
+                part = out[:, block] + part
+            if number + 1 == pieces:
+                sigma = jax.nn.sigmoid(part)
+                part = sigma * (1.0 + part * (1.0 - sigma))
+            out[:, block] = part
 
 
 def factor(core, saved, up):
@@ -124,24 +101,36 @@
         lambda *refs: factor_kernel(column, *refs),
         "factor",
         core,
-        [mine, other],
-        [up],
+        [mine, other, up],
+        [],
         [(pltpu.VMEM((rows, hidden), jnp.float32), VMEM_SPEC)],
         [
             pltpu.VMEM((pieces, rows, width // pieces), jnp.bfloat16),
-            pltpu.SemaphoreType.DMA((pieces,)),
+            pltpu.VMEM((pieces, width // pieces, hidden), jnp.bfloat16),
+            pltpu.SemaphoreType.DMA((2 * pieces,)),
         ],
     )[0]
 
 
-def add_act(rows_buf, numbers, core, down, block):
-    act = None
-    halves = down.shape[1] // rows_buf.shape[2] // 2
+def act_sums(sources, column, numbers, core, down, rows_buf, down_buf, semaphores):
+    quarter = rows_buf.shape[2]
+    copies = row_copies(sources, column, rows_buf, semaphores)
+    count = len(numbers)
     for slot, number in enumerate(numbers):
-        first = first_feature(number, halves, core, rows_buf.shape[2])
-        part = contract_last(rows_buf[slot], down[block, pl.ds(first, rows_buf.shape[2])])
-        act = part if act is None else act + part
-    return act
+        first = first_feature(number, sources[0].shape[0], core, quarter)
+        copies.append(
+            pltpu.make_async_copy(
+                down.at[:, pl.ds(first, quarter)],
+                down_buf.at[slot],
+                semaphores.at[count + slot],
+            )
+        )
+        copies[-1].start()
+    for slot in range(count):
+        copies[slot].wait()
+        copies[count + slot].wait()
+        for block in hidden_blocks(down.shape[0]):
+            yield slot, block, contract_last(rows_buf[slot], down_buf[slot, block, :])
 
 
 def branch_parts(numbers, core, grad_pre, up, results, targets, semaphores):
@@ -161,20 +150,29 @@
 
 
 def branch_kernel(
-    column, core_ref, mine, other, up, down, factors, send, keep, rows_buf, grad_pre, results,
-    semaphores, out_semaphores,
+    column, core_ref, mine, other, down, up, factors, send, keep, rows_buf, down_buf, acc,
+    grad_pre, results, semaphores, out_semaphores,
 ):
-    copies = row_copies((mine, other), column, rows_buf, semaphores)
     pieces = rows_buf.shape[0]
     halves = pieces // 2
-    for copy in copies:
-        copy.wait()
-    for block in hidden_blocks(down.shape[0]):
-        act = add_act(rows_buf, range(pieces), core_ref[0], down, block)
-        grad_pre[:, block] = (act * factors[:, block]).astype(jnp.bfloat16)
+    for slot, block, part in act_sums(
+        (mine, other), column, range(pieces), core_ref[0], down, rows_buf, down_buf, semaphores
+    ):
+        total = acc[:, block] + part if slot else part
+        if slot + 1 < pieces:
+            acc[:, block] = total
+        else:
+            grad_pre[:, block] = (total * factors[:, block]).astype(jnp.bfloat16)
     numbers = [halves + n for n in range(halves)] + list(range(halves))
     targets = [send.at[n] for n in range(halves)] + [keep.at[n] for n in range(halves)]
     branch_parts(numbers, core_ref[0], grad_pre, up, results, targets, out_semaphores)
+
+
+def act_buffers(pieces, rows, quarter, hidden):
+    return [
+        pltpu.VMEM((pieces, rows, quarter), jnp.bfloat16),
+        pltpu.VMEM((pieces, hidden, quarter), jnp.bfloat16),
+    ]
 
 
 def branch(core, grads, up, down, factors):
@@ -188,27 +186,28 @@
         lambda *refs: branch_kernel(column, *refs),
         "branch",
         core,
-        [mine, other],
-        [up, down, factors],
+        [mine, other, down],
+        [up, factors],
         [
             (jax.ShapeDtypeStruct(part, jnp.bfloat16), HBM_SPEC),
             (pltpu.HBM(part, jnp.bfloat16), HBM_SPEC),
         ],
-        [
-            pltpu.VMEM((pieces, rows, quarter), jnp.bfloat16),
+        act_buffers(pieces, rows, quarter, hidden)
+        + [
+            pltpu.VMEM((rows, hidden), jnp.float32),
             pltpu.VMEM((rows, hidden), jnp.bfloat16),
             pltpu.VMEM((pieces, rows, quarter), jnp.bfloat16),
-            pltpu.SemaphoreType.DMA((pieces,)),
+            pltpu.SemaphoreType.DMA((2 * pieces,)),
             pltpu.SemaphoreType.DMA((pieces,)),
         ],
     )
 
 
-def own_act_kernel(core_ref, mine, down, out, rows_buf, semaphores):
-    for copy in row_copies((mine,), 0, rows_buf, semaphores):
-        copy.wait()
-    for block in hidden_blocks(down.shape[0]):
-        out[:, block] = add_act(rows_buf, range(rows_buf.shape[0]), core_ref[0], down, block)
+def own_act_kernel(core_ref, mine, down, out, rows_buf, down_buf, semaphores):
+    for slot, block, part in act_sums(
+        (mine,), 0, range(mine.shape[0]), core_ref[0], down, rows_buf, down_buf, semaphores
+    ):
+        out[:, block] = out[:, block] + part if slot else part
 
 
 def own_act(core, mine, down):
@@ -217,47 +216,50 @@
         own_act_kernel,
         "own_act",
         core,
-        [mine],
-        [down],
+        [mine, down],
+        [],
         [(pltpu.VMEM((rows, down.shape[0]), jnp.float32), VMEM_SPEC)],
-        [
-            pltpu.VMEM((halves, rows, quarter), jnp.bfloat16),
-            pltpu.SemaphoreType.DMA((halves,)),
-        ],
+        act_buffers(halves, rows, quarter, down.shape[0])
+        + [pltpu.SemaphoreType.DMA((2 * halves,))],
     )[0]
 
 
 def sent_kernel(
-    core_ref, other, up, down, own, factors, grad_pre, send, rows_buf, results, semaphores,
-    out_semaphores,
+    core_ref, other, down, up, own, factors, grad_pre, send, rows_buf, down_buf, acc, results,
+    semaphores, out_semaphores,
 ):
     halves = rows_buf.shape[0]
     late = [halves + n for n in range(halves)]
-    for copy in row_copies((other,), 0, rows_buf, semaphores):
-        copy.wait()
-    for block in hidden_blocks(down.shape[0]):
-        act = own[:, block] + add_act(rows_buf, late, core_ref[0], down, block)
-        grad_pre[:, block] = (act * factors[:, block]).astype(jnp.bfloat16)
+    for slot, block, part in act_sums(
+        (other,), 0, late, core_ref[0], down, rows_buf, down_buf, semaphores
+    ):
+        total = (acc if slot else own)[:, block] + part
+        if slot + 1 < halves:
+            acc[:, block] = total
+        else:
+            grad_pre[:, block] = (total * factors[:, block]).astype(jnp.bfloat16)
     targets = [send.at[n] for n in range(halves)]
     branch_parts(late, core_ref[0], grad_pre, up, results, targets, out_semaphores)
 
 
 def sent_part(core, other, up, down, own, factors):
     halves, rows, quarter = other.shape
+    hidden = down.shape[0]
     return local_kernel(
         sent_kernel,
         "sent_part",
         core,
-        [other],
-        [up, down, own, factors],
+        [other, down],
+        [up, own, factors],
         [
-            (pltpu.VMEM((rows, down.shape[0]), jnp.bfloat16), VMEM_SPEC),
+            (pltpu.VMEM((rows, hidden), jnp.bfloat16), VMEM_SPEC),
             (jax.ShapeDtypeStruct(other.shape, jnp.bfloat16), HBM_SPEC),
         ],
-        [
+        act_buffers(halves, rows, quarter, hidden)
+        + [
+            pltpu.VMEM((rows, hidden), jnp.float32),
             pltpu.VMEM((halves, rows, quarter), jnp.bfloat16),
-            pltpu.VMEM((halves, rows, quarter), jnp.bfloat16),
-            pltpu.SemaphoreType.DMA((halves,)),
+            pltpu.SemaphoreType.DMA((2 * halves,)),
             pltpu.SemaphoreType.DMA((halves,)),
         ],
     )
@@ -390,8 +392,9 @@
     per_expert = n_expert // EXPERTS
     peers = n_xhi * n_expert
     rows, quarter = grad_in.shape[1:]
-    up_local = pltpu.with_memory_space_constraint(up_weight[0], pltpu.HBM)
-    down_local = pltpu.with_memory_space_constraint(down_weight[0], pltpu.HBM)
+    up_near = up_weight[0]
+    up_far = pltpu.with_memory_space_constraint(up_near, pltpu.HBM)
+    down_far = pltpu.with_memory_space_constraint(down_weight[0], pltpu.HBM)
     core = lax.axis_index("core").astype(jnp.int32).reshape(1)
 
     def swap_cores(value):
@@ -440,44 +443,39 @@
         return pick(tick, micros, routes_by_choice, values, n_xhi, per_expert)
 
     both = deliver(pick_rows(0, (saved_all, True), (current[None], False)))
-    up_near, down_near = stage(up_local, down_local, "stage_first")
-    both, up_near, down_near = together(both, up_near, down_near)
     later = None
     if ticks > 1:
         saved_sent, both = together(pick_rows(1, (saved_all, True)), both)
         later = deliver(saved_sent)
     swapped = swap_cores(both)
-    factors = factor(core, (both, swapped, 0), up_near)
-    send, keep = branch(core, (both, swapped, 1), up_near, down_near, factors)
+    factors = factor(core, (both, swapped, 0), up_far)
+    send, keep = branch(core, (both, swapped, 1), up_near, down_far, factors)
     for tick in range(ticks):
         got = swap_cores(send)
         if tick + 1 < ticks:
             keep, later = together(keep, landed(later))
         partial_rows = (keep.astype(jnp.float32) + got.astype(jnp.float32)).astype(jnp.bfloat16)
-        arrived = exchange(partial_rows.reshape(peers, CAPACITY, quarter))
+        partial_rows = partial_rows.reshape(peers, CAPACITY, quarter)
+        if tick + 1 < ticks:
+            partial_rows, later = together(partial_rows, later)
+        arrived = exchange(partial_rows)
         _, mixing = slots_of(tick)
         if tick + 1 == ticks:
             return combine(current, mixing, arrived)[None]
-        later_swapped = swap_cores(later)
+        factors = factor(core, (later, swap_cores(later), 0), up_far)
         hit, _ = slots_of(tick + 1)
         picks = jnp.broadcast_to(
             hit[None, :, None], (n_xhi, EXPERTS, per_expert, CAPACITY, rows)
         ).reshape(peers * CAPACITY, rows)
-        arrived, later_swapped, picks = together(arrived, later_swapped, picks)
+        arrived, factors, picks = together(arrived, factors, picks)
         current = combine(current, mixing, arrived)
         grad_sent = jnp.dot(
             picks.astype(jnp.bfloat16), current, preferred_element_type=jnp.float32
         ).astype(jnp.bfloat16)
-        grad_sent, later, later_swapped = together(
-            grad_sent.reshape(peers, CAPACITY, quarter), later, later_swapped
-        )
-        grad_rows = deliver(grad_sent)
-        up_near, down_near = stage(up_local, down_local, "stage_next")
-        factors = factor(core, (later, later_swapped, 0), up_near)
-        grad_rows, factors, down_near = together(grad_rows, factors, down_near)
+        grad_rows = deliver(grad_sent.reshape(peers, CAPACITY, quarter))
         swapped = swap_cores(grad_rows)
-        own = own_act(core, grad_rows, down_near)
-        grad_pre, send = sent_part(core, swapped, up_near, down_near, own, factors)
+        own = own_act(core, grad_rows, down_far)
+        grad_pre, send = sent_part(core, swapped, up_near, down_far, own, factors)
         keep = kept_part(core, up_near, grad_pre, send.shape)
 
 

time: 227 us -> 228 us (level)
  blocking collectives: 0 us -> 27.7 us
  local copies, waits for them, and re-layouts: 19.7 us -> 5.54 us
  starting transfers between devices: 47.1 us -> 41.2 us
    all_to_all x0 -> x1, blocking collectives: none -> 27.7 us  [exchange(): lax.all_to_all(value, ('xhi', 'expert'), split_axis=0, concat_axis=0, til...]
    unnamed x33 -> x23, local copies, waits for them, and re-layouts: 18.2 us -> 4.87 us
    pallas_call x2 -> x0, Pallas kernels: 9.52 us -> none  [stage(): pl.pallas_call(stage_kernel, out_shape=(pltpu.VMEM(up.shape, up.dtype), p...]
    pallas_call x6, Pallas kernels: 33.7 us -> 41.2 us  [local_kernel(): pl.pallas_call(kernel, out_shape=tuple((shape for shape, _ in outs)), in_...]
    all_to_all x5 -> x4, starting transfers between devices: 37 us -> 30.7 us  [exchange(): lax.all_to_all(value, ('xhi', 'expert'), split_axis=0, concat_axis=0, til...]
    all_to_all x5 -> x4, waiting for transfers between devices: 88 us -> 86.5 us  [exchange(): lax.all_to_all(value, ('xhi', 'expert'), split_axis=0, concat_axis=0, til...]
  transfers between devices with their start and end apart: 12 -> 11, of which waited for: 8 -> 7; matrix products, arithmetic and copies ran while one was open for 2% -> 0% of each run, Pallas kernels for 18% -> 16%
where the time goes in v7:
time: 228 us
  waiting for transfers between devices  93 us (41%)
  Pallas kernels  48.5 us (21%)
  starting transfers between devices  41.2 us (18%)
  blocking collectives  27.7 us (12%)
  local copies, waits for them, and re-layouts  5.54 us (2%)
  other arithmetic  5.5 us (2%)
  between operations  3.9 us (2%)
  matrix products  2.57 us (1%)
    all_to_all x4, waiting for transfers between devices, exchange(): lax.all_to_all(value, ('xhi', 'expert'), split_axis=0, concat_axis=0, til...  86.5 us
    pallas_call x6, Pallas kernels, local_kernel(): pl.pallas_call(kernel, out_shape=tuple((shape for shape, _ in outs)), in_...  41.2 us
    all_to_all x4, starting transfers between devices, exchange(): lax.all_to_all(value, ('xhi', 'expert'), split_axis=0, concat_axis=0, til...  30.7 us
    all_to_all x1, blocking collectives, exchange(): lax.all_to_all(value, ('xhi', 'expert'), split_axis=0, concat_axis=0, til...  27.7 us
    ppermute x2, starting transfers between devices, combine(): lax.ppermute(result, 'section', [(i, (i - 1) % n_section) for i in range(...  9.72 us
    pallas_call x2, Pallas kernels, pick(): pl.pallas_call(pick_kernel, out_shape=jax.ShapeDtypeStruct((n_xhi, EXPERT...  7.3 us
    ppermute x2, waiting for transfers between devices, combine(): lax.ppermute(result, 'section', [(i, (i - 1) % n_section) for i in range(...  6.38 us
    unnamed x23, local copies, waits for them, and re-layouts  4.87 us
  transfers between devices with their start and end apart: 11, of which 7 were waited for; matrix products, arithmetic and copies ran while one was open for 0% of the time, Pallas kernels for 16%

profile of v7, /device:TPU:8, one launch (start us, length us, event | category | flops | bytes accessed | tf_op | source)
XLA Modules:
  0.0 227.9 jit_solution(3050151841981823427)
XLA Ops:
  0.0 4.0 %pick.3 = bf16[2,4,2,72,1536]{4,3,2,1,0:T(8,128)(2,1)} custom-call(s32[2]{0:T(128)} %bitcast.83, s32[2,2,128]{2,1,0:T(2,128)} %bitcast.81, bf16[2,128,768]{2,1,0:T(8,128)(2,1)} %bitcast.77, bf16[1,128,768]{2,1,0:T(8,128)(2,1)} %refs_1_.1), custom_call_target="tpu_custom_call" | custom-call | tf_op jit(solution)/shard_map/pick/pallas_call | solution.py:336
  4.0 7.4 %all-to-all-start = ((bf16[16,72,1536]{2,1,0:T(8,128)(2,1)}), bf16[16,72,1536]{2,1,0:T(8,128)(2,1)}, u32[]{:S(2)}, u32[]{:S(2)}) async-start(bf16[16,72,1536]{2,1,0:T(8,128)(2,1)} %bitcast.73), calls=%async_computation | async-start | bytes 7077888 | tf_op jit(solution)/shard_map/all_to_all | solution.py:404
  11.4 3.3 %pick.2 = bf16[2,4,2,72,768]{4,3,2,1,0:T(8,128)(2,1)} custom-call(s32[2]{0:T(128)} %bitcast.84, s32[2,2,128]{2,1,0:T(2,128)} %bitcast.82, bf16[2,128,768]{2,1,0:T(8,128)(2,1)} %bitcast.78), custom_call_target="tpu_custom_call" | custom-call | tf_op jit(solution)/shard_map/pick/pallas_call | solution.py:336
  14.7 42.5 %all-to-all-done = bf16[16,72,1536]{2,1,0:T(8,128)(2,1)} async-done(((bf16[16,72,1536]{2,1,0:T(8,128)(2,1)}), bf16[16,72,1536]{2,1,0:T(8,128)(2,1)}, u32[]{:S(2)}, u32[]{:S(2)}) %all-to-all-start) | async-done | bytes 3538976 | tf_op jit(solution)/shard_map/all_to_all | solution.py:404
  57.2 0.0 collective-permute-start
  57.2 0.0 slice-start
  57.2 12.1 %all-to-all-start.1 = ((bf16[16,72,768]{2,1,0:T(8,128)(2,1)}), bf16[16,72,768]{2,1,0:T(8,128)(2,1)}, u32[]{:S(2)}, u32[]{:S(2)}) async-start(bf16[16,72,768]{2,1,0:T(8,128)(2,1)} %bitcast.74), calls=%async_computation.1 | async-start | bytes 3538944 | tf_op jit(solution)/shard_map/all_to_all | solution.py:404
  69.3 0.0 collective-permute-done.refs_2_
  69.3 0.0 slice-start.1
  69.3 8.2 %factor.2.refs_5_ = f32[576,1024]{1,0:T(8,128)S(1)} custom-call(s32[1]{0:T(128)} %bitcast.6.refs_0_.core_ref, bf16[2,576,1536]{2,1,0:T(8,128)(2,1)} %bitcast.14.refs_1_, bf16[2,576,1536]{2,1,0:T(8,128)(2,1)} %collective-permute-done.refs_2_, bf16[3072,1024]{1,0:T(8,128)(2,1)} %bitcast.59), custom_call_target="tpu_custom_call" | custom-call | flops 1000 | bytes 1000 | tf_op jit(solution)/shard_map/factor/pallas_call | solution.py:29
  77.6 0.0 slice-done
  77.6 0.0 slice-done.1
  77.6 11.7 %branch.1 = (bf16[2,576,768]{2,1,0:T(8,128)(2,1)}, bf16[2,576,768]{2,1,0:T(8,128)(2,1)}) custom-call(s32[1]{0:T(128)} %bitcast.6.refs_0_.core_ref, bf16[2,576,1536]{2,1,0:T(8,128)(2,1)} %bitcast.14.refs_1_, bf16[2,576,1536]{2,1,0:T(8,128)(2,1)} %collective-permute-done.refs_2_, bf16[1024,3072]{1,0:T(8,128)(2,1)} %bitcast.70, ...), custom_call_target="tpu_custom_call" | custom-call | flops 1000 | bytes 1000 | tf_op jit(solution)/shard_map/branch/pallas_call | solution.py:29
  89.3 0.1 collective-permute-start.1
  89.4 5.9 %all-to-all-done.1 = bf16[16,72,768]{2,1,0:T(8,128)(2,1)} async-done(((bf16[16,72,768]{2,1,0:T(8,128)(2,1)}), bf16[16,72,768]{2,1,0:T(8,128)(2,1)}, u32[]{:S(2)}, u32[]{:S(2)}) %all-to-all-start.1) | async-done | bytes 1769504 | tf_op jit(solution)/shard_map/all_to_all | solution.py:404
  95.3 0.0 copy-start.2
  95.3 0.0 collective-permute-done.1
  95.3 1.5 copy-done.2
  96.8 1.6 add_convert_fusion.1
  98.4 0.0 copy-start.5
  98.4 0.0 copy-start.4
  98.4 0.0 copy-start.6
  98.4 0.0 collective-permute-start.2
  98.4 6.0 %all-to-all-start.2 = ((bf16[16,72,768]{2,1,0:T(8,128)(2,1)}), bf16[16,72,768]{2,1,0:T(8,128)(2,1)}, u32[]{:S(2)}, u32[]{:S(2)}) async-start(bf16[16,72,768]{2,1,0:T(8,128)(2,1)} %bitcast.18), calls=%async_computation.2 | async-start | bytes 3538944 | tf_op jit(solution)/shard_map/all_to_all | solution.py:404
  104.4 0.0 copy-done.5
  104.4 0.6 fusion.17
  108.7 0.0 copy-done.4
  108.7 0.0 copy-done.6
  108.8 0.1 fusion.2
  108.9 0.1 fusion.3
  109.1 0.0 collective-permute-done.2.refs_2_
  109.1 0.0 copy-start
  109.1 1.2 copy-done
  110.3 0.0 copy-start.1
  110.3 1.5 copy-done.1
  111.8 6.7 %factor.3.factors = f32[576,1024]{1,0:T(8,128)S(1)} custom-call(s32[1]{0:T(128)} %bitcast.6.refs_0_.core_ref, bf16[2,576,768]{2,1,0:T(8,128)(2,1)} %landed.1.refs_1_, bf16[2,576,768]{2,1,0:T(8,128)(2,1)S(1)} %copy-done.1, bf16[3072,1024]{1,0:T(8,128)(2,1)} %bitcast.60), custom_call_target="tpu_custom_call" | custom-call | flops 1000 | bytes 1000 | tf_op jit(solution)/shard_map/factor/pallas_call | solution.py:29
  118.4 0.0 copy-start.3
  118.5 12.1 %all-to-all-done.2 = bf16[16,72,768]{2,1,0:T(8,128)(2,1)} async-done(((bf16[16,72,768]{2,1,0:T(8,128)(2,1)}), bf16[16,72,768]{2,1,0:T(8,128)(2,1)}, u32[]{:S(2)}, u32[]{:S(2)}) %all-to-all-start.2) | async-done | bytes 1769504 | tf_op jit(solution)/shard_map/all_to_all | solution.py:404
  130.6 1.8 convert_reduce_fusion.1
  132.4 0.0 copy-done.3
  132.4 0.8 fusion.1
  133.3 5.9 %collective-permute-start.3 = (bf16[128,768]{1,0:T(8,128)(2,1)S(1)}, bf16[128,768]{1,0:T(8,128)(2,1)S(1)}, u32[]{:S(2)}, u32[]{:S(2)}) collective-permute-start(bf16[128,768]{1,0:T(8,128)(2,1)S(1)} %fusion.1), channel_id=1, source_target_pairs={{0,224},{32,0},{64,32},{96,64},{128,96},{160,128},{192,160},{224,1... | collective-permute-start | bytes 589832 | tf_op jit(solution)/shard_map/ppermute | solution.py:422
  139.2 3.2 %collective-permute-done.3 = bf16[128,768]{1,0:T(8,128)(2,1)S(1)} collective-permute-done((bf16[128,768]{1,0:T(8,128)(2,1)S(1)}, bf16[128,768]{1,0:T(8,128)(2,1)S(1)}, u32[]{:S(2)}, u32[]{:S(2)}) %collective-permute-start.3) | collective-permute-done | bytes 196640 | tf_op jit(solution)/shard_map/ppermute | solution.py:422
  142.4 0.0 slice-start.2
  142.4 0.6 convolution_convert_fusion
  143.0 27.7 %all_to_all.25 = bf16[16,72,768]{2,1,0:T(8,128)(2,1)S(1)} all-to-all(bf16[16,72,768]{2,1,0:T(8,128)(2,1)S(1)} %bitcast.76), channel_id=1, replica_groups=mesh['section'=8,'expert'=8,'xhi'=2,'core'=2] {'xhi','expert'}, dimensions={0} | all-to-all | bytes 3538944 | tf_op jit(solution)/shard_map/all_to_all | solution.py:404
  170.7 0.0 slice-start.3
  170.7 0.0 collective-permute-start.4
  170.7 4.2 %own_act.1.own = f32[576,1024]{1,0:T(8,128)S(1)} custom-call(s32[1]{0:T(128)} %bitcast.6.refs_0_.core_ref, bf16[2,576,768]{2,1,0:T(8,128)(2,1)S(1)} %bitcast.69, bf16[1024,3072]{1,0:T(8,128)(2,1)} %bitcast.71), custom_call_target="tpu_custom_call" | custom-call | flops 1000 | bytes 1000 | tf_op jit(solution)/shard_map/own_act/pallas_call | solution.py:29
  174.9 0.0 collective-permute-done.4.other
  174.9 0.0 slice-done.2
  174.9 0.0 slice-done.3
  174.9 7.2 %sent_part.1 = (bf16[576,1024]{1,0:T(8,128)(2,1)S(1)}, bf16[2,576,768]{2,1,0:T(8,128)(2,1)S(1)}) custom-call(s32[1]{0:T(128)} %bitcast.6.refs_0_.core_ref, bf16[2,576,768]{2,1,0:T(8,128)(2,1)S(1)} %collective-permute-done.4.other, bf16[1024,3072]{1,0:T(8,128)(2,1)} %bitcast.72, bf16[3072,1024]{1,0:T(8,128)(2,1)S(1)} %bitcast.66, ...), custom_call_target="tpu_custom_call" | custom-call | flops 1000 | bytes 1000 | tf_op jit(solution)/shard_map/sent_part/pallas_call | solution.py:29
  182.2 0.6 collective-permute-start.5
  182.8 3.2 %kept_part.1 = bf16[2,576,768]{2,1,0:T(8,128)(2,1)S(1)} custom-call(s32[1]{0:T(128)} %bitcast.6.refs_0_.core_ref, bf16[3072,1024]{1,0:T(8,128)(2,1)S(1)} %bitcast.67, bf16[576,1024]{1,0:T(8,128)(2,1)S(1)} %get-tuple-element.29.grad_pre), custom_call_target="tpu_custom_call" | custom-call | flops 10000000000 | bytes 1000 | tf_op jit(solution)/shard_map/kept_part/pallas_call | solution.py:29
  186.0 0.2 collective-permute-done.5
  186.2 1.7 add_convert_fusion
  187.9 5.3 %all-to-all-start.4 = ((bf16[16,72,768]{2,1,0:T(8,128)(2,1)}), bf16[16,72,768]{2,1,0:T(8,128)(2,1)S(1)}, u32[]{:S(2)}, u32[]{:S(2)}) async-start(bf16[16,72,768]{2,1,0:T(8,128)(2,1)} %bitcast.29), calls=%async_computation.4 | async-start | bytes 3538944 | tf_op jit(solution)/shard_map/all_to_all | solution.py:404
  193.2 26.0 %all-to-all-done.4 = bf16[16,72,768]{2,1,0:T(8,128)(2,1)S(1)} async-done(((bf16[16,72,768]{2,1,0:T(8,128)(2,1)}), bf16[16,72,768]{2,1,0:T(8,128)(2,1)S(1)}, u32[]{:S(2)}, u32[]{:S(2)}) %all-to-all-start.4) | async-done | bytes 1769504 | tf_op jit(solution)/shard_map/all_to_all | solution.py:404
  219.2 0.2 convert_reduce_fusion
  219.4 0.8 add_convert_fusion.2
  220.3 3.8 %collective-permute-start.6 = (bf16[128,768]{1,0:T(8,128)(2,1)S(1)}, bf16[128,768]{1,0:T(8,128)(2,1)S(1)}, u32[]{:S(2)}, u32[]{:S(2)}) collective-permute-start(bf16[128,768]{1,0:T(8,128)(2,1)S(1)} %add_convert_fusion.2), channel_id=1, source_target_pairs={{0,224},{32,0},{64,32},{96,64},{128,96},{160,128},{192,160},{224,1... | collective-permute-start | bytes 589832 | tf_op jit(solution)/shard_map/ppermute | solution.py:422
  224.1 3.2 %collective-permute-done.6 = bf16[128,768]{1,0:T(8,128)(2,1)S(1)} collective-permute-done((bf16[128,768]{1,0:T(8,128)(2,1)S(1)}, bf16[128,768]{1,0:T(8,128)(2,1)S(1)}, u32[]{:S(2)}, u32[]{:S(2)}) %collective-permute-start.6) | collective-permute-done | bytes 196640 | tf_op jit(solution)/shard_map/ppermute | solution.py:422
  227.3 0.7 copy.11
  (10 shorter events, 0.1 us)
Async XLA Ops:
  4.0 53.3 %all-to-all-start = ((bf16[16,72,1536]{2,1,0:T(8,128)(2,1)}), bf16[16,72,1536]{2,1,0:T(8,128)(2,1)}, u32[]{:S(2)}, u32[]{:S(2)}) async-start(bf16[16,72,1536]{2,1,0:T(8,128)(2,1)} %bitcast.73), calls=%async_computation | async-start | bytes 7077888 | tf_op jit(solution)/shard_map/all_to_all | solution.py:404
  57.2 12.1 %collective-permute-start = (bf16[2,576,1536]{2,1,0:T(8,128)(2,1)}, bf16[2,576,1536]{2,1,0:T(8,128)(2,1)}, u32[]{:S(2)}, u32[]{:S(2)}) collective-permute-start(bf16[2,576,1536]{2,1,0:T(8,128)(2,1)} %bitcast.14.refs_1_), channel_id=1, source_target_pairs={{0,1},{1,0},{2,3},{3,2},{4,5},{5,4},{6,7},{7,6},{8,9},{9,8},{10,11... | collective-permute-start | bytes 10616840 | tf_op jit(solution)/shard_map/ppermute | solution.py:401
  57.2 20.3 %slice-start = ((s8[6291456]{0:T(1024)(128)(4,1)}), s8[2097152]{0:T(1024)(128)(4,1)S(1)}, s32[]{:S(2)}) async-start(s8[6291456]{0:T(1024)(128)(4,1)} %bitcast.61), calls=%async_computation.5 | async-start | bytes 4194304
  57.2 38.1 %all-to-all-start.1 = ((bf16[16,72,768]{2,1,0:T(8,128)(2,1)}), bf16[16,72,768]{2,1,0:T(8,128)(2,1)}, u32[]{:S(2)}, u32[]{:S(2)}) async-start(bf16[16,72,768]{2,1,0:T(8,128)(2,1)} %bitcast.74), calls=%async_computation.1 | async-start | bytes 3538944 | tf_op jit(solution)/shard_map/all_to_all | solution.py:404
  69.3 8.3 %slice-start.1 = ((s8[6291456]{0:T(1024)(128)(4,1)}), s8[4194304]{0:T(1024)(128)(4,1)S(1)}, s32[]{:S(2)}) async-start(s8[6291456]{0:T(1024)(128)(4,1)} %bitcast.61), calls=%async_computation.6 | async-start | bytes 8388608
  89.3 6.0 %collective-permute-start.1 = (bf16[2,576,768]{2,1,0:T(8,128)(2,1)}, bf16[2,576,768]{2,1,0:T(8,128)(2,1)S(1)}, u32[]{:S(2)}, u32[]{:S(2)}) collective-permute-start(bf16[2,576,768]{2,1,0:T(8,128)(2,1)} %get-tuple-element.22), channel_id=1, source_target_pairs={{0,1},{1,0},{2,3},{3,2},{4,5},{5,4},{6,7},{7,6},{8,9},{9,8},{10,11... | collective-permute-start | bytes 5308424 | tf_op jit(solution)/shard_map/ppermute | solution.py:401
  95.3 1.5 copy-start.2
  98.4 6.0 %copy-start.5 = (s32[1,2]{1,0:T(1,128)S(1)}, s32[1,2]{1,0:T(1,128)}, u32[]{:S(2)}) copy-start(s32[1,2]{1,0:T(1,128)} %param.11) | copy-start | bytes 28
  98.4 10.2 %copy-start.4 = (s32[1,2,128,2]{2,3,1,0:T(2,128)S(1)}, s32[1,2,128,2]{2,3,1,0:T(2,128)}, u32[]{:S(2)}) copy-start(s32[1,2,128,2]{2,3,1,0:T(2,128)} %param.9) | copy-start | bytes 6148
  98.4 10.3 %copy-start.6 = (f32[1,2,128,2]{2,3,1,0:T(2,128)S(1)}, f32[1,2,128,2]{2,3,1,0:T(2,128)}, u32[]{:S(2)}) copy-start(f32[1,2,128,2]{2,3,1,0:T(2,128)} %param.10) | copy-start | bytes 6148
  98.4 10.6 %collective-permute-start.2 = (bf16[2,576,768]{2,1,0:T(8,128)(2,1)}, bf16[2,576,768]{2,1,0:T(8,128)(2,1)S(1)}, u32[]{:S(2)}, u32[]{:S(2)}) collective-permute-start(bf16[2,576,768]{2,1,0:T(8,128)(2,1)} %landed.1.refs_1_), channel_id=1, source_target_pairs={{0,1},{1,0},{2,3},{3,2},{4,5},{5,4},{6,7},{7,6},{8,9},{9,8},{10,11... | collective-permute-start | bytes 5308424 | tf_op jit(solution)/shard_map/ppermute | solution.py:401
  98.4 32.1 %all-to-all-start.2 = ((bf16[16,72,768]{2,1,0:T(8,128)(2,1)}), bf16[16,72,768]{2,1,0:T(8,128)(2,1)}, u32[]{:S(2)}, u32[]{:S(2)}) async-start(bf16[16,72,768]{2,1,0:T(8,128)(2,1)} %bitcast.18), calls=%async_computation.2 | async-start | bytes 3538944 | tf_op jit(solution)/shard_map/all_to_all | solution.py:404
  109.1 1.2 copy-start
  110.3 1.5 copy-start.1
  118.4 13.9 %copy-start.3 = (bf16[1,128,768]{2,1,0:T(8,128)(2,1)S(1)}, bf16[1,128,768]{2,1,0:T(8,128)(2,1)}, u32[]{:S(2)}) copy-start(bf16[1,128,768]{2,1,0:T(8,128)(2,1)} %refs_1_.1) | copy-start | bytes 589828
  133.3 9.1 %collective-permute-start.3 = (bf16[128,768]{1,0:T(8,128)(2,1)S(1)}, bf16[128,768]{1,0:T(8,128)(2,1)S(1)}, u32[]{:S(2)}, u32[]{:S(2)}) collective-permute-start(bf16[128,768]{1,0:T(8,128)(2,1)S(1)} %fusion.1), channel_id=1, source_target_pairs={{0,224},{32,0},{64,32},{96,64},{128,96},{160,128},{192,160},{224,1... | collective-permute-start | bytes 589832 | tf_op jit(solution)/shard_map/ppermute | solution.py:422
  142.4 32.5 %slice-start.2 = ((s8[6291456]{0:T(1024)(128)(4,1)}), s8[4194304]{0:T(1024)(128)(4,1)S(1)}, s32[]{:S(2)}) async-start(s8[6291456]{0:T(1024)(128)(4,1)} %bitcast.64), calls=%async_computation.7 | async-start | bytes 8388608
  170.7 4.2 %slice-start.3 = ((s8[6291456]{0:T(1024)(128)(4,1)}), s8[2097152]{0:T(1024)(128)(4,1)S(1)}, s32[]{:S(2)}) async-start(s8[6291456]{0:T(1024)(128)(4,1)} %bitcast.64), calls=%async_computation.8 | async-start | bytes 4194304
  170.7 4.2 %collective-permute-start.4 = (bf16[2,576,768]{2,1,0:T(8,128)(2,1)S(1)}, bf16[2,576,768]{2,1,0:T(8,128)(2,1)S(1)}, u32[]{:S(2)}, u32[]{:S(2)}) collective-permute-start(bf16[2,576,768]{2,1,0:T(8,128)(2,1)S(1)} %bitcast.68), channel_id=1, source_target_pairs={{0,1},{1,0},{2,3},{3,2},{4,5},{5,4},{6,7},{7,6},{8,9},{9,8},{10,11... | collective-permute-start | bytes 5308424 | tf_op jit(solution)/shard_map/ppermute | solution.py:401
  182.2 4.0 %collective-permute-start.5 = (bf16[2,576,768]{2,1,0:T(8,128)(2,1)S(1)}, bf16[2,576,768]{2,1,0:T(8,128)(2,1)S(1)}, u32[]{:S(2)}, u32[]{:S(2)}) collective-permute-start(bf16[2,576,768]{2,1,0:T(8,128)(2,1)S(1)} %get-tuple-element.30), channel_id=1, source_target_pairs={{0,1},{1,0},{2,3},{3,2},{4,5},{5,4},{6,7},{7,6},{8,9},{9,8},{10,11... | collective-permute-start | bytes 5308424 | tf_op jit(solution)/shard_map/ppermute | solution.py:401
  187.9 31.3 %all-to-all-start.4 = ((bf16[16,72,768]{2,1,0:T(8,128)(2,1)}), bf16[16,72,768]{2,1,0:T(8,128)(2,1)S(1)}, u32[]{:S(2)}, u32[]{:S(2)}) async-start(bf16[16,72,768]{2,1,0:T(8,128)(2,1)} %bitcast.29), calls=%async_computation.4 | async-start | bytes 3538944 | tf_op jit(solution)/shard_map/all_to_all | solution.py:404
  220.3 7.0 %collective-permute-start.6 = (bf16[128,768]{1,0:T(8,128)(2,1)S(1)}, bf16[128,768]{1,0:T(8,128)(2,1)S(1)}, u32[]{:S(2)}, u32[]{:S(2)}) collective-permute-start(bf16[128,768]{1,0:T(8,128)(2,1)S(1)} %add_convert_fusion.2), channel_id=1, source_target_pairs={{0,224},{32,0},{64,32},{96,64},{128,96},{160,128},{192,160},{224,1... | collective-permute-start | bytes 589832 | tf_op jit(solution)/shard_map/ppermute | solution.py:422

commit v8 on v7

--- a/solution.py
+++ b/solution.py
@@ -131,6 +131,33 @@
         copies[count + slot].wait()
         for block in hidden_blocks(down.shape[0]):
             yield slot, block, contract_last(rows_buf[slot], down_buf[slot, block, :])
+
+
+def up_copies(up, numbers, core, up_buf, semaphores):
+    quarter = up_buf.shape[1]
+    copies = []
+    for slot, number in enumerate(numbers):
+        first = first_feature(number, up.shape[0] // quarter // 2, core, quarter)
+        copies.append(
+            pltpu.make_async_copy(
+                up.at[pl.ds(first, quarter), :], up_buf.at[slot], semaphores.at[slot]
+            )
+        )
+        copies[-1].start()
+    return copies
+
+
+def loaded_parts(copies, grad_pre, up_buf, results, targets, semaphores):
+    sent = []
+    for slot, copy in enumerate(copies):
+        copy.wait()
+        results[slot] = contract_last(grad_pre[...], up_buf[slot]).astype(jnp.bfloat16)
+        sent.append(
+            pltpu.make_async_copy(results.at[slot], targets[slot], semaphores.at[slot])
+        )
+        sent[-1].start()
+    for copy in sent:
+        copy.wait()
 
 
 def branch_parts(numbers, core, grad_pre, up, results, targets, semaphores):
@@ -225,21 +252,24 @@
 
 
 def sent_kernel(
-    core_ref, other, down, up, own, factors, grad_pre, send, rows_buf, down_buf, acc, results,
-    semaphores, out_semaphores,
+    core_ref, other, down, up, own, factors, grad_pre, send, rows_buf, down_buf, up_buf, acc,
+    results, semaphores, up_semaphores, out_semaphores,
 ):
     halves = rows_buf.shape[0]
     late = [halves + n for n in range(halves)]
+    copies = None
     for slot, block, part in act_sums(
         (other,), 0, late, core_ref[0], down, rows_buf, down_buf, semaphores
     ):
+        if copies is None:
+            copies = up_copies(up, late, core_ref[0], up_buf, up_semaphores)
         total = (acc if slot else own)[:, block] + part
         if slot + 1 < halves:
             acc[:, block] = total
         else:
             grad_pre[:, block] = (total * factors[:, block]).astype(jnp.bfloat16)
     targets = [send.at[n] for n in range(halves)]
-    branch_parts(late, core_ref[0], grad_pre, up, results, targets, out_semaphores)
+    loaded_parts(copies, grad_pre, up_buf, results, targets, out_semaphores)
 
 
 def sent_part(core, other, up, down, own, factors):
@@ -249,26 +279,29 @@
         sent_kernel,
         "sent_part",
         core,
-        [other, down],
-        [up, own, factors],
+        [other, down, up],
+        [own, factors],
         [
             (pltpu.VMEM((rows, hidden), jnp.bfloat16), VMEM_SPEC),
             (jax.ShapeDtypeStruct(other.shape, jnp.bfloat16), HBM_SPEC),
         ],
         act_buffers(halves, rows, quarter, hidden)
         + [
+            pltpu.VMEM((halves, quarter, hidden), jnp.bfloat16),
             pltpu.VMEM((rows, hidden), jnp.float32),
             pltpu.VMEM((halves, rows, quarter), jnp.bfloat16),
             pltpu.SemaphoreType.DMA((2 * halves,)),
             pltpu.SemaphoreType.DMA((halves,)),
+            pltpu.SemaphoreType.DMA((halves,)),
         ],
     )
 
 
-def kept_kernel(core_ref, up, grad_pre, keep, results, semaphores):
+def kept_kernel(core_ref, up, grad_pre, keep, up_buf, results, up_semaphores, semaphores):
     halves = keep.shape[0]
+    copies = up_copies(up, range(halves), core_ref[0], up_buf, up_semaphores)
     targets = [keep.at[n] for n in range(halves)]
-    branch_parts(range(halves), core_ref[0], grad_pre, up, results, targets, semaphores)
+    loaded_parts(copies, grad_pre, up_buf, results, targets, semaphores)
 
 
 def kept_part(core, up, grad_pre, part):
@@ -276,10 +309,15 @@
         kept_kernel,
         "kept_part",
         core,
-        [],
-        [up, grad_pre],
+        [up],
+        [grad_pre],
         [(jax.ShapeDtypeStruct(part, jnp.bfloat16), HBM_SPEC)],
-        [pltpu.VMEM(part, jnp.bfloat16), pltpu.SemaphoreType.DMA((part[0],))],
+        [
+            pltpu.VMEM((part[0], part[2], up.shape[1]), jnp.bfloat16),
+            pltpu.VMEM(part, jnp.bfloat16),
+            pltpu.SemaphoreType.DMA((part[0],)),
+            pltpu.SemaphoreType.DMA((part[0],)),
+        ],
         flops=10**10,
     )[0]
 
@@ -455,28 +493,30 @@
         if tick + 1 < ticks:
             keep, later = together(keep, landed(later))
         partial_rows = (keep.astype(jnp.float32) + got.astype(jnp.float32)).astype(jnp.bfloat16)
-        partial_rows = partial_rows.reshape(peers, CAPACITY, quarter)
-        if tick + 1 < ticks:
-            partial_rows, later = together(partial_rows, later)
-        arrived = exchange(partial_rows)
+        arrived = exchange(partial_rows.reshape(peers, CAPACITY, quarter))
         _, mixing = slots_of(tick)
         if tick + 1 == ticks:
             return combine(current, mixing, arrived)[None]
-        factors = factor(core, (later, swap_cores(later), 0), up_far)
+        later_swapped = pltpu.with_memory_space_constraint(swap_cores(later), pltpu.HBM)
         hit, _ = slots_of(tick + 1)
         picks = jnp.broadcast_to(
             hit[None, :, None], (n_xhi, EXPERTS, per_expert, CAPACITY, rows)
         ).reshape(peers * CAPACITY, rows)
-        arrived, factors, picks = together(arrived, factors, picks)
+        arrived, later_swapped, picks = together(arrived, later_swapped, picks)
         current = combine(current, mixing, arrived)
         grad_sent = jnp.dot(
             picks.astype(jnp.bfloat16), current, preferred_element_type=jnp.float32
         ).astype(jnp.bfloat16)
-        grad_rows = deliver(grad_sent.reshape(peers, CAPACITY, quarter))
+        grad_sent, later, later_swapped = together(
+            grad_sent.reshape(peers, CAPACITY, quarter), later, later_swapped
+        )
+        grad_rows = deliver(grad_sent)
+        factors = factor(core, (later, later_swapped, 0), up_far)
+        grad_rows, factors = together(grad_rows, factors)
         swapped = swap_cores(grad_rows)
         own = own_act(core, grad_rows, down_far)
-        grad_pre, send = sent_part(core, swapped, up_near, down_far, own, factors)
-        keep = kept_part(core, up_near, grad_pre, send.shape)
+        grad_pre, send = sent_part(core, swapped, up_far, down_far, own, factors)
+        keep = kept_part(core, up_far, grad_pre, send.shape)
 
 
 def solution(mesh):

time: 228 us -> 228 us (level)
  blocking collectives: 27.7 us -> 0 us
  waiting for transfers between devices: 93 us -> 111 us
  starting transfers between devices: 41.2 us -> 47.1 us
    all_to_all x1 -> x0, blocking collectives: 27.7 us -> none  [exchange(): lax.all_to_all(value, ('xhi', 'expert'), split_axis=0, concat_axis=0, til...]
    all_to_all x4 -> x5, waiting for transfers between devices: 86.5 us -> 104 us  [exchange(): lax.all_to_all(value, ('xhi', 'expert'), split_axis=0, concat_axis=0, til...]
    all_to_all x4 -> x5, starting transfers between devices: 30.7 us -> 37.1 us  [exchange(): lax.all_to_all(value, ('xhi', 'expert'), split_axis=0, concat_axis=0, til...]
  transfers between devices with their start and end apart: 11 -> 12, of which waited for: 7 -> 7; matrix products, arithmetic and copies ran while one was open for 0% -> 2% of each run, Pallas kernels for 16% -> 17%
where the time goes in v8:
time: 228 us; the launch traced here: 227 us
  waiting for transfers between devices  111 us (49%)
  Pallas kernels  50.6 us (22%)
  starting transfers between devices  47.1 us (21%)
  other arithmetic  5.96 us (3%)
  matrix products  4.39 us (2%)
  local copies, waits for them, and re-layouts  4.38 us (2%)
  between operations  4.26 us (2%)
    all_to_all x5, waiting for transfers between devices, exchange(): lax.all_to_all(value, ('xhi', 'expert'), split_axis=0, concat_axis=0, til...  104 us
    pallas_call x6, Pallas kernels, local_kernel(): pl.pallas_call(kernel, out_shape=tuple((shape for shape, _ in outs)), in_...  43.3 us
    all_to_all x5, starting transfers between devices, exchange(): lax.all_to_all(value, ('xhi', 'expert'), split_axis=0, concat_axis=0, til...  37.1 us
    ppermute x2, starting transfers between devices, combine(): lax.ppermute(result, 'section', [(i, (i - 1) % n_section) for i in range(...  9.1 us
    pallas_call x2, Pallas kernels, pick(): pl.pallas_call(pick_kernel, out_shape=jax.ShapeDtypeStruct((n_xhi, EXPERT...  7.3 us
    ppermute x2, waiting for transfers between devices, combine(): lax.ppermute(result, 'section', [(i, (i - 1) % n_section) for i in range(...  6.38 us
    convert_element_type x2, other arithmetic, per_device(): (keep.astype(jnp.float32) + got.astype(jnp.float32)).astype(jnp.bfloat16)  4.79 us
  transfers between devices with their start and end apart: 12, of which 7 were waited for; matrix products, arithmetic and copies ran while one was open for 2% of the time, Pallas kernels for 17%

profile of v8, /device:TPU:8, one launch (start us, length us, event | category | flops | bytes accessed | tf_op | source)
XLA Modules:
  0.0 227.3 jit_solution(17557014329414460842)
XLA Ops:
  0.0 4.0 %pick.3 = bf16[2,4,2,72,1536]{4,3,2,1,0:T(8,128)(2,1)} custom-call(s32[2]{0:T(128)} %bitcast.79, s32[2,2,128]{2,1,0:T(2,128)} %bitcast.77, bf16[2,128,768]{2,1,0:T(8,128)(2,1)} %bitcast.73, bf16[1,128,768]{2,1,0:T(8,128)(2,1)} %refs_1_.1), custom_call_target="tpu_custom_call" | custom-call | tf_op jit(solution)/shard_map/pick/pallas_call | solution.py:374
  4.0 7.4 %all-to-all-start = ((bf16[16,72,1536]{2,1,0:T(8,128)(2,1)}), bf16[16,72,1536]{2,1,0:T(8,128)(2,1)}, u32[]{:S(2)}, u32[]{:S(2)}) async-start(bf16[16,72,1536]{2,1,0:T(8,128)(2,1)} %bitcast.69), calls=%async_computation | async-start | bytes 7077888 | tf_op jit(solution)/shard_map/all_to_all | solution.py:442
  11.4 3.3 %pick.2 = bf16[2,4,2,72,768]{4,3,2,1,0:T(8,128)(2,1)} custom-call(s32[2]{0:T(128)} %bitcast.80, s32[2,2,128]{2,1,0:T(2,128)} %bitcast.78, bf16[2,128,768]{2,1,0:T(8,128)(2,1)} %bitcast.74), custom_call_target="tpu_custom_call" | custom-call | tf_op jit(solution)/shard_map/pick/pallas_call | solution.py:374
  14.7 42.5 %all-to-all-done = bf16[16,72,1536]{2,1,0:T(8,128)(2,1)} async-done(((bf16[16,72,1536]{2,1,0:T(8,128)(2,1)}), bf16[16,72,1536]{2,1,0:T(8,128)(2,1)}, u32[]{:S(2)}, u32[]{:S(2)}) %all-to-all-start) | async-done | bytes 3538976 | tf_op jit(solution)/shard_map/all_to_all | solution.py:442
  57.2 0.0 collective-permute-start
  57.2 0.0 slice-start
  57.2 12.1 %all-to-all-start.1 = ((bf16[16,72,768]{2,1,0:T(8,128)(2,1)}), bf16[16,72,768]{2,1,0:T(8,128)(2,1)}, u32[]{:S(2)}, u32[]{:S(2)}) async-start(bf16[16,72,768]{2,1,0:T(8,128)(2,1)} %bitcast.71), calls=%async_computation.1 | async-start | bytes 3538944 | tf_op jit(solution)/shard_map/all_to_all | solution.py:442
  69.3 0.0 collective-permute-done.refs_2_
  69.3 0.0 slice-start.1
  69.3 8.2 %factor.2.refs_5_ = f32[576,1024]{1,0:T(8,128)S(1)} custom-call(s32[1]{0:T(128)} %bitcast.6.refs_0_.core_ref, bf16[2,576,1536]{2,1,0:T(8,128)(2,1)} %bitcast.14.refs_1_, bf16[2,576,1536]{2,1,0:T(8,128)(2,1)} %collective-permute-done.refs_2_, bf16[3072,1024]{1,0:T(8,128)(2,1)} %bitcast.59), custom_call_target="tpu_custom_call" | custom-call | flops 1000 | bytes 1000 | tf_op jit(solution)/shard_map/factor/pallas_call | solution.py:29
  77.6 0.0 slice-done
  77.6 0.0 slice-done.1
  77.6 11.7 %branch.1 = (bf16[2,576,768]{2,1,0:T(8,128)(2,1)}, bf16[2,576,768]{2,1,0:T(8,128)(2,1)}) custom-call(s32[1]{0:T(128)} %bitcast.6.refs_0_.core_ref, bf16[2,576,1536]{2,1,0:T(8,128)(2,1)} %bitcast.14.refs_1_, bf16[2,576,1536]{2,1,0:T(8,128)(2,1)} %collective-permute-done.refs_2_, bf16[1024,3072]{1,0:T(8,128)(2,1)} %bitcast.66, ...), custom_call_target="tpu_custom_call" | custom-call | flops 1000 | bytes 1000 | tf_op jit(solution)/shard_map/branch/pallas_call | solution.py:29
  89.3 0.1 collective-permute-start.1
  89.4 5.9 %all-to-all-done.1 = bf16[16,72,768]{2,1,0:T(8,128)(2,1)} async-done(((bf16[16,72,768]{2,1,0:T(8,128)(2,1)}), bf16[16,72,768]{2,1,0:T(8,128)(2,1)}, u32[]{:S(2)}, u32[]{:S(2)}) %all-to-all-start.1) | async-done | bytes 1769504 | tf_op jit(solution)/shard_map/all_to_all | solution.py:442
  95.3 0.0 copy-start.1
  95.3 0.0 collective-permute-start.2
  95.3 0.0 collective-permute-done.1
  95.3 1.5 copy-done.1
  96.8 3.1 %add_convert_fusion.1 = bf16[2,576,768]{2,1,0:T(8,128)(2,1)} fusion(bf16[2,576,768]{2,1,0:T(8,128)(2,1)} %collective-permute-done.1, bf16[2,576,768]{2,1,0:T(8,128)(2,1)S(1)} %copy-done.1), kind=kLoop, calls=%fused_computation.3 | loop fusion | flops 3538944 | bytes 5308416 | tf_op jit(solution)/shard_map/convert_element_type | solution.py:495
  99.9 0.0 copy-start.6
  99.9 0.0 copy-start.5
  99.9 0.0 copy-start.8
  99.9 6.0 %all-to-all-start.2 = ((bf16[16,72,768]{2,1,0:T(8,128)(2,1)}), bf16[16,72,768]{2,1,0:T(8,128)(2,1)S(1)}, u32[]{:S(2)}, u32[]{:S(2)}) async-start(bf16[16,72,768]{2,1,0:T(8,128)(2,1)} %bitcast.18), calls=%async_computation.2 | async-start | bytes 3538944 | tf_op jit(solution)/shard_map/all_to_all | solution.py:442
  105.9 0.0 copy-done.6
  105.9 0.7 fusion.17
  110.5 0.0 copy-done.5
  110.6 0.0 copy-done.8
  110.6 0.1 fusion.2
  110.8 0.7 fusion.3
  111.5 0.6 iota_compare_fusion
  112.1 0.0 collective-permute-done.2.refs_2_
  112.1 0.0 copy-start
  112.1 17.7 %all-to-all-done.2 = bf16[16,72,768]{2,1,0:T(8,128)(2,1)S(1)} async-done(((bf16[16,72,768]{2,1,0:T(8,128)(2,1)}), bf16[16,72,768]{2,1,0:T(8,128)(2,1)S(1)}, u32[]{:S(2)}, u32[]{:S(2)}) %all-to-all-start.2) | async-done | bytes 1769504 | tf_op jit(solution)/shard_map/all_to_all | solution.py:442
  129.8 0.0 copy-start.2
  129.8 0.8 broadcast_in_dim.78
  130.7 0.2 convert_reduce_fusion.1
  130.9 0.0 copy-done.2
  130.9 0.0 copy-done.7
  130.9 0.9 fusion.1
  131.8 0.0 copy-done
  131.8 5.9 %collective-permute-start.3 = (bf16[128,768]{1,0:T(8,128)(2,1)S(1)}, bf16[128,768]{1,0:T(8,128)(2,1)S(1)}, u32[]{:S(2)}, u32[]{:S(2)}) collective-permute-start(bf16[128,768]{1,0:T(8,128)(2,1)S(1)} %fusion.1), channel_id=1, source_target_pairs={{0,224},{32,0},{64,32},{96,64},{128,96},{160,128},{192,160},{224,1... | collective-permute-start | bytes 589832 | tf_op jit(solution)/shard_map/ppermute | solution.py:460
  137.8 3.2 %collective-permute-done.3 = bf16[128,768]{1,0:T(8,128)(2,1)S(1)} collective-permute-done((bf16[128,768]{1,0:T(8,128)(2,1)S(1)}, bf16[128,768]{1,0:T(8,128)(2,1)S(1)}, u32[]{:S(2)}, u32[]{:S(2)}) %collective-permute-start.3) | collective-permute-done | bytes 196640 | tf_op jit(solution)/shard_map/ppermute | solution.py:460
  140.9 0.7 copy-done.3
  141.6 1.8 convolution_convert_fusion
  143.4 5.6 %all-to-all-start.3 = ((bf16[16,72,768]{2,1,0:T(8,128)(2,1)}), bf16[16,72,768]{2,1,0:T(8,128)(2,1)}, u32[]{:S(2)}, u32[]{:S(2)}) async-start(bf16[16,72,768]{2,1,0:T(8,128)(2,1)} %bitcast.27), calls=%async_computation.3 | async-start | bytes 3538944 | tf_op jit(solution)/shard_map/all_to_all | solution.py:442
  149.1 7.1 %factor.3.factors = f32[576,1024]{1,0:T(8,128)S(1)} custom-call(s32[1]{0:T(128)} %bitcast.6.refs_0_.core_ref, bf16[2,576,768]{2,1,0:T(8,128)(2,1)} %landed.1.refs_1_, bf16[2,576,768]{2,1,0:T(8,128)(2,1)} %copy-done, bf16[3072,1024]{1,0:T(8,128)(2,1)} %bitcast.60), custom_call_target="tpu_custom_call" | custom-call | flops 1000 | bytes 1000 | tf_op jit(solution)/shard_map/factor/pallas_call | solution.py:29
  156.2 12.8 %all-to-all-done.3 = bf16[16,72,768]{2,1,0:T(8,128)(2,1)} async-done(((bf16[16,72,768]{2,1,0:T(8,128)(2,1)}), bf16[16,72,768]{2,1,0:T(8,128)(2,1)}, u32[]{:S(2)}, u32[]{:S(2)}) %all-to-all-start.3) | async-done | bytes 1769504 | tf_op jit(solution)/shard_map/all_to_all | solution.py:442
  169.0 0.0 collective-permute-start.4
  169.0 4.2 %own_act.1.own = f32[576,1024]{1,0:T(8,128)S(1)} custom-call(s32[1]{0:T(128)} %bitcast.6.refs_0_.core_ref, bf16[2,576,768]{2,1,0:T(8,128)(2,1)} %bitcast.28.mine, bf16[1024,3072]{1,0:T(8,128)(2,1)} %bitcast.67), custom_call_target="tpu_custom_call" | custom-call | flops 1000 | bytes 1000 | tf_op jit(solution)/shard_map/own_act/pallas_call | solution.py:29
  173.2 0.0 collective-permute-done.4.other
  173.3 7.4 %sent_part.1 = (bf16[576,1024]{1,0:T(8,128)(2,1)S(1)}, bf16[2,576,768]{2,1,0:T(8,128)(2,1)S(1)}) custom-call(s32[1]{0:T(128)} %bitcast.6.refs_0_.core_ref, bf16[2,576,768]{2,1,0:T(8,128)(2,1)S(1)} %collective-permute-done.4.other, bf16[1024,3072]{1,0:T(8,128)(2,1)} %bitcast.68, bf16[3072,1024]{1,0:T(8,128)(2,1)} %bitcast.61, f32[576,1024]{1,0:T(8,128)S(1)} %own_act.1.own, ...), custom_call_target="tpu_custom_call" | custom-call | flops 1000 | bytes 1000 | tf_op jit(solution)/shard_map/sent_part/pallas_call | solution.py:29
  180.7 0.8 collective-permute-start.5
  181.5 4.6 %kept_part.1 = bf16[2,576,768]{2,1,0:T(8,128)(2,1)S(1)} custom-call(s32[1]{0:T(128)} %bitcast.6.refs_0_.core_ref, bf16[3072,1024]{1,0:T(8,128)(2,1)} %bitcast.62, bf16[576,1024]{1,0:T(8,128)(2,1)S(1)} %get-tuple-element.35.grad_pre), custom_call_target="tpu_custom_call" | custom-call | flops 10000000000 | bytes 1000 | tf_op jit(solution)/shard_map/kept_part/pallas_call | solution.py:29
  186.2 0.0 collective-permute-done.5
  186.2 1.7 add_convert_fusion
  187.8 6.1 %all-to-all-start.4 = ((bf16[16,72,768]{2,1,0:T(8,128)(2,1)}), bf16[16,72,768]{2,1,0:T(8,128)(2,1)S(1)}, u32[]{:S(2)}, u32[]{:S(2)}) async-start(bf16[16,72,768]{2,1,0:T(8,128)(2,1)} %bitcast.29), calls=%async_computation.4 | async-start | bytes 3538944 | tf_op jit(solution)/shard_map/all_to_all | solution.py:442
  193.9 25.2 %all-to-all-done.4 = bf16[16,72,768]{2,1,0:T(8,128)(2,1)S(1)} async-done(((bf16[16,72,768]{2,1,0:T(8,128)(2,1)}), bf16[16,72,768]{2,1,0:T(8,128)(2,1)S(1)}, u32[]{:S(2)}, u32[]{:S(2)}) %all-to-all-start.4) | async-done | bytes 1769504 | tf_op jit(solution)/shard_map/all_to_all | solution.py:442
  219.2 0.2 convert_reduce_fusion
  219.4 0.0 copy-done.4
  219.4 0.8 add_convert_fusion.2
  220.3 3.2 %collective-permute-start.6 = (bf16[128,768]{1,0:T(8,128)(2,1)S(1)}, bf16[128,768]{1,0:T(8,128)(2,1)S(1)}, u32[]{:S(2)}, u32[]{:S(2)}) collective-permute-start(bf16[128,768]{1,0:T(8,128)(2,1)S(1)} %add_convert_fusion.2), channel_id=1, source_target_pairs={{0,224},{32,0},{64,32},{96,64},{128,96},{160,128},{192,160},{224,1... | collective-permute-start | bytes 589832 | tf_op jit(solution)/shard_map/ppermute | solution.py:460
  223.5 3.2 %collective-permute-done.6 = bf16[128,768]{1,0:T(8,128)(2,1)S(1)} collective-permute-done((bf16[128,768]{1,0:T(8,128)(2,1)S(1)}, bf16[128,768]{1,0:T(8,128)(2,1)S(1)}, u32[]{:S(2)}, u32[]{:S(2)}) %collective-permute-start.6) | collective-permute-done | bytes 196640 | tf_op jit(solution)/shard_map/ppermute | solution.py:460
  226.6 0.7 copy.11
  (10 shorter events, 0.1 us)
Async XLA Ops:
  4.0 53.3 %all-to-all-start = ((bf16[16,72,1536]{2,1,0:T(8,128)(2,1)}), bf16[16,72,1536]{2,1,0:T(8,128)(2,1)}, u32[]{:S(2)}, u32[]{:S(2)}) async-start(bf16[16,72,1536]{2,1,0:T(8,128)(2,1)} %bitcast.69), calls=%async_computation | async-start | bytes 7077888 | tf_op jit(solution)/shard_map/all_to_all | solution.py:442
  57.2 12.1 %collective-permute-start = (bf16[2,576,1536]{2,1,0:T(8,128)(2,1)}, bf16[2,576,1536]{2,1,0:T(8,128)(2,1)}, u32[]{:S(2)}, u32[]{:S(2)}) collective-permute-start(bf16[2,576,1536]{2,1,0:T(8,128)(2,1)} %bitcast.14.refs_1_), channel_id=1, source_target_pairs={{0,1},{1,0},{2,3},{3,2},{4,5},{5,4},{6,7},{7,6},{8,9},{9,8},{10,11... | collective-permute-start | bytes 10616840 | tf_op jit(solution)/shard_map/ppermute | solution.py:439
  57.2 20.3 %slice-start = ((s8[6291456]{0:T(1024)(128)(4,1)}), s8[2097152]{0:T(1024)(128)(4,1)S(1)}, s32[]{:S(2)}) async-start(s8[6291456]{0:T(1024)(128)(4,1)} %bitcast.63), calls=%async_computation.5 | async-start | bytes 4194304
  57.2 38.1 %all-to-all-start.1 = ((bf16[16,72,768]{2,1,0:T(8,128)(2,1)}), bf16[16,72,768]{2,1,0:T(8,128)(2,1)}, u32[]{:S(2)}, u32[]{:S(2)}) async-start(bf16[16,72,768]{2,1,0:T(8,128)(2,1)} %bitcast.71), calls=%async_computation.1 | async-start | bytes 3538944 | tf_op jit(solution)/shard_map/all_to_all | solution.py:442
  69.3 8.3 %slice-start.1 = ((s8[6291456]{0:T(1024)(128)(4,1)}), s8[4194304]{0:T(1024)(128)(4,1)S(1)}, s32[]{:S(2)}) async-start(s8[6291456]{0:T(1024)(128)(4,1)} %bitcast.63), calls=%async_computation.6 | async-start | bytes 8388608
  89.3 6.0 %collective-permute-start.1 = (bf16[2,576,768]{2,1,0:T(8,128)(2,1)}, bf16[2,576,768]{2,1,0:T(8,128)(2,1)}, u32[]{:S(2)}, u32[]{:S(2)}) collective-permute-start(bf16[2,576,768]{2,1,0:T(8,128)(2,1)} %get-tuple-element.25), channel_id=1, source_target_pairs={{0,1},{1,0},{2,3},{3,2},{4,5},{5,4},{6,7},{7,6},{8,9},{9,8},{10,11... | collective-permute-start | bytes 5308424 | tf_op jit(solution)/shard_map/ppermute | solution.py:439
  95.3 1.5 copy-start.1
  95.3 16.8 %collective-permute-start.2 = (bf16[2,576,768]{2,1,0:T(8,128)(2,1)}, bf16[2,576,768]{2,1,0:T(8,128)(2,1)S(1)}, u32[]{:S(2)}, u32[]{:S(2)}) collective-permute-start(bf16[2,576,768]{2,1,0:T(8,128)(2,1)} %landed.1.refs_1_), channel_id=1, source_target_pairs={{0,1},{1,0},{2,3},{3,2},{4,5},{5,4},{6,7},{7,6},{8,9},{9,8},{10,11... | collective-permute-start | bytes 5308424 | tf_op jit(solution)/shard_map/ppermute | solution.py:439
  99.9 6.0 %copy-start.6 = (s32[1,2]{1,0:T(1,128)S(1)}, s32[1,2]{1,0:T(1,128)}, u32[]{:S(2)}) copy-start(s32[1,2]{1,0:T(1,128)} %param.11) | copy-start | bytes 28
  99.9 10.6 %copy-start.5 = (s32[1,2,128,2]{2,3,1,0:T(2,128)S(1)}, s32[1,2,128,2]{2,3,1,0:T(2,128)}, u32[]{:S(2)}) copy-start(s32[1,2,128,2]{2,3,1,0:T(2,128)} %param.9) | copy-start | bytes 6148
  99.9 10.7 %copy-start.8 = (f32[1,2,128,2]{2,3,1,0:T(2,128)S(1)}, f32[1,2,128,2]{2,3,1,0:T(2,128)}, u32[]{:S(2)}) copy-start(f32[1,2,128,2]{2,3,1,0:T(2,128)} %param.10) | copy-start | bytes 6148
  99.9 29.9 %all-to-all-start.2 = ((bf16[16,72,768]{2,1,0:T(8,128)(2,1)}), bf16[16,72,768]{2,1,0:T(8,128)(2,1)S(1)}, u32[]{:S(2)}, u32[]{:S(2)}) async-start(bf16[16,72,768]{2,1,0:T(8,128)(2,1)} %bitcast.18), calls=%async_computation.2 | async-start | bytes 3538944 | tf_op jit(solution)/shard_map/all_to_all | solution.py:442
  112.1 19.7 %copy-start = (bf16[2,576,768]{2,1,0:T(8,128)(2,1)}, bf16[2,576,768]{2,1,0:T(8,128)(2,1)S(1)}, u32[]{:S(2)}) copy-start(bf16[2,576,768]{2,1,0:T(8,128)(2,1)S(1)} %collective-permute-done.2.refs_2_) | copy-start | bytes 5308420
  129.8 1.1 copy-start.2
  129.8 1.1 copy-start.7
  131.8 9.1 %collective-permute-start.3 = (bf16[128,768]{1,0:T(8,128)(2,1)S(1)}, bf16[128,768]{1,0:T(8,128)(2,1)S(1)}, u32[]{:S(2)}, u32[]{:S(2)}) collective-permute-start(bf16[128,768]{1,0:T(8,128)(2,1)S(1)} %fusion.1), channel_id=1, source_target_pairs={{0,224},{32,0},{64,32},{96,64},{128,96},{160,128},{192,160},{224,1... | collective-permute-start | bytes 589832 | tf_op jit(solution)/shard_map/ppermute | solution.py:460
  140.9 0.7 copy-start.3
  143.4 25.6 %all-to-all-start.3 = ((bf16[16,72,768]{2,1,0:T(8,128)(2,1)}), bf16[16,72,768]{2,1,0:T(8,128)(2,1)}, u32[]{:S(2)}, u32[]{:S(2)}) async-start(bf16[16,72,768]{2,1,0:T(8,128)(2,1)} %bitcast.27), calls=%async_computation.3 | async-start | bytes 3538944 | tf_op jit(solution)/shard_map/all_to_all | solution.py:442
  169.0 4.2 %collective-permute-start.4 = (bf16[2,576,768]{2,1,0:T(8,128)(2,1)}, bf16[2,576,768]{2,1,0:T(8,128)(2,1)S(1)}, u32[]{:S(2)}, u32[]{:S(2)}) collective-permute-start(bf16[2,576,768]{2,1,0:T(8,128)(2,1)} %bitcast.28.mine), channel_id=1, source_target_pairs={{0,1},{1,0},{2,3},{3,2},{4,5},{5,4},{6,7},{7,6},{8,9},{9,8},{10,11... | collective-permute-start | bytes 5308424 | tf_op jit(solution)/shard_map/ppermute | solution.py:439
  180.7 5.4 %collective-permute-start.5 = (bf16[2,576,768]{2,1,0:T(8,128)(2,1)S(1)}, bf16[2,576,768]{2,1,0:T(8,128)(2,1)S(1)}, u32[]{:S(2)}, u32[]{:S(2)}) collective-permute-start(bf16[2,576,768]{2,1,0:T(8,128)(2,1)S(1)} %get-tuple-element.36), channel_id=1, source_target_pairs={{0,1},{1,0},{2,3},{3,2},{4,5},{5,4},{6,7},{7,6},{8,9},{9,8},{10,11... | collective-permute-start | bytes 5308424 | tf_op jit(solution)/shard_map/ppermute | solution.py:439
  187.8 31.3 %all-to-all-start.4 = ((bf16[16,72,768]{2,1,0:T(8,128)(2,1)}), bf16[16,72,768]{2,1,0:T(8,128)(2,1)S(1)}, u32[]{:S(2)}, u32[]{:S(2)}) async-start(bf16[16,72,768]{2,1,0:T(8,128)(2,1)} %bitcast.29), calls=%async_computation.4 | async-start | bytes 3538944 | tf_op jit(solution)/shard_map/all_to_all | solution.py:442
  193.9 25.5 %copy-start.4 = (bf16[128,768]{1,0:T(8,128)(2,1)S(1)}, bf16[128,768]{1,0:T(8,128)(2,1)}, u32[]{:S(2)}) copy-start(bf16[128,768]{1,0:T(8,128)(2,1)} %copy-done.3) | copy-start | bytes 589828
  220.3 6.4 %collective-permute-start.6 = (bf16[128,768]{1,0:T(8,128)(2,1)S(1)}, bf16[128,768]{1,0:T(8,128)(2,1)S(1)}, u32[]{:S(2)}, u32[]{:S(2)}) collective-permute-start(bf16[128,768]{1,0:T(8,128)(2,1)S(1)} %add_convert_fusion.2), channel_id=1, source_target_pairs={{0,224},{32,0},{64,32},{96,64},{128,96},{160,128},{192,160},{224,1... | collective-permute-start | bytes 589832 | tf_op jit(solution)/shard_map/ppermute | solution.py:460

commit v9 on v8

--- a/solution.py
+++ b/solution.py
@@ -493,7 +493,10 @@
         if tick + 1 < ticks:
             keep, later = together(keep, landed(later))
         partial_rows = (keep.astype(jnp.float32) + got.astype(jnp.float32)).astype(jnp.bfloat16)
-        arrived = exchange(partial_rows.reshape(peers, CAPACITY, quarter))
+        partial_rows = partial_rows.reshape(peers, CAPACITY, quarter)
+        if tick + 1 < ticks:
+            partial_rows, later = together(partial_rows, later)
+        arrived = exchange(partial_rows)
         _, mixing = slots_of(tick)
         if tick + 1 == ticks:
             return combine(current, mixing, arrived)[None]

time: 228 us -> 231 us (1.013)
  waiting for transfers between devices: 111 us -> 115 us
    all_to_all x5, waiting for transfers between devices: 104 us -> 109 us  [exchange(): lax.all_to_all(value, ('xhi', 'expert'), split_axis=0, concat_axis=0, til...]
  transfers between devices with their start and end apart: 12 -> 12, of which waited for: 7 -> 7; matrix products, arithmetic and copies ran while one was open for 2% -> 1% of each run, Pallas kernels for 17% -> 17%
where the time goes in v9:
time: 231 us; the launch traced here: 230 us
  waiting for transfers between devices  115 us (50%)
  Pallas kernels  50.6 us (22%)
  starting transfers between devices  46.9 us (20%)
  other arithmetic  4.51 us (2%)
  local copies, waits for them, and re-layouts  4.44 us (2%)
  matrix products  4.39 us (2%)
  between operations  4.23 us (2%)
    all_to_all x5, waiting for transfers between devices, exchange(): lax.all_to_all(value, ('xhi', 'expert'), split_axis=0, concat_axis=0, til...  109 us
    pallas_call x6, Pallas kernels, local_kernel(): pl.pallas_call(kernel, out_shape=tuple((shape for shape, _ in outs)), in_...  43.3 us
    all_to_all x5, starting transfers between devices, exchange(): lax.all_to_all(value, ('xhi', 'expert'), split_axis=0, concat_axis=0, til...  36.8 us
    ppermute x2, starting transfers between devices, combine(): lax.ppermute(result, 'section', [(i, (i - 1) % n_section) for i in range(...  9.23 us
    pallas_call x2, Pallas kernels, pick(): pl.pallas_call(pick_kernel, out_shape=jax.ShapeDtypeStruct((n_xhi, EXPERT...  7.3 us
    ppermute x2, waiting for transfers between devices, combine(): lax.ppermute(result, 'section', [(i, (i - 1) % n_section) for i in range(...  6.38 us
  transfers between devices with their start and end apart: 12, of which 7 were waited for; matrix products, arithmetic and copies ran while one was open for 1% of the time, Pallas kernels for 17%

profile of v9, /device:TPU:8, one launch (start us, length us, event | category | flops | bytes accessed | tf_op | source)
XLA Modules:
  0.0 230.3 jit_solution(3099790339857258624)
XLA Ops:
  0.0 4.0 %pick.3 = bf16[2,4,2,72,1536]{4,3,2,1,0:T(8,128)(2,1)} custom-call(s32[2]{0:T(128)} %bitcast.79, s32[2,2,128]{2,1,0:T(2,128)} %bitcast.77, bf16[2,128,768]{2,1,0:T(8,128)(2,1)} %bitcast.73, bf16[1,128,768]{2,1,0:T(8,128)(2,1)} %refs_1_.1), custom_call_target="tpu_custom_call" | custom-call | tf_op jit(solution)/shard_map/pick/pallas_call | solution.py:374
  4.0 7.4 %all-to-all-start = ((bf16[16,72,1536]{2,1,0:T(8,128)(2,1)}), bf16[16,72,1536]{2,1,0:T(8,128)(2,1)}, u32[]{:S(2)}, u32[]{:S(2)}) async-start(bf16[16,72,1536]{2,1,0:T(8,128)(2,1)} %bitcast.69), calls=%async_computation | async-start | bytes 7077888 | tf_op jit(solution)/shard_map/all_to_all | solution.py:442
  11.4 3.3 %pick.2 = bf16[2,4,2,72,768]{4,3,2,1,0:T(8,128)(2,1)} custom-call(s32[2]{0:T(128)} %bitcast.80, s32[2,2,128]{2,1,0:T(2,128)} %bitcast.78, bf16[2,128,768]{2,1,0:T(8,128)(2,1)} %bitcast.74), custom_call_target="tpu_custom_call" | custom-call | tf_op jit(solution)/shard_map/pick/pallas_call | solution.py:374
  14.7 42.5 %all-to-all-done = bf16[16,72,1536]{2,1,0:T(8,128)(2,1)} async-done(((bf16[16,72,1536]{2,1,0:T(8,128)(2,1)}), bf16[16,72,1536]{2,1,0:T(8,128)(2,1)}, u32[]{:S(2)}, u32[]{:S(2)}) %all-to-all-start) | async-done | bytes 3538976 | tf_op jit(solution)/shard_map/all_to_all | solution.py:442
  57.2 0.0 collective-permute-start
  57.2 0.0 slice-start
  57.2 12.1 %all-to-all-start.1 = ((bf16[16,72,768]{2,1,0:T(8,128)(2,1)}), bf16[16,72,768]{2,1,0:T(8,128)(2,1)}, u32[]{:S(2)}, u32[]{:S(2)}) async-start(bf16[16,72,768]{2,1,0:T(8,128)(2,1)} %bitcast.71), calls=%async_computation.1 | async-start | bytes 3538944 | tf_op jit(solution)/shard_map/all_to_all | solution.py:442
  69.3 0.0 collective-permute-done.refs_2_
  69.3 0.0 slice-start.1
  69.3 8.2 %factor.2.refs_5_ = f32[576,1024]{1,0:T(8,128)S(1)} custom-call(s32[1]{0:T(128)} %bitcast.6.refs_0_.core_ref, bf16[2,576,1536]{2,1,0:T(8,128)(2,1)} %bitcast.14.refs_1_, bf16[2,576,1536]{2,1,0:T(8,128)(2,1)} %collective-permute-done.refs_2_, bf16[3072,1024]{1,0:T(8,128)(2,1)} %bitcast.59), custom_call_target="tpu_custom_call" | custom-call | flops 1000 | bytes 1000 | tf_op jit(solution)/shard_map/factor/pallas_call | solution.py:29
  77.6 0.0 slice-done
  77.6 0.0 slice-done.1
  77.6 11.7 %branch.1 = (bf16[2,576,768]{2,1,0:T(8,128)(2,1)}, bf16[2,576,768]{2,1,0:T(8,128)(2,1)}) custom-call(s32[1]{0:T(128)} %bitcast.6.refs_0_.core_ref, bf16[2,576,1536]{2,1,0:T(8,128)(2,1)} %bitcast.14.refs_1_, bf16[2,576,1536]{2,1,0:T(8,128)(2,1)} %collective-permute-done.refs_2_, bf16[1024,3072]{1,0:T(8,128)(2,1)} %bitcast.66, ...), custom_call_target="tpu_custom_call" | custom-call | flops 1000 | bytes 1000 | tf_op jit(solution)/shard_map/branch/pallas_call | solution.py:29
  89.3 0.1 collective-permute-start.1
  89.4 5.9 %all-to-all-done.1 = bf16[16,72,768]{2,1,0:T(8,128)(2,1)} async-done(((bf16[16,72,768]{2,1,0:T(8,128)(2,1)}), bf16[16,72,768]{2,1,0:T(8,128)(2,1)}, u32[]{:S(2)}, u32[]{:S(2)}) %all-to-all-start.1) | async-done | bytes 1769504 | tf_op jit(solution)/shard_map/all_to_all | solution.py:442
  95.3 0.0 copy-start.1
  95.3 0.0 collective-permute-done.1
  95.3 1.5 copy-done.1
  96.8 1.7 add_convert_fusion.1
  98.5 0.0 copy-start.6
  98.5 0.0 copy-start.5
  98.5 0.0 copy-start.8
  98.5 0.0 collective-permute-start.2
  98.5 6.0 %all-to-all-start.2 = ((bf16[16,72,768]{2,1,0:T(8,128)(2,1)}), bf16[16,72,768]{2,1,0:T(8,128)(2,1)S(1)}, u32[]{:S(2)}, u32[]{:S(2)}) async-start(bf16[16,72,768]{2,1,0:T(8,128)(2,1)} %bitcast.18), calls=%async_computation.2 | async-start | bytes 3538944 | tf_op jit(solution)/shard_map/all_to_all | solution.py:442
  104.5 0.0 copy-done.6
  104.5 0.7 fusion.17
  109.1 0.0 copy-done.5
  109.1 0.0 copy-done.8
  109.2 0.1 fusion.2
  109.3 0.7 fusion.3
  110.0 0.6 iota_compare_fusion
  110.7 19.7 %all-to-all-done.2 = bf16[16,72,768]{2,1,0:T(8,128)(2,1)S(1)} async-done(((bf16[16,72,768]{2,1,0:T(8,128)(2,1)}), bf16[16,72,768]{2,1,0:T(8,128)(2,1)S(1)}, u32[]{:S(2)}, u32[]{:S(2)}) %all-to-all-start.2) | async-done | bytes 1769504 | tf_op jit(solution)/shard_map/all_to_all | solution.py:442
  130.4 0.0 copy-start.2
  130.4 0.0 collective-permute-done.2.refs_2_
  130.4 0.0 copy-start
  130.4 0.9 broadcast_in_dim.78
  131.3 0.2 convert_reduce_fusion.1
  131.6 0.0 copy-done.2
  131.6 0.0 copy-done.7
  131.6 0.8 fusion.1
  132.5 0.0 copy-done
  132.5 5.9 %collective-permute-start.3 = (bf16[128,768]{1,0:T(8,128)(2,1)S(1)}, bf16[128,768]{1,0:T(8,128)(2,1)S(1)}, u32[]{:S(2)}, u32[]{:S(2)}) collective-permute-start(bf16[128,768]{1,0:T(8,128)(2,1)S(1)} %fusion.1), channel_id=1, source_target_pairs={{0,224},{32,0},{64,32},{96,64},{128,96},{160,128},{192,160},{224,1... | collective-permute-start | bytes 589832 | tf_op jit(solution)/shard_map/ppermute | solution.py:460
  138.4 3.2 %collective-permute-done.3 = bf16[128,768]{1,0:T(8,128)(2,1)S(1)} collective-permute-done((bf16[128,768]{1,0:T(8,128)(2,1)S(1)}, bf16[128,768]{1,0:T(8,128)(2,1)S(1)}, u32[]{:S(2)}, u32[]{:S(2)}) %collective-permute-start.3) | collective-permute-done | bytes 196640 | tf_op jit(solution)/shard_map/ppermute | solution.py:460
  141.6 0.7 copy-done.3
  142.3 1.8 convolution_convert_fusion
  144.1 5.7 %all-to-all-start.3 = ((bf16[16,72,768]{2,1,0:T(8,128)(2,1)}), bf16[16,72,768]{2,1,0:T(8,128)(2,1)}, u32[]{:S(2)}, u32[]{:S(2)}) async-start(bf16[16,72,768]{2,1,0:T(8,128)(2,1)} %bitcast.27), calls=%async_computation.3 | async-start | bytes 3538944 | tf_op jit(solution)/shard_map/all_to_all | solution.py:442
  149.8 7.1 %factor.3.factors = f32[576,1024]{1,0:T(8,128)S(1)} custom-call(s32[1]{0:T(128)} %bitcast.6.refs_0_.core_ref, bf16[2,576,768]{2,1,0:T(8,128)(2,1)} %landed.1.refs_1_, bf16[2,576,768]{2,1,0:T(8,128)(2,1)} %copy-done, bf16[3072,1024]{1,0:T(8,128)(2,1)} %bitcast.60), custom_call_target="tpu_custom_call" | custom-call | flops 1000 | bytes 1000 | tf_op jit(solution)/shard_map/factor/pallas_call | solution.py:29
  156.9 15.5 %all-to-all-done.3 = bf16[16,72,768]{2,1,0:T(8,128)(2,1)} async-done(((bf16[16,72,768]{2,1,0:T(8,128)(2,1)}), bf16[16,72,768]{2,1,0:T(8,128)(2,1)}, u32[]{:S(2)}, u32[]{:S(2)}) %all-to-all-start.3) | async-done | bytes 1769504 | tf_op jit(solution)/shard_map/all_to_all | solution.py:442
  172.4 0.0 collective-permute-start.4
  172.4 4.2 %own_act.1.own = f32[576,1024]{1,0:T(8,128)S(1)} custom-call(s32[1]{0:T(128)} %bitcast.6.refs_0_.core_ref, bf16[2,576,768]{2,1,0:T(8,128)(2,1)} %bitcast.28.mine, bf16[1024,3072]{1,0:T(8,128)(2,1)} %bitcast.67), custom_call_target="tpu_custom_call" | custom-call | flops 1000 | bytes 1000 | tf_op jit(solution)/shard_map/own_act/pallas_call | solution.py:29
  176.6 0.0 collective-permute-done.4.other
  176.6 7.4 %sent_part.1 = (bf16[576,1024]{1,0:T(8,128)(2,1)S(1)}, bf16[2,576,768]{2,1,0:T(8,128)(2,1)S(1)}) custom-call(s32[1]{0:T(128)} %bitcast.6.refs_0_.core_ref, bf16[2,576,768]{2,1,0:T(8,128)(2,1)S(1)} %collective-permute-done.4.other, bf16[1024,3072]{1,0:T(8,128)(2,1)} %bitcast.68, bf16[3072,1024]{1,0:T(8,128)(2,1)} %bitcast.61, f32[576,1024]{1,0:T(8,128)S(1)} %own_act.1.own, ...), custom_call_target="tpu_custom_call" | custom-call | flops 1000 | bytes 1000 | tf_op jit(solution)/shard_map/sent_part/pallas_call | solution.py:29
  184.0 0.8 collective-permute-start.5
  184.9 4.6 %kept_part.1 = bf16[2,576,768]{2,1,0:T(8,128)(2,1)S(1)} custom-call(s32[1]{0:T(128)} %bitcast.6.refs_0_.core_ref, bf16[3072,1024]{1,0:T(8,128)(2,1)} %bitcast.62, bf16[576,1024]{1,0:T(8,128)(2,1)S(1)} %get-tuple-element.39.grad_pre), custom_call_target="tpu_custom_call" | custom-call | flops 10000000000 | bytes 1000 | tf_op jit(solution)/shard_map/kept_part/pallas_call | solution.py:29
  189.5 0.0 collective-permute-done.5
  189.5 1.7 add_convert_fusion
  191.2 5.7 %all-to-all-start.4 = ((bf16[16,72,768]{2,1,0:T(8,128)(2,1)}), bf16[16,72,768]{2,1,0:T(8,128)(2,1)S(1)}, u32[]{:S(2)}, u32[]{:S(2)}) async-start(bf16[16,72,768]{2,1,0:T(8,128)(2,1)} %bitcast.29), calls=%async_computation.4 | async-start | bytes 3538944 | tf_op jit(solution)/shard_map/all_to_all | solution.py:442
  196.8 25.2 %all-to-all-done.4 = bf16[16,72,768]{2,1,0:T(8,128)(2,1)S(1)} async-done(((bf16[16,72,768]{2,1,0:T(8,128)(2,1)}), bf16[16,72,768]{2,1,0:T(8,128)(2,1)S(1)}, u32[]{:S(2)}, u32[]{:S(2)}) %all-to-all-start.4) | async-done | bytes 1769504 | tf_op jit(solution)/shard_map/all_to_all | solution.py:442
  222.1 0.2 convert_reduce_fusion
  222.3 0.0 copy-done.4
  222.3 0.8 add_convert_fusion.2
  223.2 3.3 %collective-permute-start.6 = (bf16[128,768]{1,0:T(8,128)(2,1)S(1)}, bf16[128,768]{1,0:T(8,128)(2,1)S(1)}, u32[]{:S(2)}, u32[]{:S(2)}) collective-permute-start(bf16[128,768]{1,0:T(8,128)(2,1)S(1)} %add_convert_fusion.2), channel_id=1, source_target_pairs={{0,224},{32,0},{64,32},{96,64},{128,96},{160,128},{192,160},{224,1... | collective-permute-start | bytes 589832 | tf_op jit(solution)/shard_map/ppermute | solution.py:460
  226.5 3.2 %collective-permute-done.6 = bf16[128,768]{1,0:T(8,128)(2,1)S(1)} collective-permute-done((bf16[128,768]{1,0:T(8,128)(2,1)S(1)}, bf16[128,768]{1,0:T(8,128)(2,1)S(1)}, u32[]{:S(2)}, u32[]{:S(2)}) %collective-permute-start.6) | collective-permute-done | bytes 196640 | tf_op jit(solution)/shard_map/ppermute | solution.py:460
  229.7 0.7 copy.11
  (10 shorter events, 0.1 us)
Async XLA Ops:
  4.0 53.3 %all-to-all-start = ((bf16[16,72,1536]{2,1,0:T(8,128)(2,1)}), bf16[16,72,1536]{2,1,0:T(8,128)(2,1)}, u32[]{:S(2)}, u32[]{:S(2)}) async-start(bf16[16,72,1536]{2,1,0:T(8,128)(2,1)} %bitcast.69), calls=%async_computation | async-start | bytes 7077888 | tf_op jit(solution)/shard_map/all_to_all | solution.py:442
  57.2 12.1 %collective-permute-start = (bf16[2,576,1536]{2,1,0:T(8,128)(2,1)}, bf16[2,576,1536]{2,1,0:T(8,128)(2,1)}, u32[]{:S(2)}, u32[]{:S(2)}) collective-permute-start(bf16[2,576,1536]{2,1,0:T(8,128)(2,1)} %bitcast.14.refs_1_), channel_id=1, source_target_pairs={{0,1},{1,0},{2,3},{3,2},{4,5},{5,4},{6,7},{7,6},{8,9},{9,8},{10,11... | collective-permute-start | bytes 10616840 | tf_op jit(solution)/shard_map/ppermute | solution.py:439
  57.2 20.3 %slice-start = ((s8[6291456]{0:T(1024)(128)(4,1)}), s8[2097152]{0:T(1024)(128)(4,1)S(1)}, s32[]{:S(2)}) async-start(s8[6291456]{0:T(1024)(128)(4,1)} %bitcast.63), calls=%async_computation.5 | async-start | bytes 4194304
  57.2 38.1 %all-to-all-start.1 = ((bf16[16,72,768]{2,1,0:T(8,128)(2,1)}), bf16[16,72,768]{2,1,0:T(8,128)(2,1)}, u32[]{:S(2)}, u32[]{:S(2)}) async-start(bf16[16,72,768]{2,1,0:T(8,128)(2,1)} %bitcast.71), calls=%async_computation.1 | async-start | bytes 3538944 | tf_op jit(solution)/shard_map/all_to_all | solution.py:442
  69.3 8.3 %slice-start.1 = ((s8[6291456]{0:T(1024)(128)(4,1)}), s8[4194304]{0:T(1024)(128)(4,1)S(1)}, s32[]{:S(2)}) async-start(s8[6291456]{0:T(1024)(128)(4,1)} %bitcast.63), calls=%async_computation.6 | async-start | bytes 8388608
  89.3 6.0 %collective-permute-start.1 = (bf16[2,576,768]{2,1,0:T(8,128)(2,1)}, bf16[2,576,768]{2,1,0:T(8,128)(2,1)S(1)}, u32[]{:S(2)}, u32[]{:S(2)}) collective-permute-start(bf16[2,576,768]{2,1,0:T(8,128)(2,1)} %get-tuple-element.27), channel_id=1, source_target_pairs={{0,1},{1,0},{2,3},{3,2},{4,5},{5,4},{6,7},{7,6},{8,9},{9,8},{10,11... | collective-permute-start | bytes 5308424 | tf_op jit(solution)/shard_map/ppermute | solution.py:439
  95.3 1.5 copy-start.1
  98.5 6.0 %copy-start.6 = (s32[1,2]{1,0:T(1,128)S(1)}, s32[1,2]{1,0:T(1,128)}, u32[]{:S(2)}) copy-start(s32[1,2]{1,0:T(1,128)} %param.11) | copy-start | bytes 28
  98.5 10.6 %copy-start.5 = (s32[1,2,128,2]{2,3,1,0:T(2,128)S(1)}, s32[1,2,128,2]{2,3,1,0:T(2,128)}, u32[]{:S(2)}) copy-start(s32[1,2,128,2]{2,3,1,0:T(2,128)} %param.9) | copy-start | bytes 6148
  98.5 10.7 %copy-start.8 = (f32[1,2,128,2]{2,3,1,0:T(2,128)S(1)}, f32[1,2,128,2]{2,3,1,0:T(2,128)}, u32[]{:S(2)}) copy-start(f32[1,2,128,2]{2,3,1,0:T(2,128)} %param.10) | copy-start | bytes 6148
  98.5 32.0 %collective-permute-start.2 = (bf16[2,576,768]{2,1,0:T(8,128)(2,1)}, bf16[2,576,768]{2,1,0:T(8,128)(2,1)S(1)}, u32[]{:S(2)}, u32[]{:S(2)}) collective-permute-start(bf16[2,576,768]{2,1,0:T(8,128)(2,1)} %landed.1.refs_1_), channel_id=1, source_target_pairs={{0,1},{1,0},{2,3},{3,2},{4,5},{5,4},{6,7},{7,6},{8,9},{9,8},{10,11... | collective-permute-start | bytes 5308424 | tf_op jit(solution)/shard_map/ppermute | solution.py:439
  98.5 31.9 %all-to-all-start.2 = ((bf16[16,72,768]{2,1,0:T(8,128)(2,1)}), bf16[16,72,768]{2,1,0:T(8,128)(2,1)S(1)}, u32[]{:S(2)}, u32[]{:S(2)}) async-start(bf16[16,72,768]{2,1,0:T(8,128)(2,1)} %bitcast.18), calls=%async_computation.2 | async-start | bytes 3538944 | tf_op jit(solution)/shard_map/all_to_all | solution.py:442
  130.4 1.2 copy-start.2
  130.4 1.2 copy-start.7
  130.4 2.0 copy-start
  132.5 9.1 %collective-permute-start.3 = (bf16[128,768]{1,0:T(8,128)(2,1)S(1)}, bf16[128,768]{1,0:T(8,128)(2,1)S(1)}, u32[]{:S(2)}, u32[]{:S(2)}) collective-permute-start(bf16[128,768]{1,0:T(8,128)(2,1)S(1)} %fusion.1), channel_id=1, source_target_pairs={{0,224},{32,0},{64,32},{96,64},{128,96},{160,128},{192,160},{224,1... | collective-permute-start | bytes 589832 | tf_op jit(solution)/shard_map/ppermute | solution.py:460
  141.6 0.7 copy-start.3
  144.1 28.3 %all-to-all-start.3 = ((bf16[16,72,768]{2,1,0:T(8,128)(2,1)}), bf16[16,72,768]{2,1,0:T(8,128)(2,1)}, u32[]{:S(2)}, u32[]{:S(2)}) async-start(bf16[16,72,768]{2,1,0:T(8,128)(2,1)} %bitcast.27), calls=%async_computation.3 | async-start | bytes 3538944 | tf_op jit(solution)/shard_map/all_to_all | solution.py:442
  172.4 4.2 %collective-permute-start.4 = (bf16[2,576,768]{2,1,0:T(8,128)(2,1)}, bf16[2,576,768]{2,1,0:T(8,128)(2,1)S(1)}, u32[]{:S(2)}, u32[]{:S(2)}) collective-permute-start(bf16[2,576,768]{2,1,0:T(8,128)(2,1)} %bitcast.28.mine), channel_id=1, source_target_pairs={{0,1},{1,0},{2,3},{3,2},{4,5},{5,4},{6,7},{7,6},{8,9},{9,8},{10,11... | collective-permute-start | bytes 5308424 | tf_op jit(solution)/shard_map/ppermute | solution.py:439
  184.0 5.4 %collective-permute-start.5 = (bf16[2,576,768]{2,1,0:T(8,128)(2,1)S(1)}, bf16[2,576,768]{2,1,0:T(8,128)(2,1)S(1)}, u32[]{:S(2)}, u32[]{:S(2)}) collective-permute-start(bf16[2,576,768]{2,1,0:T(8,128)(2,1)S(1)} %get-tuple-element.40), channel_id=1, source_target_pairs={{0,1},{1,0},{2,3},{3,2},{4,5},{5,4},{6,7},{7,6},{8,9},{9,8},{10,11... | collective-permute-start | bytes 5308424 | tf_op jit(solution)/shard_map/ppermute | solution.py:439
  191.2 30.9 %all-to-all-start.4 = ((bf16[16,72,768]{2,1,0:T(8,128)(2,1)}), bf16[16,72,768]{2,1,0:T(8,128)(2,1)S(1)}, u32[]{:S(2)}, u32[]{:S(2)}) async-start(bf16[16,72,768]{2,1,0:T(8,128)(2,1)} %bitcast.29), calls=%async_computation.4 | async-start | bytes 3538944 | tf_op jit(solution)/shard_map/all_to_all | solution.py:442
  196.8 25.5 %copy-start.4 = (bf16[128,768]{1,0:T(8,128)(2,1)S(1)}, bf16[128,768]{1,0:T(8,128)(2,1)}, u32[]{:S(2)}) copy-start(bf16[128,768]{1,0:T(8,128)(2,1)} %copy-done.3) | copy-start | bytes 589828
  223.2 6.5 %collective-permute-start.6 = (bf16[128,768]{1,0:T(8,128)(2,1)S(1)}, bf16[128,768]{1,0:T(8,128)(2,1)S(1)}, u32[]{:S(2)}, u32[]{:S(2)}) collective-permute-start(bf16[128,768]{1,0:T(8,128)(2,1)S(1)} %add_convert_fusion.2), channel_id=1, source_target_pairs={{0,224},{32,0},{64,32},{96,64},{128,96},{160,128},{192,160},{224,1... | collective-permute-start | bytes 589832 | tf_op jit(solution)/shard_map/ppermute | solution.py:460
